TPU v7x, 128 devices: a whole 4x4x4 slice. The times are simulated.
128 devices in a mesh: gx: 16 (over y, x), gy: 8 (over z, core).
Axes of the slice: x: 4, y: 4, z: 4, core: 2. Of those that a mesh axis runs over, the one named last changes fastest.
Arguments:
- charge_blocks: float32 [524288, 128], P(('gx', 'gy')), may hold values from -6 to 6
- block_tile: int32 [524288], P(('gx', 'gy')), may hold values from 0 to 196607, as said below
- block_count: int32 [128], P(('gx', 'gy')), may hold values from 2048 to 4096, as said below
- near_kernel: float32 [9, 9, 9], replicated, may hold values from -0.21875 to 0.21875
- mid_kernel: float32 [9, 9, 9], replicated, may hold values from -0.109375 to 0.109375
- top_weights: float32 [4], replicated, may hold values from 0.00072168784 to 0.1
- top_widths: float32 [4], replicated, may hold values from 1 to 12
Outputs:
- potential: float32 [512, 192, 256], P('gx', 'gy')
Inputs may be any that keep to these rules, and one draw needn't show every extreme that they name: `block_tile`: of the 4096 slots of one device, exactly 32 name tiles in the pencil of each device, dead slots included. Slots 0 to block_count - 1 of a device are live, the others hold values that are ignored.
All inputs are finite; a program needn't handle non-finite values.
Results may differ from a plain program's by a relative error of at most 0.000082.
Values sent between devices are 32-bit elements; how exact they have to be, the bound alone decides.
No kernel may reach another device: no remote copies, remote signals or barrier semaphores. Data moves between devices by JAX's collectives and lax.ppermute only.
A program may use at most 128 MiB of HBM per device.

v0:
```python
import jax
import jax.numpy as jnp
from jax import lax
from jax.sharding import PartitionSpec as P

CX = 32
CY = 24
NZ = 256
RADIUS = 4
ZB = 128


PRECISE = lax.Precision.HIGHEST


def extended_2(block, sides, width):
    for axis, dim in sides:
        count = lax.axis_size(axis)
        forward = [(i, i + 1) for i in range(count - 1)]
        forward.append((count - 1, 0))
        backward = [(target, source) for source, target in forward]
        low = lax.ppermute(
            lax.slice_in_dim(block, block.shape[dim] - width, None, axis=dim), axis, forward
        )
        high = lax.ppermute(lax.slice_in_dim(block, 0, width, axis=dim), axis, backward)
        block = jnp.concatenate([low, block, high], axis=dim)
    return block


def shifted(block, axis, distance):
    devices = range(lax.axis_size(axis))
    route = [((i - distance) % len(devices), i) for i in devices]
    return lax.ppermute(block, axis, route)


def band_table(width_z, radius):
    level_ids = jnp.arange(2 * radius + 1, dtype=jnp.int32)[:, None, None]
    window_ids = jnp.arange(width_z + 2 * radius, dtype=jnp.int32)[None, :, None]
    output_ids = jnp.arange(width_z, dtype=jnp.int32)[None, None, :]
    return (window_ids - output_ids == level_ids).astype(jnp.float32)


def widen(values):
    return extended_2(values, (("gx", 0), ("gy", 1)), RADIUS)


def cutoff(padded, kernel):
    diameter = 2 * RADIUS + 1
    span = ZB + 2 * RADIUS
    row_count = padded.shape[0] - 2 * RADIUS
    col_count = padded.shape[1] - 2 * RADIUS
    depth_z = padded.shape[2]
    extended = jnp.concatenate(
        [padded[:, :, depth_z - RADIUS :], padded, padded[:, :, :RADIUS]], axis=2
    )
    table = band_table(ZB, RADIUS)

    def add_shift(row_shift, running):
        slab_rows = lax.dynamic_slice_in_dim(extended, row_shift, row_count, 0)
        weights = lax.dynamic_index_in_dim(kernel, row_shift, 0, keepdims=False)
        banded = jnp.einsum("ye,ewz->ywz", weights, table, precision=PRECISE).reshape(
            diameter * span, ZB
        )
        pieces = []
        for stripe in range(depth_z // ZB):
            window = slab_rows[:, :, stripe * ZB : stripe * ZB + span]
            stacked = jnp.stack(
                [window[:, shift_y : shift_y + col_count] for shift_y in range(diameter)], axis=2
            )
            stacked = stacked.reshape(row_count * col_count, diameter * span)
            pieces.append(
                jnp.dot(stacked, banded, precision=PRECISE, preferred_element_type=jnp.float32)
            )
        return running + jnp.concatenate(pieces, axis=1)

    start_sum = jnp.zeros((row_count * col_count, depth_z), jnp.float32)
    summed = lax.fori_loop(0, diameter, add_shift, start_sum)
    return summed.reshape(row_count, col_count, depth_z)


def wrap_depth(values):
    return jnp.concatenate([values[:, :, -1:], values, values[:, :, :1]], axis=2)


def thin_out(extended, axis_dim):
    length = extended.shape[axis_dim] - 2
    centre = lax.slice_in_dim(extended, 1, length + 1, 2, axis_dim)
    before = lax.slice_in_dim(extended, 0, length, 2, axis_dim)
    behind = lax.slice_in_dim(extended, 2, length + 2, 2, axis_dim)
    return centre + 0.5 * (before + behind)


def restrict(padded):
    row_count = padded.shape[0] - 2 * RADIUS
    col_count = padded.shape[1] - 2 * RADIUS
    inner = padded[RADIUS - 1 : RADIUS + row_count + 1, RADIUS - 1 : RADIUS + col_count + 1]
    halved = thin_out(inner, 0)
    halved = thin_out(halved, 1)
    return thin_out(wrap_depth(halved), 2)


def spread_next(extended, axis_dim):
    length = extended.shape[axis_dim] - 1
    centre = lax.slice_in_dim(extended, 0, length, 1, axis_dim)
    following = lax.slice_in_dim(extended, 1, length + 1, 1, axis_dim)
    paired = jnp.stack([centre, 0.5 * (centre + following)], axis=axis_dim + 1)
    layout = list(centre.shape)
    layout[axis_dim] = 2 * length
    return paired.reshape(layout)


def prolong(values):
    upper_row = shifted(values[:1], "gx", -1)
    taller = jnp.concatenate([values, upper_row], axis=0)
    upper_col = shifted(taller[:, :1], "gy", -1)
    padded = jnp.concatenate([taller, upper_col], axis=1)
    finer = spread_next(padded, 0)
    finer = spread_next(finer, 1)
    finer = jnp.concatenate([finer, finer[:, :, :1]], axis=2)
    return spread_next(finer, 2)


def gaussians(period, widths, first_row, row_count):
    row_ids = first_row + jnp.arange(row_count, dtype=jnp.int32)[:, None]
    col_ids = jnp.arange(period, dtype=jnp.int32)[None, :]
    offset = (row_ids - col_ids) % period
    distance = jnp.minimum(offset, period - offset).astype(jnp.float32)
    return jnp.exp(-(distance * distance)[None] / (widths * widths)[:, None, None])


def top_level(top_charge, top_weights, top_widths):
    rows_x, rows_y, depth_z = top_charge.shape
    period_x = rows_x * lax.axis_size("gx")
    period_y = rows_y * lax.axis_size("gy")
    gauss_x = gaussians(period_x, top_widths, lax.axis_index("gx") * rows_x, rows_x)
    gauss_y = gaussians(period_y, top_widths, lax.axis_index("gy") * rows_y, rows_y)
    gauss_z = gaussians(depth_z, top_widths, 0, depth_z)
    column = lax.all_gather(top_charge, "gx", axis=0, tiled=True)
    whole = lax.all_gather(column, "gy", axis=1, tiled=True)
    plane = jnp.einsum("kia,abc->kibc", gauss_x, whole, precision=PRECISE)
    along_y = jnp.einsum("kjb,kibc->kijc", gauss_y, plane, precision=PRECISE)
    along_z = jnp.einsum("kzc,kijc->kijz", gauss_z, along_y, precision=PRECISE)
    return jnp.einsum("k,kijz->ijz", top_weights, along_z, precision=PRECISE)


def on_device(
    charge_blocks, block_tile, block_count, near_kernel, mid_kernel, top_weights, top_widths
):
    size_x = lax.axis_size("gx")
    size_y = lax.axis_size("gy")
    device_total = size_x * size_y
    slot_total = charge_blocks.shape[0]
    per_owner = slot_total // device_total
    stripes = NZ // ZB
    grid_y = CY * size_y
    live_slot = jnp.arange(slot_total, dtype=jnp.int32) < block_count[0]
    masked = charge_blocks * live_slot[:, None].astype(jnp.float32)
    column_ids = block_tile // stripes
    stripe_ids = block_tile % stripes
    global_x = column_ids // grid_y
    global_y = column_ids % grid_y
    owner_ids = global_x // CX * size_y + global_y // CY
    local_tile = (global_x % CX * CY + global_y % CY) * stripes + stripe_ids
    ordering = jnp.argsort(owner_ids, stable=True)
    outgoing = masked[ordering].reshape(size_x, size_y, per_owner, ZB)
    outgoing_ids = local_tile[ordering].reshape(size_x, size_y, per_owner)
    arrived, arrived_ids = (
        lax.all_to_all(
            outgoing.reshape(device_total, per_owner, ZB),
            ("gx", "gy"),
            split_axis=0,
            concat_axis=0,
            tiled=True,
        ),
        lax.all_to_all(
            outgoing_ids.reshape(device_total, per_owner),
            ("gx", "gy"),
            split_axis=0,
            concat_axis=0,
            tiled=True,
        ),
    )
    fine_charge = jax.ops.segment_sum(
        arrived.reshape(-1, ZB), arrived_ids.reshape(-1), num_segments=CX * CY * stripes
    )
    fine_charge = fine_charge.reshape(CX, CY, NZ)
    fine_padded = widen(fine_charge)
    mid_charge = restrict(fine_padded)
    mid_padded = widen(mid_charge)
    top_charge = restrict(mid_padded)
    top_potential = top_level(top_charge, top_weights, top_widths)
    mid_potential = cutoff(mid_padded, mid_kernel) + prolong(top_potential)
    return cutoff(fine_padded, near_kernel) + prolong(mid_potential)


def solution(mesh):
    placed = (P(("gx", "gy"), None), P(("gx", "gy")), P(("gx", "gy")), P(), P(), P(), P())
    return jax.shard_map(
        on_device, mesh=mesh, in_specs=placed, out_specs=P("gx", "gy", None), check_vma=False
    )
```

profile of v0, /device:TPU:1, one launch (start us, length us, event | category | flops | bytes accessed | tf_op | source)
XLA Modules:
  0.0 1010.9 jit_solution(12922607085960281120)
XLA Ops:
  13.1 23.0 %gather_fusion = s32[4096]{0:T(1024)S(1)} fusion(s32[4096]{0:T(1024)S(1)} %get-tuple-element.337, s32[4096]{0:T(1024)S(1)} %fusion.87), kind=kCustom, calls=%fused_computation | custom fusion | bytes 49152 | tf_op jit(solution)/shard_map/gather | solution.py:166
  51.2 14.2 %gather_fusion.1 = f32[4096,128]{1,0:T(8,128)} fusion(f32[4096,128]{1,0:T(8,128)S(1)} %broadcast_multiply_fusion, s32[4096]{0:T(1024)S(1)} %fusion.87), kind=kCustom, calls=%fused_computation.1 | custom fusion | bytes 4210688 | tf_op jit(solution)/shard_map/gather | solution.py:165
  76.6 28.6 %all-to-all-done.1 = f32[128,32,128]{2,1,0:T(8,128)S(1)} async-done(((f32[128,32,128]{2,1,0:T(8,128)}), f32[128,32,128]{2,1,0:T(8,128)S(1)}, u32[]{:S(2)}, u32[]{:S(2)}) %all-to-all-start.1) | async-done | bytes 2097184 | tf_op jit(solution)/shard_map/all_to_all | solution.py:168
  105.3 22.5 %scatter_custom_fusion = f32[1536,128]{1,0:T(8,128)S(1)} fusion(s32[4096]{0:T(1024)S(1)} %reshape.227, f32[4096,128]{1,0:T(8,128)S(1)} %bitcast.259, f32[]{:T(128)} %constant.186.clone.1), kind=kCustom, calls=%fused_computation.101 | custom fusion | flops 524288 | bytes 786436 | tf_op jit(solution)/shard_map/scatter-add | solution.py:183
  167.7 19.2 %all_gather.6 = f32[128,6,64]{2,0,1:T(8,128)S(1)} all-gather(f32[8,6,64]{2,0,1:T(8,128)S(1)} %multiply_add_fusion.3), channel_id=1, replica_groups=mesh['gx'=16,'gy'=8] {'gx'}, dimensions={0}, use_global_device_ids=true | all-gather | bytes 208896 | tf_op jit(solution)/shard_map/all_gather | solution.py:138
  189.4 28.4 %all-gather.2.cloned.1.call-done = f32[128,48,64]{0,2,1:T(8,128)} async-done(((f32[128,6,64]{0,2,1:T(8,128)}), f32[128,48,64]{0,2,1:T(8,128)}) %all-gather.2.cloned.1.call-update) | async-done | bytes 1572880 | tf_op jit(solution)/shard_map/all_gather | solution.py:139
  231.6 77.1 %while.29 = (s32[]{:T(128)}, f32[192,128]{1,0:T(8,128)S(1)}, f32[24,20,136]{2,0,1:T(8,128)S(1)}, f32[9,9,9]{2,1,0:T(8,128)}, s32[136,128]{1,0:T(8,128)S(1)}, /*i...) while((s32[]{:T(128)}, f32[192,128]{1,0:T(8,128)S(1)}, ...), condition=%wide.region_5.6_spmd.clone, body=%wide.region_4.5_spmd.clone.sunk | while | flops 378255360 | bytes 19247984 | solution.py:77
  318.7 673.9 %while.28 = (s32[]{:T(128)}, f32[768,256]{0,1:T(8,128)}, f32[40,32,264]{2,1,0:T(8,128)S(1)}, f32[9,9,9]{2,1,0:T(8,128)}, s32[136,128]{1,0:T(8,128)S(1)}, /*index...) while((s32[]{:T(128)}, f32[768,256]{0,1:T(8,128)}, ...), condition=%wide.region_3.4_spmd.clone, body=%wide.region_2.3_spmd.clone.sunk | while | flops 2905602048 | bytes 65639792 | solution.py:77
  347.8 12.1 %copy.166 = f32[32,24,9,136]{3,2,1,0:T(8,128)} copy(f32[32,24,9,136]{3,1,0,2:T(8,128)} %fusion.179) | data formatting | bytes 7520256 | tf_op jit(solution)/shard_map/while/body/eval_jaxpr/stack | solution.py:67
  377.7 12.1 %copy.168 = f32[32,24,9,136]{3,2,1,0:T(8,128)} copy(f32[32,24,9,136]{3,1,0,2:T(8,128)} %get-tuple-element.435) | data formatting | bytes 7520256 | tf_op jit(solution)/shard_map/while/body/eval_jaxpr/stack | solution.py:67
  419.9 12.1 %copy.166 = f32[32,24,9,136]{3,2,1,0:T(8,128)} copy(f32[32,24,9,136]{3,1,0,2:T(8,128)} %fusion.179) | data formatting | bytes 7520256 | tf_op jit(solution)/shard_map/while/body/eval_jaxpr/stack | solution.py:67
  449.9 12.1 %copy.168 = f32[32,24,9,136]{3,2,1,0:T(8,128)} copy(f32[32,24,9,136]{3,1,0,2:T(8,128)} %get-tuple-element.435) | data formatting | bytes 7520256 | tf_op jit(solution)/shard_map/while/body/eval_jaxpr/stack | solution.py:67
  493.2 12.1 %copy.166 = f32[32,24,9,136]{3,2,1,0:T(8,128)} copy(f32[32,24,9,136]{3,1,0,2:T(8,128)} %fusion.179) | data formatting | bytes 7520256 | tf_op jit(solution)/shard_map/while/body/eval_jaxpr/stack | solution.py:67
  523.1 12.1 %copy.168 = f32[32,24,9,136]{3,2,1,0:T(8,128)} copy(f32[32,24,9,136]{3,1,0,2:T(8,128)} %get-tuple-element.435) | data formatting | bytes 7520256 | tf_op jit(solution)/shard_map/while/body/eval_jaxpr/stack | solution.py:67
  566.4 12.1 %copy.166 = f32[32,24,9,136]{3,2,1,0:T(8,128)} copy(f32[32,24,9,136]{3,1,0,2:T(8,128)} %fusion.179) | data formatting | bytes 7520256 | tf_op jit(solution)/shard_map/while/body/eval_jaxpr/stack | solution.py:67
  596.4 12.1 %copy.168 = f32[32,24,9,136]{3,2,1,0:T(8,128)} copy(f32[32,24,9,136]{3,1,0,2:T(8,128)} %get-tuple-element.435) | data formatting | bytes 7520256 | tf_op jit(solution)/shard_map/while/body/eval_jaxpr/stack | solution.py:67
  639.7 12.1 %copy.166 = f32[32,24,9,136]{3,2,1,0:T(8,128)} copy(f32[32,24,9,136]{3,1,0,2:T(8,128)} %fusion.179) | data formatting | bytes 7520256 | tf_op jit(solution)/shard_map/while/body/eval_jaxpr/stack | solution.py:67
  669.6 12.1 %copy.168 = f32[32,24,9,136]{3,2,1,0:T(8,128)} copy(f32[32,24,9,136]{3,1,0,2:T(8,128)} %get-tuple-element.435) | data formatting | bytes 7520256 | tf_op jit(solution)/shard_map/while/body/eval_jaxpr/stack | solution.py:67
  712.9 12.1 %copy.166 = f32[32,24,9,136]{3,2,1,0:T(8,128)} copy(f32[32,24,9,136]{3,1,0,2:T(8,128)} %fusion.179) | data formatting | bytes 7520256 | tf_op jit(solution)/shard_map/while/body/eval_jaxpr/stack | solution.py:67
  742.9 12.1 %copy.168 = f32[32,24,9,136]{3,2,1,0:T(8,128)} copy(f32[32,24,9,136]{3,1,0,2:T(8,128)} %get-tuple-element.435) | data formatting | bytes 7520256 | tf_op jit(solution)/shard_map/while/body/eval_jaxpr/stack | solution.py:67
  816.1 12.1 %copy.168 = f32[32,24,9,136]{3,2,1,0:T(8,128)} copy(f32[32,24,9,136]{3,1,0,2:T(8,128)} %get-tuple-element.435) | data formatting | bytes 7520256 | tf_op jit(solution)/shard_map/while/body/eval_jaxpr/stack | solution.py:67
  859.4 12.1 %copy.166 = f32[32,24,9,136]{3,2,1,0:T(8,128)} copy(f32[32,24,9,136]{3,1,0,2:T(8,128)} %fusion.179) | data formatting | bytes 7520256 | tf_op jit(solution)/shard_map/while/body/eval_jaxpr/stack | solution.py:67
  889.4 12.1 %copy.168 = f32[32,24,9,136]{3,2,1,0:T(8,128)} copy(f32[32,24,9,136]{3,1,0,2:T(8,128)} %get-tuple-element.435) | data formatting | bytes 7520256 | tf_op jit(solution)/shard_map/while/body/eval_jaxpr/stack | solution.py:67
  962.6 12.1 %copy.168 = f32[32,24,9,136]{3,2,1,0:T(8,128)} copy(f32[32,24,9,136]{3,1,0,2:T(8,128)} %get-tuple-element.435) | data formatting | bytes 7520256 | tf_op jit(solution)/shard_map/while/body/eval_jaxpr/stack | solution.py:67
  (482 shorter events, 649.6 us)
Async XLA Ops:
  6.5 218.1 %copy-start = (f32[4]{0:T(128)S(1)}, f32[4]{0:T(128)}, u32[]{:S(2)}) copy-start(f32[4]{0:T(128)} %param.16) | copy-start | bytes 52
  36.9 28.5 %all-to-all-start = ((s32[128,1,32]{2,1,0:T(1,128)}), s32[128,1,32]{2,1,0:T(1,128)S(1)}, u32[]{:S(2)}, u32[]{:S(2)}) async-start(s32[128,1,32]{2,1,0:T(1,128)} %bitcast), calls=%async_computation | async-start | bytes 131072 | tf_op jit(solution)/shard_map/all_to_all | solution.py:175
  65.4 39.9 %all-to-all-start.1 = ((f32[128,32,128]{2,1,0:T(8,128)}), f32[128,32,128]{2,1,0:T(8,128)S(1)}, u32[]{:S(2)}, u32[]{:S(2)}) async-start(f32[128,32,128]{2,1,0:T(8,128)} %bitcast.253), calls=%async_computation.1 | async-start | bytes 4194304 | tf_op jit(solution)/shard_map/all_to_all | solution.py:168
  75.2 142.6 %all-gather.2.cloned.1.call-start = ((), (), s32[]{:S(2)}) async-start(), calls=%async_computation.2 | async-start | bytes 1769472 | tf_op jit(solution)/shard_map/all_gather | solution.py:139
  127.9 6.9 collective-permute-start
  128.8 6.1 collective-permute-start.1
  134.9 7.5 copy-start.5
  135.0 4.6 collective-permute-start.2
  137.3 5.0 collective-permute-start.3
  144.4 43.3 %copy-start.11 = (f32[4]{0:T(128)S(1)}, f32[4]{0:T(128)}, u32[]{:S(2)}) copy-start(f32[4]{0:T(128)} %param.17) | copy-start | bytes 52
  154.4 6.7 collective-permute-start.4
  154.4 6.7 collective-permute-start.5
  161.1 3.4 collective-permute-start.6
  162.4 3.5 collective-permute-start.7
  225.0 5.4 collective-permute-start.8
  230.5 78.3 %collective-permute-start.9 = (f32[9,1,64]{2,0,1:T(8,128)S(1)}, f32[9,1,64]{2,0,1:T(8,128)S(1)}, u32[]{:S(2)}, u32[]{:S(2)}) collective-permute-start(f32[9,1,64]{2,0,1:T(8,128)S(1)} %pad_maximum_fusion.20), channel_id=1, source_target_pairs={{1,0},{2,1},{3,2},{4,3},{5,4},{6,5},{7,6},{0,7},{9,8},{10,9},{11,1... | collective-permute-start | bytes 6920 | tf_op jit(solution)/shard_map/ppermute | solution.py:33
  237.0 3.1 copy-start.3
  288.5 3.1 copy-start.3
  305.6 3.1 copy-start.3
  308.7 6.6 copy-start.6
  309.9 8.5 copy-start.7
  309.9 7.9 collective-permute-start.10
  318.4 676.5 %collective-permute-start.11 = (f32[17,1,128]{2,1,0:T(1,128)}, f32[17,1,128]{2,1,0:T(1,128)}, u32[]{:S(2)}, u32[]{:S(2)}) collective-permute-start(f32[17,1,128]{2,1,0:T(1,128)} %pad_maximum_fusion.19), channel_id=1, source_target_pairs={{1,0},{2,1},{3,2},{4,3},{5,4},{6,5},{7,6},{0,7},{9,8},{10,9},{11,1... | collective-permute-start | bytes 26120 | tf_op jit(solution)/shard_map/ppermute | solution.py:33
  999.6 4.2 copy-start.1
  (27 other events, 48.9 us)
Sparse Core Ops, SparseCore 0:
  187.8 29.9 all-gather.1
where the time goes:
time: 1020 us; the launch traced here: 1010 us
  local copies, waits for them, and re-layouts  633 us (62%)
  matrix products  150 us (15%)
  waiting for transfers between devices  67.2 us (7%)
  other arithmetic  59.7 us (6%)
  starting transfers between devices  48.7 us (5%)
  blocking collectives  19.2 us (2%)
  loops' own time  17.5 us (2%)
  between operations  14.9 us (1%)
    another operation x54, local copies, waits for them, and re-layouts, add_shift(): jnp.stack([window[:, shift_y:shift_y + col_count] for shift_y in range(di...  252 us
    reshape x27, local copies, waits for them, and re-layouts, add_shift(): stacked = stacked.reshape(row_count * col_count, diameter * span)  206 us
    dot_general x27, matrix products, add_shift(): jnp.dot(stacked, banded, precision=PRECISE, preferred_element_type=jnp.fl...  110 us
    while x198, local copies, waits for them, and re-layouts  107 us
    dot_general x18, matrix products, add_shift(): jnp.einsum('ye,ewz->ywz', weights, table, precision=PRECISE)  32.8 us
    all_to_all x1, waiting for transfers between devices, on_device(): lax.all_to_all(outgoing.reshape(device_total, per_owner, ZB), ('gx', 'gy'...  28.6 us
    all_gather x1, waiting for transfers between devices, top_level(): whole = lax.all_gather(column, 'gy', axis=1, tiled=True)  28.4 us
    gather x1, local copies, waits for them, and re-layouts, on_device(): outgoing_ids = local_tile[ordering].reshape(size_x, size_y, per_owner)  23 us
  transfers between devices with their start and end apart: 15, of which 10 were waited for; matrix products, arithmetic and copies ran while one was open for 75% of the time, Pallas kernels for 0%

commit v1 on v0

v1 whole, which is shorter than its diff:
```python
import functools

import jax
import jax.numpy as jnp
import numpy as np
from jax import lax
from jax.experimental import pallas as pl
from jax.experimental.pallas import tpu as pltpu
from jax.sharding import PartitionSpec as P

CX = 32
CY = 24
NZ = 256
CAP = 32
DEVICES = 128
ROWS = CAP + 1
SIZE_X = 16
SIZE_Y = 8
DEAD = 2047
LOW = 9
HIGH = 10
YD = 32
F32 = jnp.float32
BF16 = jnp.bfloat16
PRECISE = lax.Precision.HIGHEST


def mm(a, b):
    return jnp.dot(a, b, preferred_element_type=F32)


def halves(value):
    top = value.astype(BF16)
    return top, (value - top.astype(F32)).astype(BF16)


def np_halves(matrix):
    matrix = np.asarray(matrix, np.float32)
    top = matrix.astype(BF16)
    return top, (matrix - top.astype(np.float32)).astype(BF16)


def route_kernel(tile_ref, info_ref, pos_ref, ids_ref, owner_s, code_s, acc_s):
    tile = tile_ref[...]
    column = tile >> 1
    high_part = column >> 6
    grid_x = (high_part * 43691) >> 17
    grid_y = column - grid_x * (CY * SIZE_Y)
    owner_y = ((grid_y >> 3) * 43) >> 7
    owner = (grid_x >> 5) * SIZE_Y + owner_y
    cell = (tile & 1) * (CX * CY) + (grid_x & (CX - 1)) * CY + (grid_y - owner_y * CY)
    slot = lax.broadcasted_iota(jnp.int32, tile.shape, 0) * 128 + lax.broadcasted_iota(
        jnp.int32, tile.shape, 1
    )
    code = jnp.where(slot < info_ref[0], cell, DEAD)
    owner_s[...] = owner
    code_s[...] = code
    lane_offset = info_ref[1]
    rows = lax.broadcasted_iota(jnp.int32, (128, 128), 0)
    before = lax.broadcasted_iota(jnp.int32, (128, 256), 0)
    after = lax.broadcasted_iota(jnp.int32, (128, 256), 1)
    prefix = jnp.where((before < after) | (after >= 128), 1.0, 0.0).astype(BF16)
    acc_s[...] = jnp.zeros_like(acc_s)

    def chunk(c, base):
        own = owner_s[pl.ds(c, 1), :]
        ids = code_s[pl.ds(c, 1), :]
        hit = rows == own
        one_hot = jnp.where(hit, 1.0, 0.0).astype(BF16)
        counted = mm(one_hot, prefix)
        rank = jnp.sum(jnp.where(hit, counted[:, :128] + base, 0.0), axis=0, keepdims=True)
        rank = rank.astype(jnp.int32)
        pos_ref[pl.ds(c, 1), :] = own * ROWS + rank
        place = jnp.where(rows == rank + lane_offset, 1.0, 0.0).astype(BF16)
        coarse = jnp.where(hit, (ids >> 4).astype(F32), 0.0)
        fine = jnp.where(hit, (ids & 15).astype(F32), 0.0)
        both = jnp.concatenate([coarse, fine], axis=0).astype(BF16)
        acc_s[...] += lax.dot_general(
            both, place, (((1,), (1,)), ((), ())), preferred_element_type=F32
        )
        return base + counted[:, 128:]

    lax.fori_loop(0, tile.shape[0], chunk, jnp.zeros((128, 128), F32), unroll=4)
    ids_ref[...] = acc_s[:128] * 16.0 + acc_s[128:]


def route(tile, info):
    return pl.pallas_call(
        route_kernel,
        out_shape=(
            jax.ShapeDtypeStruct((32, 128), jnp.int32),
            jax.ShapeDtypeStruct((128, 128), F32),
        ),
        in_specs=[
            pl.BlockSpec(memory_space=pltpu.VMEM),
            pl.BlockSpec(memory_space=pltpu.SMEM),
        ],
        out_specs=(
            pl.BlockSpec(memory_space=pltpu.VMEM),
            pl.BlockSpec(memory_space=pltpu.VMEM),
        ),
        scratch_shapes=[
            pltpu.VMEM((32, 128), jnp.int32),
            pltpu.VMEM((32, 128), jnp.int32),
            pltpu.VMEM((256, 128), F32),
        ],
        name="route",
    )(tile, info)


def pack_kernel(pos_ref, data_ref, ids_ref, out_ref):
    step = 16

    def body(b, carry):
        start = pl.multiple_of(b * step, step)
        block = data_ref[pl.ds(start, step), :]
        row = b // (128 // step)
        lane = (b % (128 // step)) * step
        for j in range(step):
            out_ref[pl.ds(pos_ref[row, lane + j], 1), :] = block[j : j + 1]
        return carry

    lax.fori_loop(0, 4096 // step, body, 0)

    def tail(b, carry):
        start = pl.multiple_of(b * 8, 8)
        block = ids_ref[pl.ds(start, 8), :]
        for j in range(8):
            out_ref[pl.ds((start + j) * ROWS + CAP, 1), :] = block[j : j + 1]
        return carry

    lax.fori_loop(0, DEVICES // 8, tail, 0)


def pack(pos, data, ids):
    return pl.pallas_call(
        pack_kernel,
        out_shape=jax.ShapeDtypeStruct((DEVICES * ROWS, 128), F32),
        in_specs=[
            pl.BlockSpec(memory_space=pltpu.SMEM),
            pl.BlockSpec(memory_space=pltpu.VMEM),
            pl.BlockSpec(memory_space=pltpu.VMEM),
        ],
        out_specs=pl.BlockSpec(memory_space=pltpu.VMEM),
        name="pack",
    )(pos, data, ids)


def gather_kernel(in_ref, out_ref, data_s, ids_s):
    for c in range(DEVICES // 4):
        total = None
        for j in range(4):
            base = (c * 4 + j) * ROWS
            top, rest = halves(in_ref[base : base + CAP, :])
            start = (c * 4 + j) * CAP
            data_s[start : start + CAP, :128] = top
            data_s[start : start + CAP, 128:] = rest
            line = in_ref[base + CAP : base + CAP + 1, :]
            total = line if total is None else total + line
        ids_s[c : c + 1, :] = total.astype(jnp.int32)
    rows = lax.broadcasted_iota(jnp.int32, (256, 128), 0)

    def block(b, carry):
        for half in range(2):
            first = half * (CX * CY) + b * 256
            acc = jnp.zeros((256, 256), F32)
            for k in range(16):
                parts = []
                for q in range(2):
                    ids = ids_s[2 * k + q : 2 * k + q + 1, :] - first
                    parts.append(jnp.where(rows == ids, 1.0, 0.0).astype(BF16))
                acc = acc + mm(jnp.concatenate(parts, axis=1), data_s[k * 256 : (k + 1) * 256, :])
            start = pl.multiple_of(b * 256, 256)
            out_ref[pl.ds(start, 256), half * 128 : half * 128 + 128] = acc[:, :128] + acc[:, 128:]
        return carry

    lax.fori_loop(0, 3, block, 0)


def collect(arrived):
    return pl.pallas_call(
        gather_kernel,
        out_shape=jax.ShapeDtypeStruct((CX * CY, NZ), F32),
        in_specs=[pl.BlockSpec(memory_space=pltpu.VMEM)],
        out_specs=pl.BlockSpec(memory_space=pltpu.VMEM),
        scratch_shapes=[
            pltpu.VMEM((DEVICES * CAP, 256), BF16),
            pltpu.VMEM((DEVICES // 4, 128), jnp.int32),
        ],
        name="collect",
    )(arrived)


def z_matrices(period, copies):
    half = period // 2
    z = np.arange(period)[:, None]
    f = np.arange(half)[None, :]
    angle = 2 * np.pi * ((z * f) % period) / period
    cosine, sine = np.cos(angle), -np.sin(angle)
    sine[:, 0] = (-1.0) ** np.arange(period)
    scale = np.full((half, 1), 2.0 / period)
    scale[0] = 1.0 / period
    forward = np.zeros((256, 256))
    inverse = np.zeros((256, 256))
    for c in range(copies):
        rows = slice(c * period, (c + 1) * period)
        real = slice(c * half, (c + 1) * half)
        imag = slice(128 + c * half, 128 + (c + 1) * half)
        forward[rows, real] = cosine
        forward[rows, imag] = sine
        inverse[real, rows] = scale * cosine.T
        inverse[imag, rows] = scale * sine.T
    return forward, inverse


def y_matrices():
    order = np.concatenate([np.arange(17), np.arange(31, 16, -1)])
    y = np.arange(YD)
    angle = 2 * np.pi * ((order[:, None] * y[None, :]) % YD) / YD
    cosine, sine = np.cos(angle), np.sin(angle)
    forward = np.block([[cosine, sine], [-sine, cosine]])
    inverse = np.block([[cosine.T, -sine.T], [sine.T, cosine.T]]) / YD
    return np.kron(np.eye(4), forward), np.kron(np.eye(4), inverse)


def stacked_rows(matrix):
    top, rest = np_halves(matrix)
    return np.concatenate([top, rest], axis=0)


def stacked_cols(matrix):
    top, rest = np_halves(matrix)
    return np.concatenate([top, rest], axis=1)


def right_product(value, matrix_ref):
    top, rest = halves(value)
    return (
        mm(top, matrix_ref[:256, :]) + mm(top, matrix_ref[256:, :]) + mm(rest, matrix_ref[:256, :])
    )


def left_product(matrix_ref, value):
    top, rest = halves(value)
    return (
        mm(matrix_ref[:, :256], top) + mm(matrix_ref[:, 256:], top) + mm(matrix_ref[:, :256], rest)
    )


def special_mask(copies, rows):
    lane = lax.broadcasted_iota(jnp.int32, (rows, 128), 1)
    row = lax.broadcasted_iota(jnp.int32, (rows, 128), 0)
    return (lane & (128 // copies - 1)) == 0, row


def forward_chunk(value, z_ref, y_ref, copies):
    z_freq = right_product(value, z_ref)
    stacks = []
    for h in range(2):
        pieces = []
        for q in range(4):
            slab = z_freq[(h * 4 + q) * YD : (h * 4 + q + 1) * YD]
            pieces += [slab[:, :128], slab[:, 128:]]
        stacks.append(jnp.concatenate(pieces, axis=0))
    freq = left_product(y_ref, jnp.concatenate(stacks, axis=1))
    lane_special, row = special_mask(copies, 16)
    special = lane_special & (row != 0)
    slabs = []
    for h in range(2):
        for q in range(4):
            slab = freq[q * 64 : (q + 1) * 64, h * 128 : (h + 1) * 128]
            ar, br, ai, bi = slab[:16], slab[16:32], slab[32:48], slab[48:]
            slabs.append(
                jnp.concatenate(
                    [
                        jnp.where(special, 0.5 * (ar + br), ar),
                        jnp.where(special, 0.5 * (ai + bi), br),
                        jnp.where(special, 0.5 * (ai - bi), ai),
                        jnp.where(special, 0.5 * (br - ar), bi),
                    ],
                    axis=0,
                )
            )
    return slabs


def inverse_chunk(slabs, z_ref, y_ref):
    stacks = [jnp.concatenate(slabs[h * 4 : h * 4 + 4], axis=0) for h in range(2)]
    space = left_product(y_ref, jnp.concatenate(stacks, axis=1))
    rows = []
    for h in range(2):
        for q in range(4):
            slab = space[q * 64 : (q + 1) * 64, h * 128 : (h + 1) * 128]
            rows.append(jnp.concatenate([slab[:YD], slab[YD:]], axis=1))
    return right_product(jnp.concatenate(rows, axis=0), z_ref)


def taps_kernel(copies, in_ref, z_ref, y_ref, real_ref, twin_ref, imag_ref):
    lane_special, row = special_mask(copies, YD)
    special = lane_special & ((row == 0) | (row == 16))
    for p in range(2):
        slabs = forward_chunk(in_ref[p * 256 : (p + 1) * 256, :], z_ref, y_ref, copies)
        for j in range(8):
            dx = p * 8 + j
            if dx > 8:
                break
            real, imag = slabs[j][:YD], slabs[j][YD:]
            at = slice(dx * YD, (dx + 1) * YD)
            real_ref[at, :] = real
            twin_ref[at, :] = jnp.where(special, imag, real)
            imag_ref[at, :] = jnp.where(special, 0.0, imag)


def taps(kernel, copies, z_matrix, y_matrix):
    flipped = kernel[:, ::-1, ::-1]
    tall = jnp.concatenate(
        [flipped[:, 8:], jnp.zeros((9, YD - 9, 9), F32), flipped[:, :8]], axis=1
    )
    period = 256 // copies
    wide = jnp.concatenate(
        [tall[:, :, 4:], jnp.zeros((9, YD, period - 9), F32), tall[:, :, :4]], axis=2
    )
    wide = jnp.concatenate([wide] * copies, axis=2)
    wide = jnp.concatenate([wide, jnp.zeros((7, YD, 256), F32)], axis=0)
    shape = jax.ShapeDtypeStruct((9 * YD, 128), F32)
    return pl.pallas_call(
        functools.partial(taps_kernel, copies),
        out_shape=(shape, shape, shape),
        in_specs=[pl.BlockSpec(memory_space=pltpu.VMEM)] * 3,
        out_specs=(pl.BlockSpec(memory_space=pltpu.VMEM),) * 3,
        name=f"taps{copies}",
    )(wide.reshape(16 * YD, 256), z_matrix, y_matrix)


def cutoff_kernel(
    copies, slabs_in, block_out, blocks, keep,
    in_ref, real_ref, twin_ref, imag_ref, zf_ref, yf_ref, zi_ref, yi_ref, out_ref, freq_s, conv_s,
):
    for p in range(slabs_in // 8):
        slabs = forward_chunk(in_ref[p * 256 : (p + 1) * 256, :], zf_ref, yf_ref, copies)
        for j in range(8):
            freq_s[(p * 8 + j) * 64 : (p * 8 + j + 1) * 64, :] = slabs[j]
    slabs_out = conv_s.shape[0] // 64
    if block_out * blocks < slabs_out:
        conv_s[block_out * blocks * 64 :, :] = jnp.zeros(
            ((slabs_out - block_out * blocks) * 64, 128), F32
        )
    lane_special, row = special_mask(copies, 8)

    def step(index, carry):
        v = index % 2
        first = (index // 2) * block_out
        sums = [[None] * 4 for _ in range(block_out)]
        for dx in range(9):
            coefs = []
            for half in range(2):
                at = pl.ds(pl.multiple_of(dx * YD + half * 16 + v * 8, 8), 8)
                coefs.append((real_ref[at, :], twin_ref[at, :], imag_ref[at, :]))
            for j in range(block_out):
                base = (first + j + dx) * 64 + v * 8
                for half in range(2):
                    at = pl.multiple_of(base + half * 16, 8)
                    re = freq_s[pl.ds(at, 8), :]
                    im = freq_s[pl.ds(pl.multiple_of(at + 32, 8), 8), :]
                    a, t, b = coefs[half]
                    new_re = a * re - b * im
                    new_im = b * re + t * im
                    old = sums[j]
                    old[2 * half] = new_re if dx == 0 else old[2 * half] + new_re
                    old[2 * half + 1] = new_im if dx == 0 else old[2 * half + 1] + new_im
        special = lane_special & ((row != 0) | (v != 0))
        for j in range(block_out):
            ar, ai, br, bi = sums[j]
            base = (first + j) * 64 + v * 8
            values = (
                jnp.where(special, ar - bi, ar),
                jnp.where(special, ar + bi, br),
                jnp.where(special, ai + br, ai),
                jnp.where(special, br - ai, bi),
            )
            for part in range(4):
                conv_s[pl.ds(pl.multiple_of(base + part * 16, 8), 8), :] = values[part]
        return carry

    lax.fori_loop(0, 2 * blocks, step, 0)
    for p in range(slabs_out // 8):
        slabs = [conv_s[(p * 8 + j) * 64 : (p * 8 + j + 1) * 64, :] for j in range(8)]
        space = inverse_chunk(slabs, zi_ref, yi_ref)
        for j in range(8):
            if p * 8 + j < out_ref.shape[0]:
                out_ref[p * 8 + j] = space[j * YD : j * YD + keep]


def cutoff(padded, spectrum, tables, copies, slabs_in, block_out, blocks, keep, name):
    slabs_out = -(-block_out * blocks // 8) * 8
    return pl.pallas_call(
        functools.partial(cutoff_kernel, copies, slabs_in, block_out, blocks, keep),
        out_shape=jax.ShapeDtypeStruct((block_out * blocks, keep, 256), F32),
        in_specs=[pl.BlockSpec(memory_space=pltpu.VMEM)] * 8,
        out_specs=pl.BlockSpec(memory_space=pltpu.VMEM),
        scratch_shapes=[
            pltpu.VMEM((slabs_in * 64, 128), F32),
            pltpu.VMEM((slabs_out * 64, 128), F32),
        ],
        cost_estimate=pl.CostEstimate(
            flops=slabs_in * 80_000_000, bytes_accessed=slabs_in * 65536, transcendentals=0
        ),
        name=name,
    )(padded, *spectrum, *tables)


def halo(block, axis, dim, low, high):
    count = lax.axis_size(axis)
    forward = [(i, (i + 1) % count) for i in range(count)]
    backward = [(target, source) for source, target in forward]
    length = block.shape[dim]
    before = lax.ppermute(lax.slice_in_dim(block, length - low, length, axis=dim), axis, forward)
    behind = lax.ppermute(lax.slice_in_dim(block, 0, high, axis=dim), axis, backward)
    return jnp.concatenate([before, block, behind], axis=dim)


def thin_x(values):
    length = values.shape[0]
    centre = values[1 : length - 1 : 2]
    return centre + 0.5 * (values[0 : length - 2 : 2] + values[2:length:2])


def thin_matrix(length):
    count = (length - 1) // 2
    matrix = np.zeros((count, length), np.float32)
    for i in range(count):
        matrix[i, 2 * i : 2 * i + 3] = (0.5, 1.0, 0.5)
    return matrix


def thin_cycle(length):
    matrix = np.zeros((length, length // 2), np.float32)
    for i in range(length // 2):
        matrix[2 * i, i] += 1.0
        matrix[(2 * i - 1) % length, i] += 0.5
        matrix[(2 * i + 1) % length, i] += 0.5
    return matrix


def grow_matrix(count, source):
    matrix = np.zeros((count, source), np.float32)
    for i in range(count):
        if i % 2 == 0:
            matrix[i, i // 2] = 1.0
        else:
            matrix[i, i // 2] = 0.5
            matrix[i, i // 2 + 1] = 0.5
    return matrix


def grow_cycle(source):
    matrix = np.zeros((source, 2 * source), np.float32)
    for i in range(source):
        matrix[i, 2 * i] = 1.0
        matrix[i, 2 * i + 1] += 0.5
        matrix[(i + 1) % source, 2 * i + 1] += 0.5
    return matrix


def thin(values):
    values = thin_x(values)
    values = jnp.einsum("xyz,zc->xyc", values, thin_cycle(values.shape[2]), precision=PRECISE)
    return jnp.einsum("by,xyc->xbc", thin_matrix(values.shape[1]), values, precision=PRECISE)


def grow(values, count_x, count_y):
    size_x, size_y, depth = values.shape
    values = jnp.einsum("jb,abc->ajc", grow_matrix(count_y, size_y), values, precision=PRECISE)
    values = jnp.einsum("ia,ajc->ijc", grow_matrix(count_x, size_x), values, precision=PRECISE)
    return jnp.einsum("ijc,cz->ijz", values, grow_cycle(depth), precision=PRECISE)


def gaussians(period, widths, first_row, row_count):
    row_ids = first_row + jnp.arange(row_count, dtype=jnp.int32)[:, None]
    col_ids = jnp.arange(period, dtype=jnp.int32)[None, :]
    offset = (row_ids - col_ids) % period
    distance = jnp.minimum(offset, period - offset).astype(F32)
    return jnp.exp(-(distance * distance)[None] / (widths * widths)[:, None, None])


def spread_all(values, axis):
    count = lax.axis_size(axis)
    copies = jnp.broadcast_to(values[None], (count,) + values.shape)
    return lax.all_to_all(copies, axis, split_axis=0, concat_axis=0, tiled=True)


def top_level(top_charge, top_weights, top_widths):
    rows_x, rows_y, depth = top_charge.shape
    gauss_x = gaussians(
        rows_x * SIZE_X, top_widths, lax.axis_index("gx") * rows_x, rows_x + 1
    )
    gauss_y = gaussians(
        rows_y * SIZE_Y, top_widths, lax.axis_index("gy") * rows_y, rows_y + 1
    )
    gauss_z = gaussians(depth, top_widths, 0, depth) * top_weights[:, None, None]
    column = spread_all(top_charge, "gx").reshape(SIZE_X * rows_x, rows_y, depth)
    plane = jnp.einsum("kia,abc->kibc", gauss_x, column, precision=PRECISE)
    whole = spread_all(plane, "gy")
    along_y = jnp.einsum(
        "kjsb,skibc->kijc",
        gauss_y.reshape(4, rows_y + 1, SIZE_Y, rows_y),
        whole,
        precision=PRECISE,
    )
    return jnp.einsum("kzc,kijc->ijz", gauss_z, along_y, precision=PRECISE)


def on_device(
    charge_blocks, block_tile, block_count, near_kernel, mid_kernel, top_weights, top_widths
):
    device = lax.axis_index("gx") * SIZE_Y + lax.axis_index("gy")
    info = jnp.stack([block_count[0], (device % 4) * CAP]).astype(jnp.int32)
    pos, ids = route(block_tile.reshape(32, 128), info)
    outgoing = pack(pos, charge_blocks, ids)
    arrived = lax.all_to_all(
        outgoing.reshape(DEVICES, ROWS, 1, 128),
        ("gx", "gy"),
        split_axis=0,
        concat_axis=0,
        tiled=True,
    ).reshape(DEVICES * ROWS, 128)

    z_fine, z_fine_back = z_matrices(256, 1)
    z_mid, z_mid_back = z_matrices(128, 2)
    y_forward, y_back = y_matrices()
    fine_tables = (
        stacked_rows(z_fine), stacked_cols(y_forward), stacked_rows(z_fine_back), stacked_cols(y_back)
    )
    mid_tables = (
        stacked_rows(z_mid), fine_tables[1], stacked_rows(z_mid_back), fine_tables[3]
    )
    fine_taps = taps(near_kernel, 1, fine_tables[0], fine_tables[1])
    mid_taps = taps(mid_kernel, 2, mid_tables[0], mid_tables[1])

    fine = collect(arrived).reshape(CX, CY, NZ)
    wide = halo(halo(fine, "gx", 0, LOW, HIGH), "gy", 1, LOW, HIGH)
    mid = thin(wide)
    top = thin(mid[3:20, 3:16])
    top_potential = top_level(top, top_weights, top_widths)
    near_input = wide[5:45, 5:37].reshape(40 * YD, NZ)
    near = cutoff(near_input, fine_taps, fine_tables, 1, 40, 8, 4, CY, "near")
    tall = jnp.pad(mid, ((0, 8), (0, YD - mid.shape[1]), (0, 0)))
    mid_input = jnp.concatenate([tall[:24], tall[9:33]], axis=2).reshape(24 * YD, 256)
    mid_pair = cutoff(mid_input, mid_taps, mid_tables, 2, 24, 9, 1, 16, "middle")
    mid_near = jnp.concatenate([mid_pair[:, :13, :128], mid_pair[:8, :13, 128:]], axis=0)
    mid_potential = mid_near + grow(top_potential, 17, 13)
    return near + grow(mid_potential, CX, CY)


def solution(mesh):
    placed = (P(("gx", "gy"), None), P(("gx", "gy")), P(("gx", "gy")), P(), P(), P(), P())
    return jax.shard_map(
        on_device, mesh=mesh, in_specs=placed, out_specs=P("gx", "gy", None), check_vma=False
    )
```

time: 1020 us -> 165 us (0.16)
  local copies, waits for them, and re-layouts: 633 us -> 27 us
  matrix products: 150 us -> 9.14 us
  other arithmetic: 59.7 us -> 9.38 us
  Pallas kernels: 0 us -> 43.1 us
  starting transfers between devices: 48.7 us -> 25.5 us
  blocking collectives: 19.2 us -> 0 us
  waiting for transfers between devices: 67.2 us -> 49 us
  loops' own time: 17.5 us -> 0 us
  between operations: 14.9 us -> 1.22 us
    another operation x59 -> x1, local copies, waits for them, and re-layouts: 255 us -> 0.01 us  [the longest x54 252 us: add_shift(): jnp.stack([window[:, shift_y:shift_y + col_count] for shift_y in range(di...]
    reshape x31 -> x1, local copies, waits for them, and re-layouts: 209 us -> 0.26 us  [on_device(): fine = collect(arrived).reshape(CX, CY, NZ)]
    dot_general x49 -> x13, matrix products: 150 us -> 9.14 us  [the longest x2 3.72 us: thin(): jnp.einsum('xyz,zc->xyc', values, thin_cycle(values.shape[2]), precision=...]
    while x199 -> x0, local copies, waits for them, and re-layouts: 110 us -> none
    pallas_call x0 -> x7, Pallas kernels: none -> 43.1 us  [the longest x1 14.2 us: pack(): pl.pallas_call(pack_kernel, out_shape=jax.ShapeDtypeStruct((DEVICES * ROW...]
    gather x2 -> x0, local copies, waits for them, and re-layouts: 37.2 us -> none  [the longest x1 23 us: on_device(): outgoing_ids = local_tile[ordering].reshape(size_x, size_y, per_owner)]
    all_gather x1 -> x0, waiting for transfers between devices: 28.4 us -> none  [top_level(): whole = lax.all_gather(column, 'gy', axis=1, tiled=True)]
    ppermute x12 -> x4, starting transfers between devices: 27.4 us -> 4.08 us  [the longest x2 2.76 us: halo(): lax.ppermute(lax.slice_in_dim(block, length - low, length, axis=dim), axi...]
  transfers between devices with their start and end apart: 15 -> 7, of which waited for: 10 -> 4; matrix products, arithmetic and copies ran while one was open for 75% -> 5% of each run, Pallas kernels for 0% -> 10%
where the time goes in v1:
time: 165 us; the launch traced here: 164 us
  waiting for transfers between devices  49 us (30%)
  Pallas kernels  43.1 us (26%)
  local copies, waits for them, and re-layouts  27 us (16%)
  starting transfers between devices  25.5 us (15%)
  other arithmetic  9.38 us (6%)
  matrix products  9.14 us (6%)
    all_to_all x1, waiting for transfers between devices, on_device(): lax.all_to_all(outgoing.reshape(DEVICES, ROWS, 1, 128), ('gx', 'gy'), spl...  30.1 us
    pallas_call x1, Pallas kernels, pack(): pl.pallas_call(pack_kernel, out_shape=jax.ShapeDtypeStruct((DEVICES * ROW...  14.2 us
    ppermute x2, waiting for transfers between devices, halo(): lax.ppermute(lax.slice_in_dim(block, length - low, length, axis=dim), axi...  12.1 us
    pallas_call x2, Pallas kernels, cutoff(): pl.pallas_call(functools.partial(cutoff_kernel, copies, slabs_in, block_o...  11.5 us
    all_to_all x1, starting transfers between devices, on_device(): lax.all_to_all(outgoing.reshape(DEVICES, ROWS, 1, 128), ('gx', 'gy'), spl...  11.5 us
    all_to_all x2, starting transfers between devices, spread_all(): return lax.all_to_all(copies, axis, split_axis=0, concat_axis=0, tiled=True)  9.93 us
    slice x2, local copies, waits for them, and re-layouts, thin_x(): return centre + 0.5 * (values[0:length - 2:2] + values[2:length:2])  8.38 us
    pallas_call x1, Pallas kernels, collect(): pl.pallas_call(gather_kernel, out_shape=jax.ShapeDtypeStruct((CX * CY, NZ...  6.62 us
  transfers between devices with their start and end apart: 7, of which 4 were waited for; matrix products, arithmetic and copies ran while one was open for 5% of the time, Pallas kernels for 10%

profile of v1, /device:TPU:1, one launch (start us, length us, event | category | flops | bytes accessed | tf_op | source)
XLA Modules:
  0.0 164.4 jit_solution(4853303477724148742)
XLA Ops:
  1.3 5.1 %route.1 = (s32[32,128]{1,0:T(8,128)}, f32[128,128]{1,0:T(8,128)}) custom-call(s32[32,128]{1,0:T(8,128)} %bitcast.90, s32[2]{0:T(128)} %pad_add_fusion.info_ref), custom_call_target="tpu_custom_call" | custom-call | tf_op jit(solution)/shard_map/route/pallas_call | solution.py:88
  6.4 14.2 %pack.1 = f32[4224,128]{1,0:T(8,128)} custom-call(s32[32,128]{1,0:T(8,128)} %get-tuple-element.13.pos_ref, f32[4096,128]{1,0:T(8,128)} %data_ref.1, f32[128,128]{1,0:T(8,128)} %get-tuple-element.14.ids_ref), custom_call_target="tpu_custom_call" | custom-call | tf_op jit(solution)/shard_map/pack/pallas_call | solution.py:136
  20.7 11.5 %all-to-all-start = ((f32[128,33,1,128]{3,2,1,0:T(1,128)}), f32[128,33,1,128]{3,2,1,0:T(1,128)S(1)}, u32[]{:S(2)}, u32[]{:S(2)}) async-start(f32[128,33,1,128]{3,2,1,0:T(1,128)} %bitcast.79), calls=%async_computation | async-start | bytes 4325376 | tf_op jit(solution)/shard_map/all_to_all | solution.py:520
  32.9 30.1 %all-to-all-done = f32[128,33,1,128]{3,2,1,0:T(1,128)S(1)} async-done(((f32[128,33,1,128]{3,2,1,0:T(1,128)}), f32[128,33,1,128]{3,2,1,0:T(1,128)S(1)}, u32[]{:S(2)}, u32[]{:S(2)}) %all-to-all-start) | async-done | bytes 2162720 | tf_op jit(solution)/shard_map/all_to_all | solution.py:520
  63.0 1.4 copy-done
  64.3 6.6 %collect.1 = f32[768,256]{1,0:T(8,128)} custom-call(f32[4224,128]{1,0:T(8,128)} %bitcast.78), custom_call_target="tpu_custom_call" | custom-call | tf_op jit(solution)/shard_map/collect/pallas_call | solution.py:181
  72.8 1.3 collective-permute-start.1
  75.0 12.1 %collective-permute-done = f32[9,24,256]{2,0,1:T(8,128)S(1)} collective-permute-done((f32[9,24,256]{2,0,1:T(8,128)S(1)}, f32[9,24,256]{2,0,1:T(8,128)S(1)}, u32[]{:S(2)}, u32[]{:S(2)}) %collective-permute-start) | collective-permute-done | bytes 221216 | tf_op jit(solution)/shard_map/ppermute | solution.py:417
  88.0 2.5 %collective-permute-start.2 = (f32[51,9,256]{2,0,1:T(8,128)}, f32[51,9,256]{2,0,1:T(8,128)S(1)}, u32[]{:S(2)}, u32[]{:S(2)}) collective-permute-start(f32[51,9,256]{2,0,1:T(8,128)} %pad_maximum_fusion.4), channel_id=1, source_target_pairs={{0,1},{1,2},{2,3},{3,4},{4,5},{5,6},{6,7},{7,0},{8,9},{9,10},{10,1... | collective-permute-start | bytes 1410056 | tf_op jit(solution)/shard_map/ppermute | solution.py:417
  93.5 2.8 %taps2.1 = (f32[288,128]{1,0:T(8,128)}, f32[288,128]{1,0:T(8,128)}, f32[288,128]{1,0:T(8,128)}) custom-call(f32[512,256]{1,0:T(8,128)} %bitcast.85, bf16[512,256]{1,0:T(8,128)(2,1)} %constant.115.clone.z_ref.zf_ref, bf16[256,512]{1,0:T(8,128)(2,1)} %constant.114.clone.y_ref.yf_ref), custom_call_target="tpu_custom_call" | custom-call | tf_op jit(solution)/shard_map/taps2/pallas_call | solution.py:326
  96.3 2.8 %taps1.1 = (f32[288,128]{1,0:T(8,128)}, f32[288,128]{1,0:T(8,128)}, f32[288,128]{1,0:T(8,128)}) custom-call(f32[512,256]{1,0:T(8,128)} %bitcast.84, bf16[512,256]{1,0:T(8,128)(2,1)} %constant.113.clone.z_ref.zf_ref, bf16[256,512]{1,0:T(8,128)(2,1)} %constant.114.clone.y_ref.yf_ref), custom_call_target="tpu_custom_call" | custom-call | tf_op jit(solution)/shard_map/taps1/pallas_call | solution.py:326
  100.9 1.7 %pad_maximum_fusion = f32[51,43,256]{2,0,1:T(8,128)S(1)} fusion(f32[51,10,256]{2,0,1:T(8,128)} %collective-permute-done.3, f32[10,24,256]{2,0,1:T(8,128)} %copy-done.2, f32[32,24,256]{2,0,1:T(8,128)S(1)} %copy.42, f32[9,24,256]{2,0,1:T(8,128)} %copy-done.3, f32[51,9,256]{2,0,1:T(8,128)} %copy-done.5), kind=kLoop, calls=%fused_computation | loop fusion | flops 2245632 | bytes 4491264 | tf_op jit(solution)/shard_map/concatenate | solution.py:419
  102.6 4.2 %slice.104 = f32[25,43,256]{2,0,1:T(8,128)} slice(f32[51,43,256]{2,0,1:T(8,128)S(1)} %pad_maximum_fusion), slice={[1:50:2], [0:43:1], [0:256:1]} | slice | bytes 2201600 | tf_op jit(solution)/shard_map/slice | solution.py:424
  106.8 4.2 %slice.105 = f32[25,43,256]{2,0,1:T(8,128)} slice(f32[51,43,256]{2,0,1:T(8,128)S(1)} %pad_maximum_fusion), slice={[0:49:2], [0:43:1], [0:256:1]} | slice | bytes 2201600 | tf_op jit(solution)/shard_map/slice | solution.py:425
  110.9 4.2 %slice.106 = f32[25,43,256]{2,0,1:T(8,128)} slice(f32[51,43,256]{2,0,1:T(8,128)S(1)} %pad_maximum_fusion), slice={[2:51:2], [0:43:1], [0:256:1]} | slice | bytes 2201600 | tf_op jit(solution)/shard_map/slice | solution.py:425
  115.2 3.5 %fusion = f32[25,43,128]{2,0,1:T(8,128)S(1)} fusion(f32[256,128,1]{1,0,2:T(8,128)S(1)} %copy-done.7, f32[25,43,256]{2,0,1:T(8,128)} %slice.104, f32[25,43,256]{2,0,1:T(8,128)} %slice.105, f32[25,43,256]{2,0,1:T(8,128)} %slice.106), kind=kOutput, calls=%fused_computation.1 | convolution fusion | flops 423532800 | bytes 3983872 | tf_op jit(solution)/shard_map/xyz,zc->xyc/dot_general | solution.py:467
  120.9 3.5 %all-to-all-start.1 = ((f32[16,1,3072]{2,1,0:T(1,128)}), f32[16,1,3072]{2,1,0:T(1,128)S(1)}, u32[]{:S(2)}, u32[]{:S(2)}) async-start(f32[16,1,3072]{2,1,0:T(1,128)} %reshape.167), calls=%async_computation.1 | async-start | bytes 393216 | tf_op jit(solution)/shard_map/all_to_all | solution.py:489
  125.4 6.1 %all-to-all-done.1 = f32[16,1,3072]{2,1,0:T(1,128)S(1)} async-done(((f32[16,1,3072]{2,1,0:T(1,128)}), f32[16,1,3072]{2,1,0:T(1,128)S(1)}, u32[]{:S(2)}, u32[]{:S(2)}) %all-to-all-start.1) | async-done | bytes 196640 | tf_op jit(solution)/shard_map/all_to_all | solution.py:489
  134.0 1.6 reshape.169
  135.6 6.4 %all-to-all-start.2 = ((f32[8,1,13824]{2,1,0:T(1,128)}), f32[8,1,13824]{2,1,0:T(1,128)S(1)}, u32[]{:S(2)}, u32[]{:S(2)}) async-start(f32[8,1,13824]{2,1,0:T(1,128)} %reshape.169), calls=%async_computation.2 | async-start | bytes 884736 | tf_op jit(solution)/shard_map/all_to_all | solution.py:489
  142.0 4.6 %middle.1 = f32[9,16,256]{2,1,0:T(8,128)} custom-call(f32[768,256]{1,0:T(8,128)} %bitcast.89, f32[288,128]{1,0:T(8,128)} %get-tuple-element.18.real_ref, f32[288,128]{1,0:T(8,128)} %get-tuple-element.19.twin_ref, f32[288,128]{1,0:T(8,128)} %get-tuple-element.20.imag_ref, bf16[512,256]{1,0:T(8,128)(2,1)} %constant.115.clone.z_ref.zf_ref, ...), custom_call_target="tpu_custom_call" | custom-call | flops 1920000000 | bytes 1572864 | tf_op jit(solution)/shard_map/middle/pallas_call | solution.py:396
  148.5 1.5 copy.43
  150.0 6.9 %near.1 = f32[32,24,256]{2,1,0:T(8,128)} custom-call(f32[1280,256]{1,0:T(8,128)} %bitcast.87, f32[288,128]{1,0:T(8,128)} %get-tuple-element.15.real_ref, f32[288,128]{1,0:T(8,128)} %get-tuple-element.16.twin_ref, f32[288,128]{1,0:T(8,128)} %get-tuple-element.17.imag_ref, bf16[512,256]{1,0:T(8,128)(2,1)} %constant.113.clone.z_ref.zf_ref, ...), custom_call_target="tpu_custom_call" | custom-call | flops 3200000000 | bytes 2621440 | tf_op jit(solution)/shard_map/near/pallas_call | solution.py:396
  156.9 1.7 %reduce.1 = f32[8,13824]{1,0:T(8,128)S(1)} reduce(f32[8,1,13824]{2,1,0:T(1,128)S(1)} %all-to-all-done.2, f32[]{:T(128)} %broadcast.145), dimensions={1}, to_apply=%all_to_all.11.reduce_sub_computation | reduce | bytes 884740 | tf_op jit(solution)/shard_map/all_to_all | solution.py:489
  (109 shorter events, 22.5 us)
Async XLA Ops:
  20.7 11.5 %copy-start.10 = (f32[9,9,9]{2,1,0:T(8,128)S(1)}, f32[9,9,9]{2,1,0:T(8,128)}, u32[]{:S(2)}) copy-start(f32[9,9,9]{2,1,0:T(8,128)} %param.27) | copy-start | bytes 8752
  20.7 11.5 %copy-start.11 = (f32[9,9,9]{2,1,0:T(8,128)S(1)}, f32[9,9,9]{2,1,0:T(8,128)}, u32[]{:S(2)}) copy-start(f32[9,9,9]{2,1,0:T(8,128)} %param.26) | copy-start | bytes 8752
  20.7 42.3 %all-to-all-start = ((f32[128,33,1,128]{3,2,1,0:T(1,128)}), f32[128,33,1,128]{3,2,1,0:T(1,128)S(1)}, u32[]{:S(2)}, u32[]{:S(2)}) async-start(f32[128,33,1,128]{3,2,1,0:T(1,128)} %bitcast.79), calls=%async_computation | async-start | bytes 4325376 | tf_op jit(solution)/shard_map/all_to_all | solution.py:520
  70.9 3.4 %slice-start = ((f32[768,256]{1,0:T(8,128)}), f32[216,256]{1,0:T(8,128)S(1)}, s32[]{:S(2)}) async-start(f32[768,256]{1,0:T(8,128)} %collect.1), calls=%async_computation.3 | async-start | bytes 442368 | tf_op jit(solution)/shard_map/slice | solution.py:417
  71.9 2.8 %copy-start.1 = (f32[768,256]{1,0:T(8,128)S(1)}, f32[768,256]{1,0:T(8,128)}, u32[]{:S(2)}) copy-start(f32[768,256]{1,0:T(8,128)} %collect.1) | copy-start | bytes 2359300
  72.8 14.3 %collective-permute-start.1 = (f32[10,24,256]{2,0,1:T(8,128)}, f32[10,24,256]{2,0,1:T(8,128)S(1)}, u32[]{:S(2)}, u32[]{:S(2)}) collective-permute-start(f32[10,24,256]{2,0,1:T(8,128)} %copy.41), channel_id=1, source_target_pairs={{8,0},{16,8},{24,16},{32,24},{40,32},{48,40},{56,48},{64,56},{72,6... | collective-permute-start | bytes 737288 | tf_op jit(solution)/shard_map/ppermute | solution.py:418
  74.4 12.7 %collective-permute-start = (f32[9,24,256]{2,0,1:T(8,128)S(1)}, f32[9,24,256]{2,0,1:T(8,128)S(1)}, u32[]{:S(2)}, u32[]{:S(2)}) collective-permute-start(f32[9,24,256]{2,0,1:T(8,128)S(1)} %copy.40), channel_id=1, source_target_pairs={{0,8},{8,16},{16,24},{24,32},{32,40},{40,48},{48,56},{56,64},{64,7... | collective-permute-start | bytes 663560 | tf_op jit(solution)/shard_map/ppermute | solution.py:417
  87.1 4.3 %copy-start.3 = (f32[9,24,256]{2,0,1:T(8,128)}, f32[9,24,256]{2,0,1:T(8,128)S(1)}, u32[]{:S(2)}) copy-start(f32[9,24,256]{2,0,1:T(8,128)S(1)} %collective-permute-done) | copy-start | bytes 663556
  87.1 4.3 %copy-start.2 = (f32[10,24,256]{2,0,1:T(8,128)}, f32[10,24,256]{2,0,1:T(8,128)S(1)}, u32[]{:S(2)}) copy-start(f32[10,24,256]{2,0,1:T(8,128)S(1)} %collective-permute-done.1) | copy-start | bytes 737284
  88.0 3.4 %copy-start.18 = (f32[4]{0:T(128)S(1)}, f32[4]{0:T(128)}, u32[]{:S(2)}) copy-start(f32[4]{0:T(128)} %param.29) | copy-start | bytes 52
  88.0 11.3 %collective-permute-start.2 = (f32[51,9,256]{2,0,1:T(8,128)}, f32[51,9,256]{2,0,1:T(8,128)S(1)}, u32[]{:S(2)}, u32[]{:S(2)}) collective-permute-start(f32[51,9,256]{2,0,1:T(8,128)} %pad_maximum_fusion.4), channel_id=1, source_target_pairs={{0,1},{1,2},{2,3},{3,4},{4,5},{5,6},{6,7},{7,0},{8,9},{9,10},{10,1... | collective-permute-start | bytes 1410056 | tf_op jit(solution)/shard_map/ppermute | solution.py:417
  91.4 9.4 %collective-permute-start.3 = (f32[51,10,256]{2,0,1:T(8,128)}, f32[51,10,256]{2,0,1:T(8,128)}, u32[]{:S(2)}, u32[]{:S(2)}) collective-permute-start(f32[51,10,256]{2,0,1:T(8,128)} %pad_maximum_fusion.2), channel_id=1, source_target_pairs={{1,0},{2,1},{3,2},{4,3},{5,4},{6,5},{7,6},{0,7},{9,8},{10,9},{11,1... | collective-permute-start | bytes 1566728 | tf_op jit(solution)/shard_map/ppermute | solution.py:418
  110.9 4.2 %copy-start.7 = (f32[256,128,1]{1,0,2:T(8,128)S(1)}, f32[256,128,1]{1,0,2:T(8,128)}, u32[]{:S(2)}) copy-start(f32[256,128,1]{1,0,2:T(8,128)} %constant.137) | copy-start | bytes 393220
  115.2 3.5 %copy-start.12 = (f32[21,43,1]{1,0,2:T(8,128)S(1)}, f32[21,43,1]{1,0,2:T(8,128)}, u32[]{:S(2)}) copy-start(f32[21,43,1]{1,0,2:T(8,128)} %constant.138) | copy-start | bytes 10840
  115.2 4.4 %copy-start.9 = (f32[128,64,1]{0,1,2:T(8,128)S(1)}, f32[128,64,1]{0,1,2:T(8,128)}, u32[]{:S(2)}) copy-start(f32[128,64,1]{0,1,2:T(8,128)} %constant.140) | copy-start | bytes 98308
  115.2 4.6 %copy-start.17 = (f32[6,13,1]{1,0,2:T(8,128)S(1)}, f32[6,13,1]{1,0,2:T(8,128)}, u32[]{:S(2)}) copy-start(f32[6,13,1]{1,0,2:T(8,128)} %constant.141) | copy-start | bytes 940
  120.9 10.7 %all-to-all-start.1 = ((f32[16,1,3072]{2,1,0:T(1,128)}), f32[16,1,3072]{2,1,0:T(1,128)S(1)}, u32[]{:S(2)}, u32[]{:S(2)}) async-start(f32[16,1,3072]{2,1,0:T(1,128)} %reshape.167), calls=%async_computation.1 | async-start | bytes 393216 | tf_op jit(solution)/shard_map/all_to_all | solution.py:489
  135.6 21.3 %all-to-all-start.2 = ((f32[8,1,13824]{2,1,0:T(1,128)}), f32[8,1,13824]{2,1,0:T(1,128)S(1)}, u32[]{:S(2)}, u32[]{:S(2)}) async-start(f32[8,1,13824]{2,1,0:T(1,128)} %reshape.169), calls=%async_computation.2 | async-start | bytes 884736 | tf_op jit(solution)/shard_map/all_to_all | solution.py:489
  158.6 2.3 %copy-start.15 = (f32[17,9,1]{0,1,2:T(8,128)S(1)}, f32[17,9,1]{0,1,2:T(8,128)}, u32[]{:S(2)}) copy-start(f32[17,9,1]{0,1,2:T(8,128)} %constant.139) | copy-start | bytes 1840
  159.1 2.1 %copy-start.8 = (f32[64,128,1]{1,0,2:T(8,128)S(1)}, f32[64,128,1]{1,0,2:T(8,128)}, u32[]{:S(2)}) copy-start(f32[64,128,1]{1,0,2:T(8,128)} %constant.143) | copy-start | bytes 98308
  159.1 2.4 %copy-start.14 = (f32[24,13,1]{0,1,2:T(8,128)S(1)}, f32[24,13,1]{0,1,2:T(8,128)}, u32[]{:S(2)}) copy-start(f32[24,13,1]{0,1,2:T(8,128)} %constant.144) | copy-start | bytes 3748
  159.2 2.8 %copy-start.13 = (f32[32,17,1]{0,1,2:T(8,128)S(1)}, f32[32,17,1]{0,1,2:T(8,128)}, u32[]{:S(2)}) copy-start(f32[32,17,1]{0,1,2:T(8,128)} %constant.136) | copy-start | bytes 6532
  160.2 2.3 %copy-start.6 = (f32[128,256,1]{1,0,2:T(8,128)S(1)}, f32[128,256,1]{1,0,2:T(8,128)}, u32[]{:S(2)}) copy-start(f32[128,256,1]{1,0,2:T(8,128)} %constant.145) | copy-start | bytes 393220
  161.3 2.1 %copy-start.4 = (f32[32,24,256]{2,1,0:T(8,128)S(1)}, f32[32,24,256]{2,1,0:T(8,128)}, u32[]{:S(2)}) copy-start(f32[32,24,256]{2,1,0:T(8,128)} %near.1) | copy-start | bytes 2359300
  (4 other events, 5.8 us)

commit v2 on v1

v2 whole, which is shorter than its diff:
```python
import functools

import jax
import jax.numpy as jnp
import numpy as np
from jax import lax
from jax.experimental import pallas as pl
from jax.experimental.pallas import tpu as pltpu
from jax.sharding import PartitionSpec as P

CX = 32
CY = 24
NZ = 256
CAP = 32
DEVICES = 128
ROWS = CAP + 1
SIZE_X = 16
SIZE_Y = 8
DEAD = 2047
SEND = 376
TOP_ROWS = 40
YD = 32
F32 = jnp.float32
BF16 = jnp.bfloat16
VM = pl.BlockSpec(memory_space=pltpu.VMEM)
SM = pl.BlockSpec(memory_space=pltpu.SMEM)
ANY = pl.BlockSpec(memory_space=pl.ANY)


def call(body, name, out, ins, scratch=(), limit=20, flops=0, moved=0):
    many = isinstance(out, tuple)
    return pl.pallas_call(
        body,
        out_shape=out,
        in_specs=ins,
        out_specs=(VM,) * len(out) if many else VM,
        scratch_shapes=list(scratch),
        compiler_params=pltpu.CompilerParams(vmem_limit_bytes=limit << 20),
        cost_estimate=pl.CostEstimate(flops=flops, bytes_accessed=moved, transcendentals=0),
        name=name,
    )


def array(*shape):
    return jax.ShapeDtypeStruct(shape, F32)


def mm(a, b):
    return jnp.dot(a, b, preferred_element_type=F32)


def halves(value):
    top = value.astype(BF16)
    return top, (value - top.astype(F32)).astype(BF16)


def np_halves(matrix):
    matrix = np.asarray(matrix, np.float32)
    top = matrix.astype(BF16)
    return top, (matrix - top.astype(np.float32)).astype(BF16)


def route_kernel(tile_ref, info_ref, pos_ref, ids_ref, owner_s, code_s, acc_s):
    tile = tile_ref[...]
    column = tile >> 1
    high_part = column >> 6
    grid_x = (high_part * 43691) >> 17
    grid_y = column - grid_x * (CY * SIZE_Y)
    owner_y = ((grid_y >> 3) * 43) >> 7
    owner = (grid_x >> 5) * SIZE_Y + owner_y
    cell = (tile & 1) * (CX * CY) + (grid_x & (CX - 1)) * CY + (grid_y - owner_y * CY)
    slot = lax.broadcasted_iota(jnp.int32, tile.shape, 0) * 128 + lax.broadcasted_iota(
        jnp.int32, tile.shape, 1
    )
    code = jnp.where(slot < info_ref[0], cell, DEAD)
    owner_s[...] = owner
    code_s[...] = code
    lane_offset = info_ref[1]
    rows = lax.broadcasted_iota(jnp.int32, (128, 128), 0)
    before = lax.broadcasted_iota(jnp.int32, (128, 256), 0)
    after = lax.broadcasted_iota(jnp.int32, (128, 256), 1)
    prefix = jnp.where((before < after) | (after >= 128), 1.0, 0.0).astype(BF16)
    acc_s[...] = jnp.zeros_like(acc_s)

    def chunk(c, base):
        own = owner_s[pl.ds(c, 1), :]
        ids = code_s[pl.ds(c, 1), :]
        hit = rows == own
        one_hot = jnp.where(hit, 1.0, 0.0).astype(BF16)
        counted = mm(one_hot, prefix)
        rank = jnp.sum(jnp.where(hit, counted[:, :128] + base, 0.0), axis=0, keepdims=True)
        rank = rank.astype(jnp.int32)
        pos_ref[pl.ds(c, 1), :] = own * ROWS + rank
        place = jnp.where(rows == rank + lane_offset, 1.0, 0.0).astype(BF16)
        coarse = jnp.where(hit, (ids >> 4).astype(F32), 0.0)
        fine = jnp.where(hit, (ids & 15).astype(F32), 0.0)
        both = jnp.concatenate([coarse, fine], axis=0).astype(BF16)
        acc_s[...] += lax.dot_general(
            both, place, (((1,), (1,)), ((), ())), preferred_element_type=F32
        )
        return base + counted[:, 128:]

    lax.fori_loop(0, tile.shape[0], chunk, jnp.zeros((128, 128), F32), unroll=4)
    ids_ref[...] = acc_s[:128] * 16.0 + acc_s[128:]


def route(tile, info):
    return call(
        route_kernel,
        "route",
        (jax.ShapeDtypeStruct((32, 128), jnp.int32), array(128, 128)),
        [VM, SM],
        [
            pltpu.VMEM((32, 128), jnp.int32),
            pltpu.VMEM((32, 128), jnp.int32),
            pltpu.VMEM((256, 128), F32),
        ],
    )(tile, info)


def pack_kernel(pos_ref, data_ref, ids_ref, out_ref):
    step = 16

    def body(b, carry):
        start = pl.multiple_of(b * step, step)
        block = data_ref[pl.ds(start, step), :]
        row = b // (128 // step)
        lane = (b % (128 // step)) * step
        for j in range(step):
            out_ref[pl.ds(pos_ref[row, lane + j], 1), :] = block[j : j + 1]
        return carry

    lax.fori_loop(0, 4096 // step, body, 0)

    def tail(b, carry):
        start = pl.multiple_of(b * 8, 8)
        block = ids_ref[pl.ds(start, 8), :]
        for j in range(8):
            out_ref[pl.ds((start + j) * ROWS + CAP, 1), :] = block[j : j + 1]
        return carry

    lax.fori_loop(0, DEVICES // 8, tail, 0)


def pack(pos, data, ids):
    return call(pack_kernel, "pack", array(DEVICES * ROWS, 128), [SM, VM, VM])(pos, data, ids)


def thin_pair(count):
    matrix = np.zeros((count // 2 + 1, count))
    for i in range(count // 2 + 1):
        for source, weight in ((2 * i - 1, 0.5), (2 * i, 1.0), (2 * i + 1, 0.5)):
            if 0 <= source < count:
                matrix[i, source] = weight
    return matrix


def thin_cycle(length):
    matrix = np.zeros((length, length // 2))
    for i in range(length // 2):
        matrix[2 * i, i] += 1.0
        matrix[(2 * i - 1) % length, i] += 0.5
        matrix[(2 * i + 1) % length, i] += 0.5
    return matrix


def grow_matrix(count, source):
    matrix = np.zeros((count, source))
    for i in range(count):
        if i % 2 == 0:
            matrix[i, i // 2] = 1.0
        else:
            matrix[i, i // 2] = 0.5
            matrix[i, i // 2 + 1] = 0.5
    return matrix


def padded(matrix, rows, columns):
    out = np.zeros((rows, columns))
    out[: matrix.shape[0], : matrix.shape[1]] = matrix
    return out


def twice(matrix):
    return np.kron(np.eye(2), matrix)


def plain(matrix):
    return np.asarray(matrix, np.float32).astype(BF16)


def top_rows_matrix():
    rows_x = padded(thin_pair(17), 9, 17)
    rows_y = padded(thin_pair(13), 8, 16)
    rows_y[7] = 0.0
    matrix = np.zeros((2 * TOP_ROWS, 17 * 16))
    for i in range(9):
        for j in range(8):
            line = (j // 2) * 8 + i if i < 8 else 32 + j // 2
            matrix[(j % 2) * TOP_ROWS + line] = np.kron(rows_x[i], rows_y[j])
    return matrix


def exact_left(matrix_ref, value):
    top, rest = halves(value)
    return mm(matrix_ref[...], top) + mm(matrix_ref[...], rest)


def exact_right(value, matrix_ref):
    top, rest = halves(value)
    return mm(top, matrix_ref[...]) + mm(rest, matrix_ref[...])


def collect_kernel(
    in_ref, thin_z_ref, thin_y_ref, top_rows_ref, top_z_ref, *refs
):
    fine_ref, mid_ref, low_ref, high_ref, top_ref, data_s, ids_s, slab_s = refs[-8:]
    for c in range(DEVICES // 4):
        total = None
        for j in range(4):
            base = (c * 4 + j) * ROWS
            top, rest = halves(in_ref[base : base + CAP, :])
            start = (c * 4 + j) * CAP
            data_s[start : start + CAP, :128] = top
            data_s[start : start + CAP, 128:] = rest
            line = in_ref[base + CAP : base + CAP + 1, :]
            total = line if total is None else total + line
        ids_s[c : c + 1, :] = total.astype(jnp.int32)
    rows = lax.broadcasted_iota(jnp.int32, (256, 128), 0)

    def block(b, carry):
        first = pl.multiple_of(b * 256, 256)
        acc = jnp.zeros((256, 256), F32)
        for k in range(16):
            parts = []
            for q in range(2):
                ids = ids_s[2 * k + q : 2 * k + q + 1, :] - first
                parts.append(jnp.where(rows == ids, 1.0, 0.0).astype(BF16))
            acc = acc + mm(jnp.concatenate(parts, axis=1), data_s[k * 256 : (k + 1) * 256, :])
        fine_ref[pl.ds(first, 256), :] = acc[:, :128] + acc[:, 128:]
        return carry

    lax.fori_loop(0, 6, block, 0)
    for i in range(17):
        total = None
        for x, weight in ((2 * i, 1.0), (2 * i - 1, 0.5), (2 * i + 1, 0.5)):
            if 0 <= x < CX:
                term = jnp.concatenate(
                    [
                        fine_ref[h * CX * CY + x * CY : h * CX * CY + (x + 1) * CY, :]
                        for h in range(2)
                    ],
                    axis=1,
                )
                term = term if weight == 1.0 else weight * term
                total = term if total is None else total + term
        slab_s[i * CY : (i + 1) * CY, :] = total
    slab_s[17 * CY :, :] = jnp.zeros((7 * CY, NZ), F32)
    for g in range(3):
        part = exact_right(slab_s[g * 192 : (g + 1) * 192, :], thin_z_ref)
        mid_ref[g * 128 : (g + 1) * 128, :] = exact_left(thin_y_ref, part)
    stacked = exact_left(top_rows_ref, mid_ref[: 17 * 16, :])
    pair = jnp.concatenate([stacked[:TOP_ROWS], stacked[TOP_ROWS:]], axis=1)
    top_charge = exact_right(pair, top_z_ref)
    for s in range(SIZE_X):
        top_ref[s * TOP_ROWS : (s + 1) * TOP_ROWS, :] = top_charge
    for h in range(2):
        for c in range(4):
            at = slice((h * 4 + c) * CX, (h * 4 + c + 1) * CX)
            low_ref[at, :] = fine_ref[pl.ds(h * CX * CY + c, CX, stride=CY), :]
            high_ref[at, :] = fine_ref[pl.ds(h * CX * CY + CY - 4 + c, CX, stride=CY), :]
    for j in range(5):
        at = slice(256 + j * 24, 256 + (j + 1) * 24)
        low_ref[at, :] = mid_ref[pl.ds(j, 24, stride=16), :]
        high_ref[at, :] = mid_ref[pl.ds(8 + j, 24, stride=16), :]


def collect(arrived, *after):
    tables = (
        plain(thin_cycle(NZ)),
        plain(np.kron(np.eye(8), padded(thin_pair(CY), 16, CY))),
        plain(top_rows_matrix()),
        plain(twice(thin_cycle(128))),
    )
    return call(
        collect_kernel,
        "collect",
        (
            array(2 * CX * CY, 128),
            array(24 * 16, 128),
            array(SEND, 128),
            array(SEND, 128),
            array(SIZE_X * TOP_ROWS, 128),
        ),
        [VM] * 5 + [ANY] * len(after),
        [
            pltpu.VMEM((DEVICES * CAP, 256), BF16),
            pltpu.VMEM((DEVICES // 4, 128), jnp.int32),
            pltpu.VMEM((24 * CY, NZ), F32),
        ],
    )(arrived, *tables, *after)


def merge_kernel(fine_ref, mid_ref, before_ref, behind_ref, near_ref, wide_ref, low_ref, high_ref):
    for n in range(2 * CX):
        near_ref[n * YD : n * YD + CY, :] = fine_ref[n * CY : (n + 1) * CY, :]
    for h in range(2):
        for c in range(4):
            at = slice((h * 4 + c) * CX, (h * 4 + c + 1) * CX)
            start = h * CX * YD + CY + c
            near_ref[pl.ds(start, CX, stride=YD), :] = behind_ref[at, :]
            near_ref[pl.ds(start + 4, CX, stride=YD), :] = before_ref[at, :]
    for i in range(24):
        wide_ref[i * YD : i * YD + 16, :] = mid_ref[i * 16 : (i + 1) * 16, :]
        wide_ref[i * YD + 16 : (i + 1) * YD, :] = jnp.zeros((16, 128), F32)
    for j in range(5):
        at = slice(256 + j * 24, 256 + (j + 1) * 24)
        behind = behind_ref[at, :]
        if j == 0:
            behind = behind + wide_ref[pl.ds(12, 24, stride=YD), :]
        wide_ref[pl.ds(12 + j, 24, stride=YD), :] = behind
        before = before_ref[at, :]
        row = 28 + j if j < 4 else 0
        if j == 4:
            before = before + wide_ref[pl.ds(0, 24, stride=YD), :]
        wide_ref[pl.ds(row, 24, stride=YD), :] = before
    for ref, first, mid_first in ((low_ref, 0, 0), (high_ref, CX - 4, 12)):
        for h in range(2):
            base = (h * CX + first) * YD
            ref[h * 128 : (h + 1) * 128, :] = near_ref[base : base + 128, :]
        for i in range(5):
            base = (mid_first + i) * YD
            at = 256 + i * 24
            ref[at : at + 16, :] = wide_ref[base : base + 16, :]
            ref[at + 16 : at + 24, :] = (
                wide_ref[base + 16 : base + 24, :] + wide_ref[base + 24 : base + 32, :]
            )


def merge(fine, mid, before, behind):
    return call(
        merge_kernel,
        "merge",
        (array(2 * CX * YD, 128), array(24 * YD, 128), array(SEND, 128), array(SEND, 128)),
        [VM] * 4,
    )(fine, mid, before, behind)


def z_matrices(period, copies):
    half = period // 2
    z = np.arange(period)[:, None]
    f = np.arange(half)[None, :]
    angle = 2 * np.pi * ((z * f) % period) / period
    cosine, sine = np.cos(angle), -np.sin(angle)
    sine[:, 0] = (-1.0) ** np.arange(period)
    scale = np.full((half, 1), 2.0 / period)
    scale[0] = 1.0 / period
    forward = np.zeros((256, 256))
    inverse = np.zeros((256, 256))
    for c in range(copies):
        rows = slice(c * period, (c + 1) * period)
        real = slice(c * half, (c + 1) * half)
        imag = slice(128 + c * half, 128 + (c + 1) * half)
        forward[rows, real] = cosine
        forward[rows, imag] = sine
        inverse[real, rows] = scale * cosine.T
        inverse[imag, rows] = scale * sine.T
    return forward, inverse


def y_matrices():
    order = np.concatenate([np.arange(17), np.arange(31, 16, -1)])
    y = np.arange(YD)
    angle = 2 * np.pi * ((order[:, None] * y[None, :]) % YD) / YD
    cosine, sine = np.cos(angle), np.sin(angle)
    forward = np.block([[cosine, sine], [-sine, cosine]])
    inverse = np.block([[cosine.T, -sine.T], [sine.T, cosine.T]]) / YD
    return np.kron(np.eye(4), forward), np.kron(np.eye(4), inverse)


def stacked_rows(matrix):
    top, rest = np_halves(matrix)
    return np.concatenate([top, rest], axis=0)


def stacked_cols(matrix):
    top, rest = np_halves(matrix)
    return np.concatenate([top, rest], axis=1)


def right_product(value, matrix_ref):
    top, rest = halves(value)
    return (
        mm(top, matrix_ref[:256, :]) + mm(top, matrix_ref[256:, :]) + mm(rest, matrix_ref[:256, :])
    )


def left_product(matrix_ref, value):
    top, rest = halves(value)
    return (
        mm(matrix_ref[:, :256], top) + mm(matrix_ref[:, 256:], top) + mm(matrix_ref[:, :256], rest)
    )


def special_mask(copies, rows):
    lane = lax.broadcasted_iota(jnp.int32, (rows, 128), 1)
    row = lax.broadcasted_iota(jnp.int32, (rows, 128), 0)
    return (lane & (128 // copies - 1)) == 0, row


def forward_chunk(value, z_ref, y_ref, copies):
    z_freq = right_product(value, z_ref)
    stacks = []
    for h in range(2):
        pieces = []
        for q in range(4):
            slab = z_freq[(h * 4 + q) * YD : (h * 4 + q + 1) * YD]
            pieces += [slab[:, :128], slab[:, 128:]]
        stacks.append(jnp.concatenate(pieces, axis=0))
    freq = left_product(y_ref, jnp.concatenate(stacks, axis=1))
    lane_special, row = special_mask(copies, 16)
    special = lane_special & (row != 0)
    slabs = []
    for h in range(2):
        for q in range(4):
            slab = freq[q * 64 : (q + 1) * 64, h * 128 : (h + 1) * 128]
            ar, br, ai, bi = slab[:16], slab[16:32], slab[32:48], slab[48:]
            slabs.append(
                jnp.concatenate(
                    [
                        jnp.where(special, 0.5 * (ar + br), ar),
                        jnp.where(special, 0.5 * (ai + bi), br),
                        jnp.where(special, 0.5 * (ai - bi), ai),
                        jnp.where(special, 0.5 * (br - ar), bi),
                    ],
                    axis=0,
                )
            )
    return slabs


def inverse_chunk(slabs, z_ref, y_ref):
    stacks = [jnp.concatenate(slabs[h * 4 : h * 4 + 4], axis=0) for h in range(2)]
    space = left_product(y_ref, jnp.concatenate(stacks, axis=1))
    rows = []
    for h in range(2):
        for q in range(4):
            slab = space[q * 64 : (q + 1) * 64, h * 128 : (h + 1) * 128]
            rows.append(jnp.concatenate([slab[:YD], slab[YD:]], axis=1))
    return right_product(jnp.concatenate(rows, axis=0), z_ref)


def taps_kernel(copies, in_ref, z_ref, y_ref, after_ref, real_ref, twin_ref, imag_ref):
    lane_special, row = special_mask(copies, YD)
    special = lane_special & ((row == 0) | (row == 16))
    for p in range(2):
        slabs = forward_chunk(in_ref[p * 256 : (p + 1) * 256, :], z_ref, y_ref, copies)
        for j in range(8):
            dx = p * 8 + j
            if dx > 8:
                break
            real, imag = slabs[j][:YD], slabs[j][YD:]
            at = slice(dx * YD, (dx + 1) * YD)
            real_ref[at, :] = real
            twin_ref[at, :] = jnp.where(special, imag, real)
            imag_ref[at, :] = jnp.where(special, 0.0, imag)


def taps(kernel, copies, z_matrix, y_matrix, after):
    flipped = kernel[:, ::-1, ::-1]
    tall = jnp.concatenate(
        [flipped[:, 4:], jnp.zeros((9, YD - 9, 9), F32), flipped[:, :4]], axis=1
    )
    period = 256 // copies
    wide = jnp.concatenate(
        [tall[:, :, 4:], jnp.zeros((9, YD, period - 9), F32), tall[:, :, :4]], axis=2
    )
    wide = jnp.concatenate([wide] * copies, axis=2)
    wide = jnp.concatenate([wide, jnp.zeros((7, YD, 256), F32)], axis=0)
    return call(
        functools.partial(taps_kernel, copies),
        f"taps{copies}",
        (array(9 * YD, 128),) * 3,
        [VM] * 3 + [ANY],
    )(wide.reshape(16 * YD, 256), z_matrix, y_matrix, after)


def own_kernel(in_ref, z_ref, y_ref, out_ref):
    for p in range(CX // 8):
        value = jnp.concatenate(
            [in_ref[h * CX * YD + p * 256 : h * CX * YD + (p + 1) * 256, :] for h in range(2)], axis=1
        )
        slabs = forward_chunk(value, z_ref, y_ref, 1)
        for j in range(8):
            out_ref[(p * 8 + j) * 64 : (p * 8 + j + 1) * 64, :] = slabs[j]


def convolve(copies, block_out, blocks, spectrum, freq_s, conv_s):
    real_ref, twin_ref, imag_ref = spectrum
    lane_special, row = special_mask(copies, 8)

    def step(index, carry):
        v = index % 2
        first = (index // 2) * block_out
        sums = [[None] * 4 for _ in range(block_out)]
        for dx in range(9):
            coefs = []
            for half in range(2):
                at = pl.ds(pl.multiple_of(dx * YD + half * 16 + v * 8, 8), 8)
                coefs.append((real_ref[at, :], twin_ref[at, :], imag_ref[at, :]))
            for j in range(block_out):
                base = (first + j + dx) * 64 + v * 8
                for half in range(2):
                    at = pl.multiple_of(base + half * 16, 8)
                    re = freq_s[pl.ds(at, 8), :]
                    im = freq_s[pl.ds(pl.multiple_of(at + 32, 8), 8), :]
                    a, t, b = coefs[half]
                    new_re = a * re - b * im
                    new_im = b * re + t * im
                    old = sums[j]
                    old[2 * half] = new_re if dx == 0 else old[2 * half] + new_re
                    old[2 * half + 1] = new_im if dx == 0 else old[2 * half + 1] + new_im
        special = lane_special & ((row != 0) | (v != 0))
        for j in range(block_out):
            ar, ai, br, bi = sums[j]
            base = (first + j) * 64 + v * 8
            values = (
                jnp.where(special, ar - bi, ar),
                jnp.where(special, ar + bi, br),
                jnp.where(special, ai + br, ai),
                jnp.where(special, br - ai, bi),
            )
            for part in range(4):
                conv_s[pl.ds(pl.multiple_of(base + part * 16, 8), 8), :] = values[part]
        return carry

    lax.fori_loop(0, 2 * blocks, step, 0)


def wide_slab(ref, index):
    at = 256 + index * 24
    last = ref[at + 16 : at + 24, :]
    row = lax.broadcasted_iota(jnp.int32, (8, 128), 0)
    return jnp.concatenate(
        [ref[at : at + 16, :], jnp.where(row < 4, last, 0.0), jnp.where(row < 4, 0.0, last)], axis=0
    )


def levels_kernel(
    own_ref, before_ref, behind_ref, wide_ref,
    nr_ref, nt_ref, ni_ref, mr_ref, mt_ref, mi_ref,
    zf_ref, yf_ref, zi_ref, yi_ref, mzf_ref, mzi_ref,
    near_ref, mid_ref, freq_s, conv_s, mid_freq_s, mid_conv_s,
):
    freq_s[4 * 64 : 36 * 64, :] = own_ref[...]
    edges = [
        jnp.concatenate([ref[:128, :], ref[128:256, :]], axis=1) for ref in (before_ref, behind_ref)
    ]
    slabs = forward_chunk(jnp.concatenate(edges, axis=0), zf_ref, yf_ref, 1)
    for j in range(8):
        at = j if j < 4 else 32 + j
        freq_s[at * 64 : (at + 1) * 64, :] = slabs[j]
    zero = jnp.zeros((YD, 128), F32)
    for p in range(3):
        pairs = []
        for j in range(8):
            pair = []
            for n in (p * 8 + j, p * 8 + j + 9):
                if n > 24 or (n == p * 8 + j and n > 16):
                    slab = zero
                elif n < 4:
                    slab = wide_slab(before_ref, n)
                elif n > 20:
                    slab = wide_slab(behind_ref, n - 20)
                else:
                    slab = wide_ref[(n - 4) * YD : (n - 3) * YD, :]
                    if n == 4:
                        slab = slab + wide_slab(before_ref, 4)
                    if n == 20:
                        slab = slab + wide_slab(behind_ref, 0)
                pair.append(slab)
            pairs.append(jnp.concatenate(pair, axis=1))
        slabs = forward_chunk(jnp.concatenate(pairs, axis=0), mzf_ref, yf_ref, 2)
        for j in range(8):
            at = p * 8 + j
            mid_freq_s[at * 64 : (at + 1) * 64, :] = slabs[j]
    convolve(1, 8, 4, (nr_ref, nt_ref, ni_ref), freq_s, conv_s)
    for p in range(4):
        slabs = [conv_s[(p * 8 + j) * 64 : (p * 8 + j + 1) * 64, :] for j in range(8)]
        space = inverse_chunk(slabs, zi_ref, yi_ref)
        for j in range(8):
            x = p * 8 + j
            near_ref[x * CY : (x + 1) * CY, :] = space[j * YD : j * YD + CY]
    convolve(2, 9, 1, (mr_ref, mt_ref, mi_ref), mid_freq_s, mid_conv_s)
    mid_conv_s[9 * 64 :, :] = jnp.zeros((7 * 64, 128), F32)
    for p in range(2):
        slabs = [mid_conv_s[(p * 8 + j) * 64 : (p * 8 + j + 1) * 64, :] for j in range(8)]
        space = inverse_chunk(slabs, mzi_ref, yi_ref)
        for j in range(8):
            i = p * 8 + j
            if i < 9:
                mid_ref[i * 16 : (i + 1) * 16, :] = space[j * YD : j * YD + 16]


def gauss(index, period, width):
    distance = jnp.minimum(index, period - index).astype(F32)
    return jnp.exp(-(distance * distance) / (width * width))


def top_kernel(in_ref, weights_ref, widths_ref, info_ref, out_ref, plane_s, depth_s):
    first_x = info_ref[2] * 8
    first_y = info_ref[3] * 6
    row = lax.broadcasted_iota(jnp.int32, (16, 256), 0)
    column = lax.broadcasted_iota(jnp.int32, (16, 256), 1)
    source = jnp.where(column < 128, column, (column - 128) * 8 + 8)
    offset = (first_x + row - source) & 127
    parts = [
        jnp.where(column < 144, gauss(offset, 128, widths_ref[k]), 0.0) for k in range(4)
    ]
    left = halves(jnp.concatenate(parts, axis=0))
    for jp in range(4):
        tiles = [in_ref[s * TOP_ROWS + jp * 8 : s * TOP_ROWS + jp * 8 + 8, :] for s in range(16)]
        tiles.append(in_ref[pl.ds(32 + jp, SIZE_X, stride=TOP_ROWS), :])
        tiles.append(jnp.zeros((112, 128), F32))
        right = halves(jnp.concatenate(tiles, axis=0))
        plane = mm(left[0], right[0]) + mm(left[0], right[1]) + mm(left[1], right[0])
        for k in range(4):
            plane_s[(k * 4 + jp) * 16 : (k * 4 + jp + 1) * 16, :] = plane[k * 16 : (k + 1) * 16]
    row = lax.broadcasted_iota(jnp.int32, (128, 128), 0)
    column = lax.broadcasted_iota(jnp.int32, (128, 128), 1)
    for k in range(4):
        weight = gauss((row - column) & 63, 64, widths_ref[k]) * weights_ref[k]
        weight = halves(jnp.where((row >> 6) == (column >> 6), weight, 0.0))
        value = halves(plane_s[k * 64 : (k + 1) * 64, :])
        depth_s[k * 64 : (k + 1) * 64, :] = (
            mm(value[0], weight[0]) + mm(value[0], weight[1]) + mm(value[1], weight[0])
        )
    lane = lax.broadcasted_iota(jnp.int32, (16, 128), 1)
    tiles = []
    for ip in range(5):
        first = depth_s[pl.ds(2 * ip, 16, stride=16), :]
        second = depth_s[pl.ds(2 * ip + 1, 16, stride=16), :]
        even = jnp.where(lane < 64, first, pltpu.roll(second, 64, 1))
        odd = jnp.where(lane < 64, pltpu.roll(first, 64, 1), second)
        tiles.append(jnp.concatenate([even, odd, jnp.zeros((96, 128), F32)], axis=0))
    right = halves(jnp.concatenate(tiles, axis=1))
    row = lax.broadcasted_iota(jnp.int32, (64, 128), 0)
    column = lax.broadcasted_iota(jnp.int32, (64, 128), 1)
    target = (row >> 3) * 6 + (row & 7)
    source = first_y + (column & 3) * 2 + ((column >> 4) & 1)
    offset = target - source
    offset = jnp.where(offset < 0, offset + 48, offset)
    offset = jnp.where(offset >= 48, offset - 48, offset)
    chosen = (column >> 2) & 3
    left = jnp.zeros((64, 128), F32)
    for k in range(4):
        left = jnp.where(chosen == k, gauss(offset, 48, widths_ref[k]), left)
    left = halves(jnp.where(column < 32, left, 0.0))
    out_ref[...] = mm(left[0], right[0]) + mm(left[0], right[1]) + mm(left[1], right[0])


def finish_kernel(near_ref, mid_ref, top_ref, grow_top_ref, grow_y_ref, grow_z_ref, grow_fine_ref, out_ref, grown_s):
    total = top_ref[:8, :]
    for s in range(1, SIZE_Y):
        total = total + top_ref[s * 8 : (s + 1) * 8, :]
    lanes = []
    for ip in range(5):
        lanes.append(exact_right(total[:, ip * 128 : (ip + 1) * 128], grow_top_ref))
    deep = jnp.concatenate(lanes, axis=1)
    tiles = []
    for i in range(17):
        tile = deep[:, (i // 2) * 128 : (i // 2 + 1) * 128]
        if i % 2:
            tile = 0.5 * (tile + deep[:, (i // 2 + 1) * 128 : (i // 2 + 2) * 128])
        tiles.append(tile)
    flat = jnp.concatenate(tiles, axis=1)
    flat = jnp.concatenate([flat, jnp.zeros((120, 17 * 128), F32)], axis=0)
    tall = exact_left(grow_y_ref, flat)
    slabs = []
    for i in range(24):
        if i > 16:
            slabs.append(jnp.zeros((16, 128), F32))
            continue
        h = i // 9
        slabs.append(
            tall[:, i * 128 : (i + 1) * 128]
            + mid_ref[(i - 9 * h) * 16 : (i - 9 * h + 1) * 16, h * 128 : (h + 1) * 128]
        )
    for g in range(3):
        part = exact_right(jnp.concatenate(slabs[g * 8 : (g + 1) * 8], axis=0), grow_z_ref)
        grown_s[g * 192 : (g + 1) * 192, :] = exact_left(grow_fine_ref, part)
    for x in range(CX):
        at = slice(x * CY, (x + 1) * CY)
        i = x // 2
        value = grown_s[i * CY : (i + 1) * CY, :]
        if x % 2:
            value = 0.5 * (value + grown_s[(i + 1) * CY : (i + 2) * CY, :])
        out_ref[at, :] = near_ref[at, :] + value


def swap(to_low, to_high, axis):
    count = lax.axis_size(axis)
    forward = [(i, (i + 1) % count) for i in range(count)]
    backward = [(target, source) for source, target in forward]
    return lax.ppermute(to_high, axis, forward), lax.ppermute(to_low, axis, backward)


def on_device(
    charge_blocks, block_tile, block_count, near_kernel, mid_kernel, top_weights, top_widths
):
    at_x = lax.axis_index("gx")
    at_y = lax.axis_index("gy")
    info = jnp.stack(
        [block_count[0], ((at_x * SIZE_Y + at_y) % 4) * CAP, at_x, at_y]
    ).astype(jnp.int32)
    pos, ids = route(block_tile.reshape(32, 128), info)
    outgoing = pack(pos, charge_blocks, ids)
    arrived = lax.all_to_all(
        outgoing.reshape(DEVICES, ROWS, 1, 128),
        ("gx", "gy"),
        split_axis=0,
        concat_axis=0,
        tiled=True,
    ).reshape(DEVICES * ROWS, 128)

    z_fine, z_fine_back = z_matrices(256, 1)
    z_mid, z_mid_back = z_matrices(128, 2)
    y_forward, y_back = y_matrices()
    zf, yf = stacked_rows(z_fine), stacked_cols(y_forward)
    zi, yi = stacked_rows(z_fine_back), stacked_cols(y_back)
    mzf, mzi = stacked_rows(z_mid), stacked_rows(z_mid_back)
    near_taps = taps(near_kernel, 1, zf, yf, outgoing)
    mid_taps = taps(mid_kernel, 2, mzf, yf, outgoing)

    fine, mid, low, high, top = collect(arrived, *near_taps, *mid_taps)
    before, behind = swap(low, high, "gy")
    tops = lax.all_to_all(
        top.reshape(SIZE_X, TOP_ROWS, 128), "gx", split_axis=0, concat_axis=0, tiled=True
    ).reshape(SIZE_X * TOP_ROWS, 128)
    partial = call(
        top_kernel,
        "top",
        array(64, 640),
        [VM, SM, SM, SM],
        [pltpu.VMEM((256, 128), F32), pltpu.VMEM((256, 128), F32)],
    )(tops, top_weights, top_widths, info)
    partial = lax.all_to_all(
        partial.reshape(SIZE_Y, 8, 640), "gy", split_axis=0, concat_axis=0, tiled=True
    ).reshape(64, 640)
    near_rows, wide, low, high = merge(fine, mid, before, behind)
    before, behind = swap(low, high, "gx")
    own = call(own_kernel, "own", array(CX * 64, 128), [VM] * 3)(near_rows, zf, yf)
    near, mid_near = call(
        levels_kernel,
        "levels",
        (array(CX * CY, NZ), array(9 * 16, 256)),
        [VM] * 16,
        [
            pltpu.VMEM((40 * 64, 128), F32),
            pltpu.VMEM((32 * 64, 128), F32),
            pltpu.VMEM((24 * 64, 128), F32),
            pltpu.VMEM((16 * 64, 128), F32),
        ],
    )(own, before, behind, wide, *near_taps, *mid_taps, zf, yf, zi, yi, mzf, mzi)
    grow_z = grow_matrix(2 * 64, 65)
    grow_z[:, 0] += grow_z[:, 64]
    grow_fine_z = grow_matrix(2 * 128, 129)
    grow_fine_z[:, 0] += grow_fine_z[:, 128]
    out = call(
        finish_kernel, "finish", array(CX * CY, NZ), [VM] * 7, [pltpu.VMEM((24 * CY, NZ), F32)]
    )(
        near,
        mid_near,
        partial,
        plain(twice(grow_z[:, :64].T)),
        plain(padded(grow_matrix(13, 7), 16, 128)),
        plain(grow_fine_z[:, :128].T),
        plain(np.kron(np.eye(8), padded(grow_matrix(CY, 13), CY, 16))),
    )
    return out.reshape(CX, CY, NZ)


def solution(mesh):
    placed = (P(("gx", "gy"), None), P(("gx", "gy")), P(("gx", "gy")), P(), P(), P(), P())
    return jax.shard_map(
        on_device, mesh=mesh, in_specs=placed, out_specs=P("gx", "gy", None), check_vma=False
    )
```

time: 165 us -> 115 us (0.70)
  waiting for transfers between devices: 49 us -> 28.4 us
  matrix products: 9.14 us -> 0 us
  local copies, waits for them, and re-layouts: 27 us -> 18.7 us
  other arithmetic: 9.38 us -> 1.19 us
  Pallas kernels: 43.1 us -> 37.8 us
    slice x22 -> x10, local copies, waits for them, and re-layouts: 18.3 us -> 0.43 us  [the longest x4 0.23 us: taps(): flipped[:, :4]]
    unnamed x46 -> x70, local copies, waits for them, and re-layouts: 5.49 us -> 15.3 us
    dot_general x13 -> x0, matrix products: 9.14 us -> none  [the longest x2 3.72 us: thin(): jnp.einsum('xyz,zc->xyc', values, thin_cycle(values.shape[2]), precision=...]
    ppermute x4, waiting for transfers between devices: 12.8 us -> 5.38 us  [the longest x2 2.7 us: swap(): lax.ppermute(to_high, axis, forward)]
    all_to_all x1, waiting for transfers between devices: 30.1 us -> 23 us  [on_device(): lax.all_to_all(outgoing.reshape(DEVICES, ROWS, 1, 128), ('gx', 'gy'), spl...]
    all_to_all x2, waiting for transfers between devices: 6.13 us -> 0.01 us  [the longest x1 0.01 us: on_device(): lax.all_to_all(top.reshape(SIZE_X, TOP_ROWS, 128), 'gx', split_axis=0, co...]
    pallas_call x7 -> x10, Pallas kernels: 43.1 us -> 37.8 us  [the longest x1 13.5 us: pack(): call(pack_kernel, 'pack', array(DEVICES * ROWS, 128), [SM, VM, VM])]
    concatenate x4 -> x1, other arithmetic: 3.63 us -> 0.09 us  [taps(): jnp.concatenate([flipped[:, 4:], jnp.zeros((9, YD - 9, 9), F32), flipped[...]
  transfers between devices with their start and end apart: 7 -> 7, of which waited for: 4 -> 3; matrix products, arithmetic and copies ran while one was open for 5% -> 4% of each run, Pallas kernels for 10% -> 11%
where the time goes in v2:
time: 115 us; the launch traced here: 114 us
  Pallas kernels  37.8 us (33%)
  waiting for transfers between devices  28.4 us (25%)
  starting transfers between devices  26.7 us (23%)
  local copies, waits for them, and re-layouts  18.7 us (16%)
  other arithmetic  1.19 us (1%)
    all_to_all x1, waiting for transfers between devices, on_device(): lax.all_to_all(outgoing.reshape(DEVICES, ROWS, 1, 128), ('gx', 'gy'), spl...  23 us
    unnamed x70, local copies, waits for them, and re-layouts  15.3 us
    pallas_call x1, Pallas kernels, pack(): call(pack_kernel, 'pack', array(DEVICES * ROWS, 128), [SM, VM, VM])  13.5 us
    all_to_all x1, starting transfers between devices, on_device(): lax.all_to_all(outgoing.reshape(DEVICES, ROWS, 1, 128), ('gx', 'gy'), spl...  11.5 us
    pallas_call x1, Pallas kernels, on_device(): call(levels_kernel, 'levels', (array(CX * CY, NZ), array(9 * 16, 256)), [...  6.41 us
    pallas_call x1, Pallas kernels, collect(): call(collect_kernel, 'collect', (array(2 * CX * CY, 128), array(24 * 16,...  5.64 us
    all_to_all x1, starting transfers between devices, on_device(): lax.all_to_all(partial.reshape(SIZE_Y, 8, 640), 'gy', split_axis=0, conca...  5.3 us
    pallas_call x1, Pallas kernels, route(): call(route_kernel, 'route', (jax.ShapeDtypeStruct((32, 128), jnp.int32),...  4.2 us
  transfers between devices with their start and end apart: 7, of which 3 were waited for; matrix products, arithmetic and copies ran while one was open for 4% of the time, Pallas kernels for 11%

profile of v2, /device:TPU:1, one launch (start us, length us, event | category | flops | bytes accessed | tf_op | source)
XLA Modules:
  0.0 113.9 jit_solution(7400917578034046796)
XLA Ops:
  1.5 4.2 %route.1 = (s32[32,128]{1,0:T(8,128)S(1)}, f32[128,128]{1,0:T(8,128)S(1)}) custom-call(s32[32,128]{1,0:T(8,128)S(1)} %bitcast.21, s32[4]{0:T(128)S(1)} %pad_add_fusion.info_ref), custom_call_target="tpu_custom_call" | custom-call | tf_op jit(solution)/shard_map/route/pallas_call | solution.py:108
  5.7 1.6 %copy-done.2 = f32[4096,128]{1,0:T(8,128)S(1)} copy-done((f32[4096,128]{1,0:T(8,128)S(1)}, f32[4096,128]{1,0:T(8,128)}, u32[]{:S(2)}) %copy-start.2) | copy-done | bytes 2097176
  7.3 13.5 %pack.1.after_ref = f32[4224,128]{1,0:T(8,128)} custom-call(s32[32,128]{1,0:T(8,128)S(1)} %get-tuple-element.24.pos_ref, f32[4096,128]{1,0:T(8,128)S(1)} %copy-done.2, f32[128,128]{1,0:T(8,128)S(1)} %get-tuple-element.25.ids_ref), custom_call_target="tpu_custom_call" | custom-call | tf_op jit(solution)/shard_map/pack/pallas_call | solution.py:146
  20.7 11.5 %all-to-all-start = ((f32[128,33,1,128]{3,2,1,0:T(1,128)}), f32[128,33,1,128]{3,2,1,0:T(1,128)S(1)}, u32[]{:S(2)}, u32[]{:S(2)}) async-start(f32[128,33,1,128]{3,2,1,0:T(1,128)} %bitcast.4), calls=%async_computation | async-start | bytes 4325376 | tf_op jit(solution)/shard_map/all_to_all | solution.py:718
  34.6 1.2 %concatenate.25 = f32[9,32,256]{2,1,0:T(8,128)S(1)} concatenate(f32[9,32,5]{2,1,0:T(8,128)} %slice.51, f32[9,32,119]{2,1,0:T(8,128)S(1)} %broadcast_in_dim.7, f32[9,32,9]{2,1,0:T(8,128)S(1)} %get-tuple-element.43, f32[9,32,119]{2,1,0:T(8,128)S(1)} %broadcast_in_dim.7, f32[9,32,4]{2,1,0:T(8,128)S(1)} %bitcast.22), dimensions={2} | concatenate | bytes 589824 | tf_op jit(solution)/shard_map/concatenate | solution.py:478
  35.8 1.0 pad_maximum_fusion
  40.0 23.0 %all-to-all-done = f32[128,33,1,128]{3,2,1,0:T(1,128)S(1)} async-done(((f32[128,33,1,128]{3,2,1,0:T(1,128)}), f32[128,33,1,128]{3,2,1,0:T(1,128)S(1)}, u32[]{:S(2)}, u32[]{:S(2)}) %all-to-all-start) | async-done | bytes 2162720 | tf_op jit(solution)/shard_map/all_to_all | solution.py:718
  63.0 0.9 copy-done.7
  63.9 0.9 copy-done.10
  68.2 5.6 %collect.1 = (f32[1536,128]{1,0:T(8,128)S(1)}, f32[384,128]{1,0:T(8,128)S(1)}, f32[376,128]{1,0:T(8,128)S(1)}, f32[376,128]{1,0:T(8,128)S(1)}, f32[640,128]{1,0:T(8,128)S(1)}) custom-call(f32[4224,128]{1,0:T(8,128)S(1)} %bitcast.15, bf16[256,128]{1,0:T(8,128)(2,1)S(1)} %copy-done.24, bf16[128,192]{1,0:T(8,128)(2,1)S(1)} %copy-done.23, ...), custom_call_target="tpu_custom_call" | custom-call | tf_op jit(solution)/shard_map/collect/pallas_call | solution.py:285
  77.5 3.6 %all-to-all-start.1 = ((f32[16,40,128]{2,1,0:T(8,128)}), f32[16,40,128]{2,1,0:T(8,128)S(1)}, u32[]{:S(2)}, u32[]{:S(2)}) async-start(f32[16,40,128]{2,1,0:T(8,128)} %bitcast.20), calls=%async_computation.1 | async-start | bytes 655360 | tf_op jit(solution)/shard_map/all_to_all | solution.py:737
  81.0 1.2 %collective-permute-start = (f32[376,128]{1,0:T(8,128)}, f32[376,128]{1,0:T(8,128)S(1)}, u32[]{:S(2)}, u32[]{:S(2)}) collective-permute-start(f32[376,128]{1,0:T(8,128)} %copy-done.32), channel_id=1, source_target_pairs={{0,1},{1,2},{2,3},{3,4},{4,5},{5,6},{6,7},{7,0},{8,9},{9,10},{10,1... | collective-permute-start | bytes 577544 | tf_op jit(solution)/shard_map/ppermute | solution.py:705
  82.4 2.7 %collective-permute-done.before_ref = f32[376,128]{1,0:T(8,128)S(1)} collective-permute-done((f32[376,128]{1,0:T(8,128)}, f32[376,128]{1,0:T(8,128)S(1)}, u32[]{:S(2)}, u32[]{:S(2)}) %collective-permute-start) | collective-permute-done | bytes 192544 | tf_op jit(solution)/shard_map/ppermute | solution.py:705
  85.1 2.7 %collective-permute-done.1.behind_ref = f32[376,128]{1,0:T(8,128)S(1)} collective-permute-done((f32[376,128]{1,0:T(8,128)}, f32[376,128]{1,0:T(8,128)S(1)}, u32[]{:S(2)}, u32[]{:S(2)}) %collective-permute-start.1) | collective-permute-done | bytes 192544 | tf_op jit(solution)/shard_map/ppermute | solution.py:705
  87.8 1.1 copy-done.5
  88.9 0.9 copy-done.19
  89.9 1.2 %merge.1 = (f32[2048,128]{1,0:T(8,128)S(1)}, f32[768,128]{1,0:T(8,128)S(1)}, f32[376,128]{1,0:T(8,128)}, f32[376,128]{1,0:T(8,128)}) custom-call(f32[1536,128]{1,0:T(8,128)S(1)} %copy-done.5, f32[384,128]{1,0:T(8,128)S(1)} %copy-done.19, f32[376,128]{1,0:T(8,128)S(1)} %collective-permute-done.before_ref, f32[376,128]{1,0:T(8,128)S(1)} %collective-permute-done.1.behind_ref), custom_call_target="tpu_custom_call" | custom-call | tf_op jit(solution)/shard_map/merge/pallas_call | solution.py:341
  91.8 1.5 %collective-permute-start.2 = (f32[376,128]{1,0:T(8,128)}, f32[376,128]{1,0:T(8,128)S(1)}, u32[]{:S(2)}, u32[]{:S(2)}) collective-permute-start(f32[376,128]{1,0:T(8,128)} %get-tuple-element.37), channel_id=1, source_target_pairs={{0,8},{8,16},{16,24},{24,32},{32,40},{40,48},{48,56},{56,64},{64,7... | collective-permute-start | bytes 577544 | tf_op jit(solution)/shard_map/ppermute | solution.py:705
  93.4 3.4 %collective-permute-start.3 = (f32[376,128]{1,0:T(8,128)}, f32[376,128]{1,0:T(8,128)}, u32[]{:S(2)}, u32[]{:S(2)}) collective-permute-start(f32[376,128]{1,0:T(8,128)} %get-tuple-element.38), channel_id=1, source_target_pairs={{8,0},{16,8},{24,16},{32,24},{40,32},{48,40},{56,48},{64,56},{72,6... | collective-permute-start | bytes 577544 | tf_op jit(solution)/shard_map/ppermute | solution.py:705
  96.8 2.0 %top.1 = f32[64,640]{1,0:T(8,128)} custom-call(f32[640,128]{1,0:T(8,128)S(1)} %bitcast.18, f32[4]{0:T(128)S(1)} %copy-done.29, f32[4]{0:T(128)S(1)} %copy-done.30, s32[4]{0:T(128)S(1)} %pad_add_fusion.info_ref), custom_call_target="tpu_custom_call" | custom-call | tf_op jit(solution)/shard_map/top/pallas_call | solution.py:740
  98.8 5.3 %all-to-all-start.2 = ((f32[8,8,640]{2,1,0:T(8,128)}), f32[8,8,640]{2,1,0:T(8,128)S(1)}, u32[]{:S(2)}, u32[]{:S(2)}) async-start(f32[8,8,640]{2,1,0:T(8,128)} %bitcast.10), calls=%async_computation.2 | async-start | bytes 327680 | tf_op jit(solution)/shard_map/all_to_all | solution.py:747
  104.2 1.3 %own.1.own_ref = f32[2048,128]{1,0:T(8,128)S(1)} custom-call(f32[2048,128]{1,0:T(8,128)S(1)} %get-tuple-element.36.in_ref, bf16[512,256]{1,0:T(8,128)(2,1)S(1)} %copy-done.1, bf16[256,512]{1,0:T(8,128)(2,1)S(1)} %copy-done), custom_call_target="tpu_custom_call" | custom-call | tf_op jit(solution)/shard_map/own/pallas_call | solution.py:752
  105.6 6.4 %levels.1 = (f32[768,256]{1,0:T(8,128)S(1)}, f32[144,256]{1,0:T(8,128)S(1)}) custom-call(f32[2048,128]{1,0:T(8,128)S(1)} %own.1.own_ref, f32[376,128]{1,0:T(8,128)S(1)} %collective-permute-done.2.before_ref, f32[376,128]{1,0:T(8,128)} %collective-permute-done.3.behind_ref, f32[768,128]{1,0:T(8,128)S(1)} %copy-done.13, ...), custom_call_target="tpu_custom_call" | custom-call | tf_op jit(solution)/shard_map/levels/pallas_call | solution.py:753
  112.1 1.8 %finish.1 = f32[768,256]{1,0:T(8,128)} custom-call(f32[768,256]{1,0:T(8,128)S(1)} %get-tuple-element.40.near_ref, f32[144,256]{1,0:T(8,128)S(1)} %get-tuple-element.41.mid_ref, f32[64,640]{1,0:T(8,128)S(1)} %bitcast.19, bf16[128,256]{1,0:T(8,128)(2,1)S(1)} %copy-done.21, bf16[16,128]{1,0:T(8,128)(2,1)S(1)} %copy-done.28, bf16[128,256]{1,0:T(8,128)(2,1)S(1)} %copy-done.20, ...), custom_call_target="tpu_custom_call" | custom-call | tf_op jit(solution)/shard_map/finish/pallas_call | solution.py:769
  (93 shorter events, 14.2 us)
Async XLA Ops:
  5.7 1.6 %copy-start.2 = (f32[4096,128]{1,0:T(8,128)S(1)}, f32[4096,128]{1,0:T(8,128)}, u32[]{:S(2)}) copy-start(f32[4096,128]{1,0:T(8,128)} %data_ref.1) | copy-start | bytes 6291460
  20.7 11.5 %copy-start.33 = (f32[9,9,9]{2,1,0:T(8,128)S(1)}, f32[9,9,9]{2,1,0:T(8,128)}, u32[]{:S(2)}) copy-start(f32[9,9,9]{2,1,0:T(8,128)} %param.24) | copy-start | bytes 8752
  20.7 11.5 %copy-start.34 = (f32[9,9,9]{2,1,0:T(8,128)S(1)}, f32[9,9,9]{2,1,0:T(8,128)}, u32[]{:S(2)}) copy-start(f32[9,9,9]{2,1,0:T(8,128)} %param.25) | copy-start | bytes 8752
  20.7 12.0 %slice-start = ((f32[9,9,9]{2,1,0:T(8,128)}), f32[9,5,9]{2,1,0:T(8,128)S(1)}, s32[]{:S(2)}) async-start(f32[9,9,9]{2,1,0:T(8,128)} %param.24), calls=%async_computation.3 | async-start | bytes 73728 | tf_op jit(solution)/shard_map/slice | solution.py:472
  20.7 12.1 %slice-start.1 = ((f32[9,9,9]{2,1,0:T(8,128)}), f32[9,5,9]{2,1,0:T(8,128)S(1)}, s32[]{:S(2)}) async-start(f32[9,9,9]{2,1,0:T(8,128)} %param.25), calls=%async_computation.4 | async-start | bytes 73728 | tf_op jit(solution)/shard_map/slice | solution.py:472
  20.7 42.3 %all-to-all-start = ((f32[128,33,1,128]{3,2,1,0:T(1,128)}), f32[128,33,1,128]{3,2,1,0:T(1,128)S(1)}, u32[]{:S(2)}, u32[]{:S(2)}) async-start(f32[128,33,1,128]{3,2,1,0:T(1,128)} %bitcast.4), calls=%async_computation | async-start | bytes 4325376 | tf_op jit(solution)/shard_map/all_to_all | solution.py:718
  32.9 4.0 %copy-start = (bf16[256,512]{1,0:T(8,128)(2,1)S(1)}, bf16[256,512]{1,0:T(8,128)(2,1)}, u32[]{:S(2)}) copy-start(bf16[256,512]{1,0:T(8,128)(2,1)} %constant.60.clone.y_ref.yf_ref) | copy-start | bytes 786436
  32.9 4.0 %copy-start.3 = (bf16[512,256]{1,0:T(8,128)(2,1)S(1)}, bf16[512,256]{1,0:T(8,128)(2,1)}, u32[]{:S(2)}) copy-start(bf16[512,256]{1,0:T(8,128)(2,1)} %constant.61.clone.z_ref.mzf_ref) | copy-start | bytes 786436
  68.2 28.6 %copy-start.29 = (f32[4]{0:T(128)S(1)}, f32[4]{0:T(128)}, u32[]{:S(2)}) copy-start(f32[4]{0:T(128)} %weights_ref.1) | copy-start | bytes 52
  68.2 28.6 %copy-start.30 = (f32[4]{0:T(128)S(1)}, f32[4]{0:T(128)}, u32[]{:S(2)}) copy-start(f32[4]{0:T(128)} %widths_ref.1) | copy-start | bytes 52
  77.5 19.3 %all-to-all-start.1 = ((f32[16,40,128]{2,1,0:T(8,128)}), f32[16,40,128]{2,1,0:T(8,128)S(1)}, u32[]{:S(2)}, u32[]{:S(2)}) async-start(f32[16,40,128]{2,1,0:T(8,128)} %bitcast.20), calls=%async_computation.1 | async-start | bytes 655360 | tf_op jit(solution)/shard_map/all_to_all | solution.py:737
  81.0 4.1 %collective-permute-start = (f32[376,128]{1,0:T(8,128)}, f32[376,128]{1,0:T(8,128)S(1)}, u32[]{:S(2)}, u32[]{:S(2)}) collective-permute-start(f32[376,128]{1,0:T(8,128)} %copy-done.32), channel_id=1, source_target_pairs={{0,1},{1,2},{2,3},{3,4},{4,5},{5,6},{6,7},{7,0},{8,9},{9,10},{10,1... | collective-permute-start | bytes 577544 | tf_op jit(solution)/shard_map/ppermute | solution.py:705
  82.2 5.6 %collective-permute-start.1 = (f32[376,128]{1,0:T(8,128)}, f32[376,128]{1,0:T(8,128)S(1)}, u32[]{:S(2)}, u32[]{:S(2)}) collective-permute-start(f32[376,128]{1,0:T(8,128)} %copy-done.31), channel_id=1, source_target_pairs={{1,0},{2,1},{3,2},{4,3},{5,4},{6,5},{7,6},{0,7},{9,8},{10,9},{11,1... | collective-permute-start | bytes 577544 | tf_op jit(solution)/shard_map/ppermute | solution.py:705
  89.9 15.7 %copy-start.8 = (f32[288,128]{1,0:T(8,128)S(1)}, f32[288,128]{1,0:T(8,128)}, u32[]{:S(2)}) copy-start(f32[288,128]{1,0:T(8,128)} %copy-done.6) | copy-start | bytes 442372
  89.9 15.7 %copy-start.11 = (f32[288,128]{1,0:T(8,128)S(1)}, f32[288,128]{1,0:T(8,128)}, u32[]{:S(2)}) copy-start(f32[288,128]{1,0:T(8,128)} %copy-done.9) | copy-start | bytes 442372
  89.9 15.7 %copy-start.15 = (bf16[512,256]{1,0:T(8,128)(2,1)S(1)}, bf16[512,256]{1,0:T(8,128)(2,1)}, u32[]{:S(2)}) copy-start(bf16[512,256]{1,0:T(8,128)(2,1)} %constant.68.clone.mzi_ref) | copy-start | bytes 786436
  91.8 13.7 %collective-permute-start.2 = (f32[376,128]{1,0:T(8,128)}, f32[376,128]{1,0:T(8,128)S(1)}, u32[]{:S(2)}, u32[]{:S(2)}) collective-permute-start(f32[376,128]{1,0:T(8,128)} %get-tuple-element.37), channel_id=1, source_target_pairs={{0,8},{8,16},{16,24},{24,32},{32,40},{40,48},{48,56},{56,64},{64,7... | collective-permute-start | bytes 577544 | tf_op jit(solution)/shard_map/ppermute | solution.py:705
  93.4 12.2 %collective-permute-start.3 = (f32[376,128]{1,0:T(8,128)}, f32[376,128]{1,0:T(8,128)}, u32[]{:S(2)}, u32[]{:S(2)}) collective-permute-start(f32[376,128]{1,0:T(8,128)} %get-tuple-element.38), channel_id=1, source_target_pairs={{8,0},{16,8},{24,16},{32,24},{40,32},{48,40},{56,48},{64,56},{72,6... | collective-permute-start | bytes 577544 | tf_op jit(solution)/shard_map/ppermute | solution.py:705
  98.8 13.2 %all-to-all-start.2 = ((f32[8,8,640]{2,1,0:T(8,128)}), f32[8,8,640]{2,1,0:T(8,128)S(1)}, u32[]{:S(2)}, u32[]{:S(2)}) async-start(f32[8,8,640]{2,1,0:T(8,128)} %bitcast.10), calls=%async_computation.2 | async-start | bytes 327680 | tf_op jit(solution)/shard_map/all_to_all | solution.py:747
  104.1 1.5 %copy-start.17 = (bf16[512,256]{1,0:T(8,128)(2,1)S(1)}, bf16[512,256]{1,0:T(8,128)(2,1)}, u32[]{:S(2)}) copy-start(bf16[512,256]{1,0:T(8,128)(2,1)} %constant.66.clone.zi_ref) | copy-start | bytes 786436
  105.5 6.6 %copy-start.20 = (bf16[128,256]{1,0:T(8,128)(2,1)S(1)}, bf16[128,256]{1,0:T(8,128)(2,1)}, u32[]{:S(2)}) copy-start(bf16[128,256]{1,0:T(8,128)(2,1)} %constant.71.clone.grow_z_ref) | copy-start | bytes 196612
  105.5 6.6 %copy-start.21 = (bf16[128,256]{1,0:T(8,128)(2,1)S(1)}, bf16[128,256]{1,0:T(8,128)(2,1)}, u32[]{:S(2)}) copy-start(bf16[128,256]{1,0:T(8,128)(2,1)} %constant.69.clone.grow_top_ref) | copy-start | bytes 196612
  105.5 6.6 %copy-start.26 = (bf16[192,128]{1,0:T(8,128)(2,1)S(1)}, bf16[192,128]{1,0:T(8,128)(2,1)}, u32[]{:S(2)}) copy-start(bf16[192,128]{1,0:T(8,128)(2,1)} %constant.72.clone.grow_fine_ref) | copy-start | bytes 147460
  105.5 6.6 %copy-start.28 = (bf16[16,128]{1,0:T(8,128)(2,1)S(1)}, bf16[16,128]{1,0:T(8,128)(2,1)}, u32[]{:S(2)}) copy-start(bf16[16,128]{1,0:T(8,128)(2,1)} %constant.70.clone.grow_y_ref) | copy-start | bytes 12292
  (20 other events, 17.5 us)

commit v3 on v2

--- a/solution.py
+++ b/solution.py
@@ -24,22 +24,49 @@
 BF16 = jnp.bfloat16
 VM = pl.BlockSpec(memory_space=pltpu.VMEM)
 SM = pl.BlockSpec(memory_space=pltpu.SMEM)
-ANY = pl.BlockSpec(memory_space=pl.ANY)
-
-
-def call(body, name, out, ins, scratch=(), limit=20, flops=0, moved=0):
+HB = pl.BlockSpec(memory_space=pltpu.HBM)
+
+
+def call(body, name, out, ins, scratch=(), limit=20, flops=0, moved=0, outs=VM):
     many = isinstance(out, tuple)
-    return pl.pallas_call(
+    outs = outs if isinstance(outs, tuple) else (outs,) * (len(out) if many else 1)
+    shapes = tuple(
+        pltpu.HBM(shape.shape, shape.dtype) if spec is HB else shape
+        for shape, spec in zip(out if many else (out,), outs)
+    )
+    kernel = pl.pallas_call(
         body,
-        out_shape=out,
+        out_shape=shapes if many else shapes[0],
         in_specs=ins,
-        out_specs=(VM,) * len(out) if many else VM,
+        out_specs=outs if many else outs[0],
         scratch_shapes=list(scratch),
         compiler_params=pltpu.CompilerParams(vmem_limit_bytes=limit << 20),
         cost_estimate=pl.CostEstimate(flops=flops, bytes_accessed=moved, transcendentals=0),
         name=name,
     )
 
+    def run(*args):
+        placed = [
+            pltpu.with_memory_space_constraint(jnp.asarray(arg), pltpu.HBM) if spec is HB else arg
+            for arg, spec in zip(args, ins)
+        ]
+        return kernel(*placed)
+
+    return run
+
+
+def started(pairs, sems, first=0):
+    copies = []
+    for n, (source, target) in enumerate(pairs):
+        copy = pltpu.make_async_copy(source, target, sems.at[first + n])
+        copy.start()
+        copies.append(copy)
+    return copies
+
+
+def buffers(*tables):
+    return [pltpu.VMEM(table.shape, table.dtype) for table in tables]
+
 
 def array(*shape):
     return jax.ShapeDtypeStruct(shape, F32)
@@ -60,7 +87,10 @@
     return top, (matrix - top.astype(np.float32)).astype(BF16)
 
 
-def route_kernel(tile_ref, info_ref, pos_ref, ids_ref, owner_s, code_s, acc_s):
+def send_kernel(
+    tile_ref, info_ref, data_ref, out_ref, data_s, out_s, pos_ref, pos_s, owner_s, code_s, acc_s, sems
+):
+    (data_copy,) = started([(data_ref, data_s)], sems)
     tile = tile_ref[...]
     column = tile >> 1
     high_part = column >> 6
@@ -101,49 +131,45 @@
         return base + counted[:, 128:]
 
     lax.fori_loop(0, tile.shape[0], chunk, jnp.zeros((128, 128), F32), unroll=4)
-    ids_ref[...] = acc_s[:128] * 16.0 + acc_s[128:]
-
-
-def route(tile, info):
+    (pos_copy,) = started([(pos_ref, pos_s)], sems, 1)
+    for b in range(DEVICES // 8):
+        ids = acc_s[b * 8 : b * 8 + 8, :] * 16.0 + acc_s[128 + b * 8 : 136 + b * 8, :]
+        for j in range(8):
+            at = (b * 8 + j) * ROWS + CAP
+            out_s[at : at + 1, :] = ids[j : j + 1]
+    pos_copy.wait()
+    data_copy.wait()
+
+    def body(c, carry):
+        for g in range(16):
+            block = data_s[pl.ds(pl.multiple_of(c * 128 + g * 8, 8), 8), :]
+            for j in range(8):
+                out_s[pl.ds(pos_s[c, g * 8 + j], 1), :] = block[j : j + 1]
+        return carry
+
+    lax.fori_loop(0, 32, body, 0)
+    (out_copy,) = started([(out_s, out_ref)], sems, 2)
+    out_copy.wait()
+
+
+def send(tile, info, data):
     return call(
-        route_kernel,
-        "route",
-        (jax.ShapeDtypeStruct((32, 128), jnp.int32), array(128, 128)),
-        [VM, SM],
+        send_kernel,
+        "send",
+        array(DEVICES * ROWS, 128),
+        [VM, SM, HB],
         [
+            pltpu.VMEM((4096, 128), F32),
+            pltpu.VMEM((DEVICES * ROWS, 128), F32),
+            pltpu.VMEM((32, 128), jnp.int32),
+            pltpu.SMEM((32, 128), jnp.int32),
             pltpu.VMEM((32, 128), jnp.int32),
             pltpu.VMEM((32, 128), jnp.int32),
             pltpu.VMEM((256, 128), F32),
+            pltpu.SemaphoreType.DMA((3,)),
         ],
-    )(tile, info)
-
-
-def pack_kernel(pos_ref, data_ref, ids_ref, out_ref):
-    step = 16
-
-    def body(b, carry):
-        start = pl.multiple_of(b * step, step)
-        block = data_ref[pl.ds(start, step), :]
-        row = b // (128 // step)
-        lane = (b % (128 // step)) * step
-        for j in range(step):
-            out_ref[pl.ds(pos_ref[row, lane + j], 1), :] = block[j : j + 1]
-        return carry
-
-    lax.fori_loop(0, 4096 // step, body, 0)
-
-    def tail(b, carry):
-        start = pl.multiple_of(b * 8, 8)
-        block = ids_ref[pl.ds(start, 8), :]
-        for j in range(8):
-            out_ref[pl.ds((start + j) * ROWS + CAP, 1), :] = block[j : j + 1]
-        return carry
-
-    lax.fori_loop(0, DEVICES // 8, tail, 0)
-
-
-def pack(pos, data, ids):
-    return call(pack_kernel, "pack", array(DEVICES * ROWS, 128), [SM, VM, VM])(pos, data, ids)
+        outs=HB,
+    )(tile, info, data)
 
 
 def thin_pair(count):
@@ -211,10 +237,13 @@
     return mm(top, matrix_ref[...]) + mm(rest, matrix_ref[...])
 
 
-def collect_kernel(
-    in_ref, thin_z_ref, thin_y_ref, top_rows_ref, top_z_ref, *refs
-):
-    fine_ref, mid_ref, low_ref, high_ref, top_ref, data_s, ids_s, slab_s = refs[-8:]
+def collect_kernel(in_ref, *refs):
+    tables = refs[:4]
+    outs = refs[-18:-13]
+    data_s, ids_s, slab_s = refs[-13:-10]
+    thin_z_ref, thin_y_ref, top_rows_ref, top_z_ref = refs[-10:-6]
+    fine_ref, mid_ref, low_ref, high_ref, top_ref, sems = refs[-6:]
+    table_copies = started(list(zip(tables, refs[-10:-6])), sems)
     for c in range(DEVICES // 4):
         total = None
         for j in range(4):
@@ -241,6 +270,7 @@
         return carry
 
     lax.fori_loop(0, 6, block, 0)
+    out_copies = started([(fine_ref, outs[0])], sems, 4)
     for i in range(17):
         total = None
         for x, weight in ((2 * i, 1.0), (2 * i - 1, 0.5), (2 * i + 1, 0.5)):
@@ -256,14 +286,11 @@
                 total = term if total is None else total + term
         slab_s[i * CY : (i + 1) * CY, :] = total
     slab_s[17 * CY :, :] = jnp.zeros((7 * CY, NZ), F32)
+    for copy in table_copies:
+        copy.wait()
     for g in range(3):
         part = exact_right(slab_s[g * 192 : (g + 1) * 192, :], thin_z_ref)
         mid_ref[g * 128 : (g + 1) * 128, :] = exact_left(thin_y_ref, part)
-    stacked = exact_left(top_rows_ref, mid_ref[: 17 * 16, :])
-    pair = jnp.concatenate([stacked[:TOP_ROWS], stacked[TOP_ROWS:]], axis=1)
-    top_charge = exact_right(pair, top_z_ref)
-    for s in range(SIZE_X):
-        top_ref[s * TOP_ROWS : (s + 1) * TOP_ROWS, :] = top_charge
     for h in range(2):
         for c in range(4):
             at = slice((h * 4 + c) * CX, (h * 4 + c + 1) * CX)
@@ -273,6 +300,15 @@
         at = slice(256 + j * 24, 256 + (j + 1) * 24)
         low_ref[at, :] = mid_ref[pl.ds(j, 24, stride=16), :]
         high_ref[at, :] = mid_ref[pl.ds(8 + j, 24, stride=16), :]
+    out_copies += started([(mid_ref, outs[1]), (low_ref, outs[2]), (high_ref, outs[3])], sems, 5)
+    stacked = exact_left(top_rows_ref, mid_ref[: 17 * 16, :])
+    pair = jnp.concatenate([stacked[:TOP_ROWS], stacked[TOP_ROWS:]], axis=1)
+    top_charge = exact_right(pair, top_z_ref)
+    for s in range(SIZE_X):
+        top_ref[s * TOP_ROWS : (s + 1) * TOP_ROWS, :] = top_charge
+    out_copies += started([(top_ref, outs[4])], sems, 8)
+    for copy in out_copies:
+        copy.wait()
 
 
 def collect(arrived, *after):
@@ -282,34 +318,50 @@
         plain(top_rows_matrix()),
         plain(twice(thin_cycle(128))),
     )
+    out = (
+        array(2 * CX * CY, 128),
+        array(24 * 16, 128),
+        array(SEND, 128),
+        array(SEND, 128),
+        array(SIZE_X * TOP_ROWS, 128),
+    )
     return call(
         collect_kernel,
         "collect",
-        (
-            array(2 * CX * CY, 128),
-            array(24 * 16, 128),
-            array(SEND, 128),
-            array(SEND, 128),
-            array(SIZE_X * TOP_ROWS, 128),
-        ),
-        [VM] * 5 + [ANY] * len(after),
+        out,
+        [VM] + [HB] * (4 + len(after)),
         [
             pltpu.VMEM((DEVICES * CAP, 256), BF16),
             pltpu.VMEM((DEVICES // 4, 128), jnp.int32),
             pltpu.VMEM((24 * CY, NZ), F32),
+            *buffers(*tables),
+            *buffers(*out),
+            pltpu.SemaphoreType.DMA((9,)),
         ],
+        outs=HB,
     )(arrived, *tables, *after)
 
 
-def merge_kernel(fine_ref, mid_ref, before_ref, behind_ref, near_ref, wide_ref, low_ref, high_ref):
-    for n in range(2 * CX):
-        near_ref[n * YD : n * YD + CY, :] = fine_ref[n * CY : (n + 1) * CY, :]
+def merge_kernel(
+    fine_hbm, mid_hbm, before_ref, behind_ref, halo_hbm, wide_hbm, low_hbm, high_hbm,
+    fine_s, mid_ref, halo_ref, wide_ref, low_ref, high_ref, sems,
+):
+    pairs = [(mid_hbm, mid_ref)]
+    for h in range(2):
+        for first, at in ((0, 0), (CX - 4, 4)):
+            start = (h * CX + first) * CY
+            pairs.append(
+                (fine_hbm.at[pl.ds(start, 4 * CY)], fine_s.at[pl.ds((h * 8 + at) * CY, 4 * CY)])
+            )
+    mid_copy, *fine_copies = started(pairs, sems)
     for h in range(2):
         for c in range(4):
             at = slice((h * 4 + c) * CX, (h * 4 + c + 1) * CX)
-            start = h * CX * YD + CY + c
-            near_ref[pl.ds(start, CX, stride=YD), :] = behind_ref[at, :]
-            near_ref[pl.ds(start + 4, CX, stride=YD), :] = before_ref[at, :]
+            start = h * CX * 8 + c
+            halo_ref[pl.ds(start, CX, stride=8), :] = behind_ref[at, :]
+            halo_ref[pl.ds(start + 4, CX, stride=8), :] = before_ref[at, :]
+    out_copies = started([(halo_ref, halo_hbm)], sems, 5)
+    mid_copy.wait()
     for i in range(24):
         wide_ref[i * YD : i * YD + 16, :] = mid_ref[i * 16 : (i + 1) * 16, :]
         wide_ref[i * YD + 16 : (i + 1) * YD, :] = jnp.zeros((16, 128), F32)
@@ -324,10 +376,17 @@
         if j == 4:
             before = before + wide_ref[pl.ds(0, 24, stride=YD), :]
         wide_ref[pl.ds(row, 24, stride=YD), :] = before
-    for ref, first, mid_first in ((low_ref, 0, 0), (high_ref, CX - 4, 12)):
+    out_copies += started([(wide_ref, wide_hbm)], sems, 6)
+    for copy in fine_copies:
+        copy.wait()
+    for ref, first, at_fine, mid_first in ((low_ref, 0, 0, 0), (high_ref, CX - 4, 4, 12)):
         for h in range(2):
-            base = (h * CX + first) * YD
-            ref[h * 128 : (h + 1) * 128, :] = near_ref[base : base + 128, :]
+            for x in range(4):
+                at = h * 128 + x * YD
+                source = (h * 8 + at_fine + x) * CY
+                ref[at : at + CY, :] = fine_s[source : source + CY, :]
+                source = (h * CX + first + x) * 8
+                ref[at + CY : at + YD, :] = halo_ref[source : source + 8, :]
         for i in range(5):
             base = (mid_first + i) * YD
             at = 256 + i * 24
@@ -335,14 +394,25 @@
             ref[at + 16 : at + 24, :] = (
                 wide_ref[base + 16 : base + 24, :] + wide_ref[base + 24 : base + 32, :]
             )
+    out_copies += started([(low_ref, low_hbm), (high_ref, high_hbm)], sems, 7)
+    for copy in out_copies:
+        copy.wait()
 
 
 def merge(fine, mid, before, behind):
+    out = (array(2 * CX * 8, 128), array(24 * YD, 128), array(SEND, 128), array(SEND, 128))
     return call(
         merge_kernel,
         "merge",
-        (array(2 * CX * YD, 128), array(24 * YD, 128), array(SEND, 128), array(SEND, 128)),
-        [VM] * 4,
+        out,
+        [HB, HB, VM, VM],
+        [
+            pltpu.VMEM((16 * CY, 128), F32),
+            pltpu.VMEM((24 * 16, 128), F32),
+            *buffers(*out),
+            pltpu.SemaphoreType.DMA((9,)),
+        ],
+        outs=HB,
     )(fine, mid, before, behind)
 
 
@@ -450,7 +520,7 @@
     return right_product(jnp.concatenate(rows, axis=0), z_ref)
 
 
-def taps_kernel(copies, in_ref, z_ref, y_ref, after_ref, real_ref, twin_ref, imag_ref):
+def taps_kernel(copies, in_ref, z_ref, y_ref, after_ref, out_ref):
     lane_special, row = special_mask(copies, YD)
     special = lane_special & ((row == 0) | (row == 16))
     for p in range(2):
@@ -460,10 +530,10 @@
             if dx > 8:
                 break
             real, imag = slabs[j][:YD], slabs[j][YD:]
-            at = slice(dx * YD, (dx + 1) * YD)
-            real_ref[at, :] = real
-            twin_ref[at, :] = jnp.where(special, imag, real)
-            imag_ref[at, :] = jnp.where(special, 0.0, imag)
+            values = (real, jnp.where(special, imag, real), jnp.where(special, 0.0, imag))
+            for part in range(3):
+                at = (part * 9 + dx) * YD
+                out_ref[at : at + YD, :] = values[part]
 
 
 def taps(kernel, copies, z_matrix, y_matrix, after):
@@ -480,23 +550,31 @@
     return call(
         functools.partial(taps_kernel, copies),
         f"taps{copies}",
-        (array(9 * YD, 128),) * 3,
-        [VM] * 3 + [ANY],
+        array(27 * YD, 128),
+        [VM] * 3 + [HB],
     )(wide.reshape(16 * YD, 256), z_matrix, y_matrix, after)
 
 
-def own_kernel(in_ref, z_ref, y_ref, out_ref):
+def own_kernel(fine_hbm, halo_hbm, z_hbm, y_hbm, out_ref, fine_s, halo_s, z_ref, y_ref, sems):
+    copies = started(
+        [(z_hbm, z_ref), (y_hbm, y_ref), (fine_hbm, fine_s), (halo_hbm, halo_s)], sems
+    )
+    for copy in copies:
+        copy.wait()
     for p in range(CX // 8):
-        value = jnp.concatenate(
-            [in_ref[h * CX * YD + p * 256 : h * CX * YD + (p + 1) * 256, :] for h in range(2)], axis=1
-        )
-        slabs = forward_chunk(value, z_ref, y_ref, 1)
+        columns = []
+        for h in range(2):
+            rows = []
+            for j in range(8):
+                n = h * CX + p * 8 + j
+                rows += [fine_s[n * CY : (n + 1) * CY, :], halo_s[n * 8 : (n + 1) * 8, :]]
+            columns.append(jnp.concatenate(rows, axis=0))
+        slabs = forward_chunk(jnp.concatenate(columns, axis=1), z_ref, y_ref, 1)
         for j in range(8):
             out_ref[(p * 8 + j) * 64 : (p * 8 + j + 1) * 64, :] = slabs[j]
 
 
-def convolve(copies, block_out, blocks, spectrum, freq_s, conv_s):
-    real_ref, twin_ref, imag_ref = spectrum
+def convolve(copies, block_out, blocks, taps_ref, freq_s, conv_s):
     lane_special, row = special_mask(copies, 8)
 
     def step(index, carry):
@@ -506,8 +584,13 @@
         for dx in range(9):
             coefs = []
             for half in range(2):
-                at = pl.ds(pl.multiple_of(dx * YD + half * 16 + v * 8, 8), 8)
-                coefs.append((real_ref[at, :], twin_ref[at, :], imag_ref[at, :]))
+                at = dx * YD + half * 16 + v * 8
+                coefs.append(
+                    [
+                        taps_ref[pl.ds(pl.multiple_of(at + part * 9 * YD, 8), 8), :]
+                        for part in range(3)
+                    ]
+                )
             for j in range(block_out):
                 base = (first + j + dx) * 64 + v * 8
                 for half in range(2):
@@ -547,20 +630,24 @@
 
 
 def levels_kernel(
-    own_ref, before_ref, behind_ref, wide_ref,
-    nr_ref, nt_ref, ni_ref, mr_ref, mt_ref, mi_ref,
-    zf_ref, yf_ref, zi_ref, yi_ref, mzf_ref, mzi_ref,
-    near_ref, mid_ref, freq_s, conv_s, mid_freq_s, mid_conv_s,
+    own_ref, before_ref, behind_ref, *refs
 ):
+    near_ref, mid_ref, freq_s, conv_s, mid_freq_s, mid_conv_s = refs[9:15]
+    zf_ref, yf_ref, mzf_ref, wide_ref, near_taps, zi_ref, yi_ref, mid_taps, mzi_ref = refs[15:24]
+    copies = started(list(zip(refs[:9], refs[15:24])), refs[24])
     freq_s[4 * 64 : 36 * 64, :] = own_ref[...]
     edges = [
         jnp.concatenate([ref[:128, :], ref[128:256, :]], axis=1) for ref in (before_ref, behind_ref)
     ]
+    copies[0].wait()
+    copies[1].wait()
     slabs = forward_chunk(jnp.concatenate(edges, axis=0), zf_ref, yf_ref, 1)
     for j in range(8):
         at = j if j < 4 else 32 + j
         freq_s[at * 64 : (at + 1) * 64, :] = slabs[j]
     zero = jnp.zeros((YD, 128), F32)
+    copies[2].wait()
+    copies[3].wait()
     for p in range(3):
         pairs = []
         for j in range(8):
@@ -584,14 +671,19 @@
         for j in range(8):
             at = p * 8 + j
             mid_freq_s[at * 64 : (at + 1) * 64, :] = slabs[j]
-    convolve(1, 8, 4, (nr_ref, nt_ref, ni_ref), freq_s, conv_s)
+    copies[4].wait()
+    convolve(1, 8, 4, near_taps, freq_s, conv_s)
+    copies[5].wait()
+    copies[6].wait()
     for p in range(4):
         slabs = [conv_s[(p * 8 + j) * 64 : (p * 8 + j + 1) * 64, :] for j in range(8)]
         space = inverse_chunk(slabs, zi_ref, yi_ref)
         for j in range(8):
             x = p * 8 + j
             near_ref[x * CY : (x + 1) * CY, :] = space[j * YD : j * YD + CY]
-    convolve(2, 9, 1, (mr_ref, mt_ref, mi_ref), mid_freq_s, mid_conv_s)
+    copies[7].wait()
+    copies[8].wait()
+    convolve(2, 9, 1, mid_taps, mid_freq_s, mid_conv_s)
     mid_conv_s[9 * 64 :, :] = jnp.zeros((7 * 64, 128), F32)
     for p in range(2):
         slabs = [mid_conv_s[(p * 8 + j) * 64 : (p * 8 + j + 1) * 64, :] for j in range(8)]
@@ -659,10 +751,17 @@
     out_ref[...] = mm(left[0], right[0]) + mm(left[0], right[1]) + mm(left[1], right[0])
 
 
-def finish_kernel(near_ref, mid_ref, top_ref, grow_top_ref, grow_y_ref, grow_z_ref, grow_fine_ref, out_ref, grown_s):
+def finish_kernel(
+    near_ref, mid_ref, top_ref, *refs
+):
+    out_ref, grown_s = refs[4:6]
+    grow_top_ref, grow_y_ref, grow_z_ref, grow_fine_ref, sems = refs[6:]
+    copies = started(list(zip(refs[:4], refs[6:10])), sems)
     total = top_ref[:8, :]
     for s in range(1, SIZE_Y):
         total = total + top_ref[s * 8 : (s + 1) * 8, :]
+    for copy in copies:
+        copy.wait()
     lanes = []
     for ip in range(5):
         lanes.append(exact_right(total[:, ip * 128 : (ip + 1) * 128], grow_top_ref))
@@ -713,10 +812,9 @@
     info = jnp.stack(
         [block_count[0], ((at_x * SIZE_Y + at_y) % 4) * CAP, at_x, at_y]
     ).astype(jnp.int32)
-    pos, ids = route(block_tile.reshape(32, 128), info)
-    outgoing = pack(pos, charge_blocks, ids)
+    outgoing = send(block_tile.reshape(32, 128), info, charge_blocks)
     arrived = lax.all_to_all(
-        outgoing.reshape(DEVICES, ROWS, 1, 128),
+        outgoing.reshape(DEVICES, 1, ROWS * 128),
         ("gx", "gy"),
         split_axis=0,
         concat_axis=0,
@@ -732,7 +830,7 @@
     near_taps = taps(near_kernel, 1, zf, yf, outgoing)
     mid_taps = taps(mid_kernel, 2, mzf, yf, outgoing)
 
-    fine, mid, low, high, top = collect(arrived, *near_taps, *mid_taps)
+    fine, mid, low, high, top = collect(arrived, near_taps, mid_taps)
     before, behind = swap(low, high, "gy")
     tops = lax.all_to_all(
         top.reshape(SIZE_X, TOP_ROWS, 128), "gx", split_axis=0, concat_axis=0, tiled=True
@@ -747,36 +845,47 @@
     partial = lax.all_to_all(
         partial.reshape(SIZE_Y, 8, 640), "gy", split_axis=0, concat_axis=0, tiled=True
     ).reshape(64, 640)
-    near_rows, wide, low, high = merge(fine, mid, before, behind)
+    halo, wide, low, high = merge(fine, mid, before, behind)
     before, behind = swap(low, high, "gx")
-    own = call(own_kernel, "own", array(CX * 64, 128), [VM] * 3)(near_rows, zf, yf)
+    own = call(
+        own_kernel,
+        "own",
+        array(CX * 64, 128),
+        [HB] * 4,
+        buffers(fine, halo, zf, yf) + [pltpu.SemaphoreType.DMA((4,))],
+    )(fine, halo, zf, yf)
+    tables = (zf, yf, mzf, wide, near_taps, zi, yi, mid_taps, mzi)
     near, mid_near = call(
         levels_kernel,
         "levels",
         (array(CX * CY, NZ), array(9 * 16, 256)),
-        [VM] * 16,
+        [VM] * 3 + [HB] * 9,
         [
             pltpu.VMEM((40 * 64, 128), F32),
             pltpu.VMEM((32 * 64, 128), F32),
             pltpu.VMEM((24 * 64, 128), F32),
             pltpu.VMEM((16 * 64, 128), F32),
+            *buffers(*tables),
+            pltpu.SemaphoreType.DMA((9,)),
         ],
-    )(own, before, behind, wide, *near_taps, *mid_taps, zf, yf, zi, yi, mzf, mzi)
+    )(own, before, behind, *tables)
     grow_z = grow_matrix(2 * 64, 65)
     grow_z[:, 0] += grow_z[:, 64]
     grow_fine_z = grow_matrix(2 * 128, 129)
     grow_fine_z[:, 0] += grow_fine_z[:, 128]
-    out = call(
-        finish_kernel, "finish", array(CX * CY, NZ), [VM] * 7, [pltpu.VMEM((24 * CY, NZ), F32)]
-    )(
-        near,
-        mid_near,
-        partial,
+    tables = (
         plain(twice(grow_z[:, :64].T)),
         plain(padded(grow_matrix(13, 7), 16, 128)),
         plain(grow_fine_z[:, :128].T),
         plain(np.kron(np.eye(8), padded(grow_matrix(CY, 13), CY, 16))),
     )
+    out = call(
+        finish_kernel,
+        "finish",
+        array(CX * CY, NZ),
+        [VM] * 3 + [HB] * 4,
+        [pltpu.VMEM((24 * CY, NZ), F32), *buffers(*tables), pltpu.SemaphoreType.DMA((4,))],
+    )(near, mid_near, partial, *tables)
     return out.reshape(CX, CY, NZ)
 
 

time: 115 us -> 97.8 us (0.85)
  local copies, waits for them, and re-layouts: 18.7 us -> 5.67 us
  Pallas kernels: 37.8 us -> 34.3 us
    unnamed x70 -> x20, local copies, waits for them, and re-layouts: 15.3 us -> 2.31 us
    pallas_call x10 -> x9, Pallas kernels: 37.8 us -> 34.3 us  [run(): return kernel(*placed)]
  transfers between devices with their start and end apart: 7 -> 7, of which waited for: 3 -> 3; matrix products, arithmetic and copies ran while one was open for 4% -> 5% of each run, Pallas kernels for 11% -> 16%
where the time goes in v3:
time: 97.8 us; the launch traced here: 97.2 us
  Pallas kernels  34.3 us (35%)
  waiting for transfers between devices  28.2 us (29%)
  starting transfers between devices  26.9 us (28%)
  local copies, waits for them, and re-layouts  5.67 us (6%)
  other arithmetic  1.19 us (1%)
    pallas_call x9, Pallas kernels, run(): return kernel(*placed)  34.3 us
    all_to_all x1, waiting for transfers between devices, on_device(): lax.all_to_all(outgoing.reshape(DEVICES, 1, ROWS * 128), ('gx', 'gy'), sp...  22.8 us
    all_to_all x1, starting transfers between devices, on_device(): lax.all_to_all(outgoing.reshape(DEVICES, 1, ROWS * 128), ('gx', 'gy'), sp...  11.5 us
    all_to_all x1, starting transfers between devices, on_device(): lax.all_to_all(partial.reshape(SIZE_Y, 8, 640), 'gy', split_axis=0, conca...  5.3 us
    ppermute x2, starting transfers between devices, swap(): lax.ppermute(to_low, axis, backward)  3.68 us
    all_to_all x1, starting transfers between devices, on_device(): lax.all_to_all(top.reshape(SIZE_X, TOP_ROWS, 128), 'gx', split_axis=0, co...  3.59 us
    ppermute x2, starting transfers between devices, swap(): lax.ppermute(to_high, axis, forward)  2.78 us
    ppermute x2, waiting for transfers between devices, swap(): lax.ppermute(to_high, axis, forward)  2.7 us
  transfers between devices with their start and end apart: 7, of which 3 were waited for; matrix products, arithmetic and copies ran while one was open for 5% of the time, Pallas kernels for 16%

profile of v3, /device:TPU:1, one launch (start us, length us, event | category | flops | bytes accessed | tf_op | source)
XLA Modules:
  0.0 97.2 jit_solution(11580204896779336296)
XLA Ops:
  1.5 9.6 %send.1.after_ref = f32[4224,128]{1,0:T(8,128)} custom-call(s32[32,128]{1,0:T(8,128)S(1)} %bitcast.20, s32[4]{0:T(128)S(1)} %pad_add_fusion.info_ref, f32[4096,128]{1,0:T(8,128)} %data_ref.1), custom_call_target="tpu_custom_call" | custom-call | tf_op jit(solution)/shard_map/send/pallas_call | solution.py:53
  11.1 11.5 %all-to-all-start = ((f32[128,1,4224]{2,1,0:T(1,128)}), f32[128,1,4224]{2,1,0:T(1,128)S(1)}, u32[]{:S(2)}, u32[]{:S(2)}) async-start(f32[128,1,4224]{2,1,0:T(1,128)} %bitcast.21), calls=%async_computation | async-start | bytes 4325376 | tf_op jit(solution)/shard_map/all_to_all | solution.py:816
  23.4 0.8 slice.49
  24.2 0.8 slice.51
  24.9 1.2 %concatenate.25 = f32[9,32,256]{2,1,0:T(8,128)S(1)} concatenate(f32[9,32,5]{2,1,0:T(8,128)} %slice.51, f32[9,32,119]{2,1,0:T(8,128)S(1)} %broadcast_in_dim.7, f32[9,32,9]{2,1,0:T(8,128)S(1)} %get-tuple-element.27, f32[9,32,119]{2,1,0:T(8,128)S(1)} %broadcast_in_dim.7, f32[9,32,4]{2,1,0:T(8,128)S(1)} %bitcast.22), dimensions={2} | concatenate | bytes 589824 | tf_op jit(solution)/shard_map/concatenate | solution.py:548
  26.1 1.0 %pad_maximum_fusion = f32[9,32,256]{2,1,0:T(8,128)S(1)} fusion(f32[9,32,4]{2,1,0:T(8,128)S(1)} %bitcast.23, f32[9,32,5]{2,1,0:T(8,128)} %slice.49, f32[256]{0:T(256)S(1)} %pad.6.clone), kind=kLoop, calls=%fused_computation | loop fusion | flops 147456 | bytes 306304 | tf_op jit(solution)/shard_map/concatenate | solution.py:545
  27.2 0.9 taps2.1.refs_5_.refs_7_
  28.2 0.8 copy-done.1
  28.9 0.9 taps1.1.refs_4_
  29.8 0.8 copy-done.2
  30.6 22.8 %all-to-all-done = f32[128,1,4224]{2,1,0:T(1,128)S(1)} async-done(((f32[128,1,4224]{2,1,0:T(1,128)}), f32[128,1,4224]{2,1,0:T(1,128)S(1)}, u32[]{:S(2)}, u32[]{:S(2)}) %all-to-all-start) | async-done | bytes 2162720 | tf_op jit(solution)/shard_map/all_to_all | solution.py:816
  53.4 6.5 %collect.1 = (f32[1536,128]{1,0:T(8,128)}, f32[384,128]{1,0:T(8,128)}, f32[376,128]{1,0:T(8,128)}, f32[376,128]{1,0:T(8,128)}, f32[640,128]{1,0:T(8,128)}) custom-call(f32[4224,128]{1,0:T(8,128)S(1)} %bitcast.15, bf16[256,128]{1,0:T(8,128)(2,1)} %constant.62.clone.refs_0_, bf16[128,192]{1,0:T(8,128)(2,1)} %constant.63.clone.refs_1_, ...), custom_call_target="tpu_custom_call" | custom-call | tf_op jit(solution)/shard_map/collect/pallas_call | solution.py:53
  59.9 3.6 %all-to-all-start.1 = ((f32[16,40,128]{2,1,0:T(8,128)}), f32[16,40,128]{2,1,0:T(8,128)S(1)}, u32[]{:S(2)}, u32[]{:S(2)}) async-start(f32[16,40,128]{2,1,0:T(8,128)} %bitcast.24), calls=%async_computation.1 | async-start | bytes 655360 | tf_op jit(solution)/shard_map/all_to_all | solution.py:835
  63.5 1.2 %collective-permute-start = (f32[376,128]{1,0:T(8,128)}, f32[376,128]{1,0:T(8,128)S(1)}, u32[]{:S(2)}, u32[]{:S(2)}) collective-permute-start(f32[376,128]{1,0:T(8,128)} %get-tuple-element.18), channel_id=1, source_target_pairs={{0,1},{1,2},{2,3},{3,4},{4,5},{5,6},{6,7},{7,0},{8,9},{9,10},{10,1... | collective-permute-start | bytes 577544 | tf_op jit(solution)/shard_map/ppermute | solution.py:804
  64.9 2.7 %collective-permute-done.before_ref = f32[376,128]{1,0:T(8,128)S(1)} collective-permute-done((f32[376,128]{1,0:T(8,128)}, f32[376,128]{1,0:T(8,128)S(1)}, u32[]{:S(2)}, u32[]{:S(2)}) %collective-permute-start) | collective-permute-done | bytes 192544 | tf_op jit(solution)/shard_map/ppermute | solution.py:804
  67.6 2.7 %collective-permute-done.1.behind_ref = f32[376,128]{1,0:T(8,128)S(1)} collective-permute-done((f32[376,128]{1,0:T(8,128)}, f32[376,128]{1,0:T(8,128)S(1)}, u32[]{:S(2)}, u32[]{:S(2)}) %collective-permute-start.1) | collective-permute-done | bytes 192544 | tf_op jit(solution)/shard_map/ppermute | solution.py:804
  70.3 2.1 %merge.1 = (f32[512,128]{1,0:T(8,128)}, f32[768,128]{1,0:T(8,128)}, f32[376,128]{1,0:T(8,128)}, f32[376,128]{1,0:T(8,128)}) custom-call(f32[1536,128]{1,0:T(8,128)} %get-tuple-element.16.fine_hbm, f32[384,128]{1,0:T(8,128)} %get-tuple-element.17.mid_hbm, f32[376,128]{1,0:T(8,128)S(1)} %collective-permute-done.before_ref, ...), custom_call_target="tpu_custom_call" | custom-call | tf_op jit(solution)/shard_map/merge/pallas_call | solution.py:53
  72.4 1.6 %collective-permute-start.2 = (f32[376,128]{1,0:T(8,128)}, f32[376,128]{1,0:T(8,128)S(1)}, u32[]{:S(2)}, u32[]{:S(2)}) collective-permute-start(f32[376,128]{1,0:T(8,128)} %get-tuple-element.21), channel_id=1, source_target_pairs={{0,8},{8,16},{16,24},{24,32},{32,40},{40,48},{48,56},{56,64},{64,7... | collective-permute-start | bytes 577544 | tf_op jit(solution)/shard_map/ppermute | solution.py:804
  74.0 3.5 %collective-permute-start.3 = (f32[376,128]{1,0:T(8,128)}, f32[376,128]{1,0:T(8,128)S(1)}, u32[]{:S(2)}, u32[]{:S(2)}) collective-permute-start(f32[376,128]{1,0:T(8,128)} %get-tuple-element.22), channel_id=1, source_target_pairs={{8,0},{16,8},{24,16},{32,24},{40,32},{48,40},{56,48},{64,56},{72,6... | collective-permute-start | bytes 577544 | tf_op jit(solution)/shard_map/ppermute | solution.py:804
  77.5 2.0 %top.1 = f32[64,640]{1,0:T(8,128)} custom-call(f32[640,128]{1,0:T(8,128)S(1)} %bitcast.18, f32[4]{0:T(128)S(1)} %copy-done.6, f32[4]{0:T(128)S(1)} %copy-done.7, s32[4]{0:T(128)S(1)} %pad_add_fusion.info_ref), custom_call_target="tpu_custom_call" | custom-call | tf_op jit(solution)/shard_map/top/pallas_call | solution.py:53
  79.5 5.3 %all-to-all-start.2 = ((f32[8,8,640]{2,1,0:T(8,128)}), f32[8,8,640]{2,1,0:T(8,128)S(1)}, u32[]{:S(2)}, u32[]{:S(2)}) async-start(f32[8,8,640]{2,1,0:T(8,128)} %bitcast.10), calls=%async_computation.2 | async-start | bytes 327680 | tf_op jit(solution)/shard_map/all_to_all | solution.py:845
  84.8 2.7 %own.1.own_ref = f32[2048,128]{1,0:T(8,128)S(1)} custom-call(f32[1536,128]{1,0:T(8,128)} %get-tuple-element.16.fine_hbm, f32[512,128]{1,0:T(8,128)} %get-tuple-element.20.halo_hbm, bf16[512,256]{1,0:T(8,128)(2,1)} %constant.59.clone.z_ref.z_hbm.refs_0_, bf16[256,512]{1,0:T(8,128)(2,1)} %constant.60.clone.y_ref.y_hbm.refs_1_), custom_call_target="tpu_custom_call" | custom-call | tf_op jit(solution)/shard_map/own/pallas_call | solution.py:53
  87.5 6.9 %levels.1 = (f32[768,256]{1,0:T(8,128)S(1)}, f32[144,256]{1,0:T(8,128)S(1)}) custom-call(f32[2048,128]{1,0:T(8,128)S(1)} %own.1.own_ref, f32[376,128]{1,0:T(8,128)S(1)} %collective-permute-done.2.before_ref, f32[376,128]{1,0:T(8,128)S(1)} %collective-permute-done.3.behind_ref, bf16[512,256]{1,0:T(8,128)(2,1)} %constant.59.clone.z_ref.z_hbm.refs_0_, ...), custom_call_target="tpu_custom_call" | custom-call | tf_op jit(solution)/shard_map/levels/pallas_call | solution.py:53
  94.5 2.7 %finish.1 = f32[768,256]{1,0:T(8,128)} custom-call(f32[768,256]{1,0:T(8,128)S(1)} %get-tuple-element.24.near_ref, f32[144,256]{1,0:T(8,128)S(1)} %get-tuple-element.25.mid_ref, f32[64,640]{1,0:T(8,128)S(1)} %bitcast.19, bf16[128,256]{1,0:T(8,128)(2,1)} %constant.69.clone.refs_0_, bf16[16,128]{1,0:T(8,128)(2,1)} %constant.70.clone.refs_1_, ...), custom_call_target="tpu_custom_call" | custom-call | tf_op jit(solution)/shard_map/finish/pallas_call | solution.py:53
  (42 shorter events, 1.8 us)
Async XLA Ops:
  0.7 0.7 copy-start.5
  11.1 11.5 %copy-start.8 = (f32[9,9,9]{2,1,0:T(8,128)S(1)}, f32[9,9,9]{2,1,0:T(8,128)}, u32[]{:S(2)}) copy-start(f32[9,9,9]{2,1,0:T(8,128)} %param.24) | copy-start | bytes 8752
  11.1 11.6 %copy-start.9 = (f32[9,9,9]{2,1,0:T(8,128)S(1)}, f32[9,9,9]{2,1,0:T(8,128)}, u32[]{:S(2)}) copy-start(f32[9,9,9]{2,1,0:T(8,128)} %param.25) | copy-start | bytes 8752
  11.1 12.0 %slice-start = ((f32[9,9,9]{2,1,0:T(8,128)}), f32[9,5,9]{2,1,0:T(8,128)S(1)}, s32[]{:S(2)}) async-start(f32[9,9,9]{2,1,0:T(8,128)} %param.24), calls=%async_computation.3 | async-start | bytes 73728 | tf_op jit(solution)/shard_map/slice | solution.py:542
  11.1 12.1 %slice-start.1 = ((f32[9,9,9]{2,1,0:T(8,128)}), f32[9,5,9]{2,1,0:T(8,128)S(1)}, s32[]{:S(2)}) async-start(f32[9,9,9]{2,1,0:T(8,128)} %param.25), calls=%async_computation.4 | async-start | bytes 73728 | tf_op jit(solution)/shard_map/slice | solution.py:542
  11.1 42.3 %all-to-all-start = ((f32[128,1,4224]{2,1,0:T(1,128)}), f32[128,1,4224]{2,1,0:T(1,128)S(1)}, u32[]{:S(2)}, u32[]{:S(2)}) async-start(f32[128,1,4224]{2,1,0:T(1,128)} %bitcast.21), calls=%async_computation | async-start | bytes 4325376 | tf_op jit(solution)/shard_map/all_to_all | solution.py:816
  23.3 4.0 %copy-start = (bf16[256,512]{1,0:T(8,128)(2,1)S(1)}, bf16[256,512]{1,0:T(8,128)(2,1)}, u32[]{:S(2)}) copy-start(bf16[256,512]{1,0:T(8,128)(2,1)} %constant.60.clone.y_ref.y_hbm.refs_1_) | copy-start | bytes 786436
  23.3 4.0 %copy-start.4 = (bf16[512,256]{1,0:T(8,128)(2,1)S(1)}, bf16[512,256]{1,0:T(8,128)(2,1)}, u32[]{:S(2)}) copy-start(bf16[512,256]{1,0:T(8,128)(2,1)} %constant.61.clone.z_ref.refs_2_) | copy-start | bytes 786436
  27.2 1.8 %copy-start.3 = (bf16[512,256]{1,0:T(8,128)(2,1)S(1)}, bf16[512,256]{1,0:T(8,128)(2,1)}, u32[]{:S(2)}) copy-start(bf16[512,256]{1,0:T(8,128)(2,1)} %constant.59.clone.z_ref.z_hbm.refs_0_) | copy-start | bytes 786436
  28.1 0.8 copy-start.1
  29.8 0.8 copy-start.2
  53.4 24.1 %copy-start.6 = (f32[4]{0:T(128)S(1)}, f32[4]{0:T(128)}, u32[]{:S(2)}) copy-start(f32[4]{0:T(128)} %weights_ref.1) | copy-start | bytes 52
  53.4 24.1 %copy-start.7 = (f32[4]{0:T(128)S(1)}, f32[4]{0:T(128)}, u32[]{:S(2)}) copy-start(f32[4]{0:T(128)} %widths_ref.1) | copy-start | bytes 52
  59.9 17.6 %all-to-all-start.1 = ((f32[16,40,128]{2,1,0:T(8,128)}), f32[16,40,128]{2,1,0:T(8,128)S(1)}, u32[]{:S(2)}, u32[]{:S(2)}) async-start(f32[16,40,128]{2,1,0:T(8,128)} %bitcast.24), calls=%async_computation.1 | async-start | bytes 655360 | tf_op jit(solution)/shard_map/all_to_all | solution.py:835
  63.5 4.1 %collective-permute-start = (f32[376,128]{1,0:T(8,128)}, f32[376,128]{1,0:T(8,128)S(1)}, u32[]{:S(2)}, u32[]{:S(2)}) collective-permute-start(f32[376,128]{1,0:T(8,128)} %get-tuple-element.18), channel_id=1, source_target_pairs={{0,1},{1,2},{2,3},{3,4},{4,5},{5,6},{6,7},{7,0},{8,9},{9,10},{10,1... | collective-permute-start | bytes 577544 | tf_op jit(solution)/shard_map/ppermute | solution.py:804
  64.7 5.6 %collective-permute-start.1 = (f32[376,128]{1,0:T(8,128)}, f32[376,128]{1,0:T(8,128)S(1)}, u32[]{:S(2)}, u32[]{:S(2)}) collective-permute-start(f32[376,128]{1,0:T(8,128)} %get-tuple-element.19), channel_id=1, source_target_pairs={{1,0},{2,1},{3,2},{4,3},{5,4},{6,5},{7,6},{0,7},{9,8},{10,9},{11,1... | collective-permute-start | bytes 577544 | tf_op jit(solution)/shard_map/ppermute | solution.py:804
  72.4 15.1 %collective-permute-start.2 = (f32[376,128]{1,0:T(8,128)}, f32[376,128]{1,0:T(8,128)S(1)}, u32[]{:S(2)}, u32[]{:S(2)}) collective-permute-start(f32[376,128]{1,0:T(8,128)} %get-tuple-element.21), channel_id=1, source_target_pairs={{0,8},{8,16},{16,24},{24,32},{32,40},{40,48},{48,56},{56,64},{64,7... | collective-permute-start | bytes 577544 | tf_op jit(solution)/shard_map/ppermute | solution.py:804
  74.0 13.6 %collective-permute-start.3 = (f32[376,128]{1,0:T(8,128)}, f32[376,128]{1,0:T(8,128)S(1)}, u32[]{:S(2)}, u32[]{:S(2)}) collective-permute-start(f32[376,128]{1,0:T(8,128)} %get-tuple-element.22), channel_id=1, source_target_pairs={{8,0},{16,8},{24,16},{32,24},{40,32},{48,40},{56,48},{64,56},{72,6... | collective-permute-start | bytes 577544 | tf_op jit(solution)/shard_map/ppermute | solution.py:804
  79.5 15.0 %all-to-all-start.2 = ((f32[8,8,640]{2,1,0:T(8,128)}), f32[8,8,640]{2,1,0:T(8,128)S(1)}, u32[]{:S(2)}, u32[]{:S(2)}) async-start(f32[8,8,640]{2,1,0:T(8,128)} %bitcast.10), calls=%async_computation.2 | async-start | bytes 327680 | tf_op jit(solution)/shard_map/all_to_all | solution.py:845

commit v4 on v3

--- a/solution.py
+++ b/solution.py
@@ -7,6 +7,7 @@
 from jax.experimental import pallas as pl
 from jax.experimental.pallas import tpu as pltpu
 from jax.sharding import PartitionSpec as P
+
 
 CX = 32
 CY = 24
@@ -27,7 +28,7 @@
 HB = pl.BlockSpec(memory_space=pltpu.HBM)
 
 
-def call(body, name, out, ins, scratch=(), limit=20, flops=0, moved=0, outs=VM):
+def call(body, out, ins, scratch=(), limit=20, flops=0, moved=0, outs=VM):
     many = isinstance(out, tuple)
     outs = outs if isinstance(outs, tuple) else (outs,) * (len(out) if many else 1)
     shapes = tuple(
@@ -42,7 +43,6 @@
         scratch_shapes=list(scratch),
         compiler_params=pltpu.CompilerParams(vmem_limit_bytes=limit << 20),
         cost_estimate=pl.CostEstimate(flops=flops, bytes_accessed=moved, transcendentals=0),
-        name=name,
     )
 
     def run(*args):
@@ -106,6 +106,7 @@
     owner_s[...] = owner
     code_s[...] = code
     lane_offset = info_ref[1]
+    lane = lax.broadcasted_iota(jnp.int32, (8, 128), 1)
     rows = lax.broadcasted_iota(jnp.int32, (128, 128), 0)
     before = lax.broadcasted_iota(jnp.int32, (128, 256), 0)
     after = lax.broadcasted_iota(jnp.int32, (128, 256), 1)
@@ -121,19 +122,21 @@
         rank = jnp.sum(jnp.where(hit, counted[:, :128] + base, 0.0), axis=0, keepdims=True)
         rank = rank.astype(jnp.int32)
         pos_ref[pl.ds(c, 1), :] = own * ROWS + rank
-        place = jnp.where(rows == rank + lane_offset, 1.0, 0.0).astype(BF16)
-        coarse = jnp.where(hit, (ids >> 4).astype(F32), 0.0)
-        fine = jnp.where(hit, (ids & 15).astype(F32), 0.0)
-        both = jnp.concatenate([coarse, fine], axis=0).astype(BF16)
+        place = rows[:CAP] == rank
+        coarse = jnp.where(place, (ids >> 4).astype(F32), 0.0)
+        fine = jnp.where(place, (ids & 15).astype(F32), 0.0)
+        both = jnp.concatenate([coarse, fine, jnp.zeros((64, 128), F32)], axis=0).astype(BF16)
         acc_s[...] += lax.dot_general(
-            both, place, (((1,), (1,)), ((), ())), preferred_element_type=F32
+            one_hot, both, (((1,), (1,)), ((), ())), preferred_element_type=F32
         )
         return base + counted[:, 128:]
 
     lax.fori_loop(0, tile.shape[0], chunk, jnp.zeros((128, 128), F32), unroll=4)
     (pos_copy,) = started([(pos_ref, pos_s)], sems, 1)
     for b in range(DEVICES // 8):
-        ids = acc_s[b * 8 : b * 8 + 8, :] * 16.0 + acc_s[128 + b * 8 : 136 + b * 8, :]
+        both = acc_s[b * 8 : b * 8 + 8, :]
+        ids = both * 16.0 + pltpu.roll(both, 128 - CAP, 1)
+        ids = pltpu.roll(jnp.where(lane < CAP, ids, 0.0), lane_offset, 1)
         for j in range(8):
             at = (b * 8 + j) * ROWS + CAP
             out_s[at : at + 1, :] = ids[j : j + 1]
@@ -155,7 +158,6 @@
 def send(tile, info, data):
     return call(
         send_kernel,
-        "send",
         array(DEVICES * ROWS, 128),
         [VM, SM, HB],
         [
@@ -165,7 +167,7 @@
             pltpu.SMEM((32, 128), jnp.int32),
             pltpu.VMEM((32, 128), jnp.int32),
             pltpu.VMEM((32, 128), jnp.int32),
-            pltpu.VMEM((256, 128), F32),
+            pltpu.VMEM((128, 128), F32),
             pltpu.SemaphoreType.DMA((3,)),
         ],
         outs=HB,
@@ -255,7 +257,8 @@
             line = in_ref[base + CAP : base + CAP + 1, :]
             total = line if total is None else total + line
         ids_s[c : c + 1, :] = total.astype(jnp.int32)
-    rows = lax.broadcasted_iota(jnp.int32, (256, 128), 0)
+    rows = lax.broadcasted_iota(jnp.int32, (256, 128), 0).astype(F32).astype(BF16)
+    one, zero = jnp.ones((256, 128), BF16), jnp.zeros((256, 128), BF16)
 
     def block(b, carry):
         first = pl.multiple_of(b * 256, 256)
@@ -263,8 +266,9 @@
         for k in range(16):
             parts = []
             for q in range(2):
-                ids = ids_s[2 * k + q : 2 * k + q + 1, :] - first
-                parts.append(jnp.where(rows == ids, 1.0, 0.0).astype(BF16))
+                ids = jnp.clip(ids_s[2 * k + q : 2 * k + q + 1, :] - first, -1, 256)
+                line = jnp.broadcast_to(ids.astype(F32), (16, 128)).astype(BF16)
+                parts.append(jnp.where(rows == jnp.concatenate([line] * 16, axis=0), one, zero))
             acc = acc + mm(jnp.concatenate(parts, axis=1), data_s[k * 256 : (k + 1) * 256, :])
         fine_ref[pl.ds(first, 256), :] = acc[:, :128] + acc[:, 128:]
         return carry
@@ -327,7 +331,6 @@
     )
     return call(
         collect_kernel,
-        "collect",
         out,
         [VM] + [HB] * (4 + len(after)),
         [
@@ -403,7 +406,6 @@
     out = (array(2 * CX * 8, 128), array(24 * YD, 128), array(SEND, 128), array(SEND, 128))
     return call(
         merge_kernel,
-        "merge",
         out,
         [HB, HB, VM, VM],
         [
@@ -548,20 +550,22 @@
     wide = jnp.concatenate([wide] * copies, axis=2)
     wide = jnp.concatenate([wide, jnp.zeros((7, YD, 256), F32)], axis=0)
     return call(
-        functools.partial(taps_kernel, copies),
-        f"taps{copies}",
-        array(27 * YD, 128),
-        [VM] * 3 + [HB],
+        functools.partial(taps_kernel, copies), array(27 * YD, 128), [VM] * 3 + [HB]
     )(wide.reshape(16 * YD, 256), z_matrix, y_matrix, after)
 
 
-def own_kernel(fine_hbm, halo_hbm, z_hbm, y_hbm, out_ref, fine_s, halo_s, z_ref, y_ref, sems):
-    copies = started(
-        [(z_hbm, z_ref), (y_hbm, y_ref), (fine_hbm, fine_s), (halo_hbm, halo_s)], sems
-    )
-    for copy in copies:
-        copy.wait()
+def own_kernel(fine_hbm, halo_hbm, z_ref, y_ref, out_ref, fine_s, halo_s, sems):
+    waits = []
     for p in range(CX // 8):
+        pairs = []
+        for h in range(2):
+            for source, target, rows in ((fine_hbm, fine_s, CY), (halo_hbm, halo_s, 8)):
+                at = pl.ds((h * CX + p * 8) * rows, 8 * rows)
+                pairs.append((source.at[at], target.at[at]))
+        waits.append(started(pairs, sems, p * 4))
+    for p in range(CX // 8):
+        for copy in waits[p]:
+            copy.wait()
         columns = []
         for h in range(2):
             rows = []
@@ -574,50 +578,34 @@
             out_ref[(p * 8 + j) * 64 : (p * 8 + j + 1) * 64, :] = slabs[j]
 
 
-def convolve(copies, block_out, blocks, taps_ref, freq_s, conv_s):
+def convolve(copies, first, count, taps_ref, freq_s, conv_s):
     lane_special, row = special_mask(copies, 8)
-
-    def step(index, carry):
-        v = index % 2
-        first = (index // 2) * block_out
-        sums = [[None] * 4 for _ in range(block_out)]
+    for v in range(2):
+        sums = [[None] * 4 for _ in range(count)]
         for dx in range(9):
             coefs = []
             for half in range(2):
                 at = dx * YD + half * 16 + v * 8
-                coefs.append(
-                    [
-                        taps_ref[pl.ds(pl.multiple_of(at + part * 9 * YD, 8), 8), :]
-                        for part in range(3)
-                    ]
-                )
-            for j in range(block_out):
-                base = (first + j + dx) * 64 + v * 8
+                coefs.append([taps_ref[at + part * 288 : at + part * 288 + 8, :] for part in range(3)])
+            for j in range(count):
+                old = sums[j]
                 for half in range(2):
-                    at = pl.multiple_of(base + half * 16, 8)
-                    re = freq_s[pl.ds(at, 8), :]
-                    im = freq_s[pl.ds(pl.multiple_of(at + 32, 8), 8), :]
+                    at = (first + j + dx) * 64 + v * 8 + half * 16
+                    re = freq_s[at : at + 8, :]
+                    im = freq_s[at + 32 : at + 40, :]
                     a, t, b = coefs[half]
                     new_re = a * re - b * im
                     new_im = b * re + t * im
-                    old = sums[j]
                     old[2 * half] = new_re if dx == 0 else old[2 * half] + new_re
                     old[2 * half + 1] = new_im if dx == 0 else old[2 * half + 1] + new_im
-        special = lane_special & ((row != 0) | (v != 0))
-        for j in range(block_out):
+        special = lane_special & (row != 0) if v == 0 else lane_special
+        for j in range(count):
             ar, ai, br, bi = sums[j]
-            base = (first + j) * 64 + v * 8
-            values = (
-                jnp.where(special, ar - bi, ar),
-                jnp.where(special, ar + bi, br),
-                jnp.where(special, ai + br, ai),
-                jnp.where(special, br - ai, bi),
-            )
-            for part in range(4):
-                conv_s[pl.ds(pl.multiple_of(base + part * 16, 8), 8), :] = values[part]
-        return carry
-
-    lax.fori_loop(0, 2 * blocks, step, 0)
+            at = (first + j) * 64 + v * 8
+            conv_s[at : at + 8, :] = jnp.where(special, ar - bi, ar)
+            conv_s[at + 16 : at + 24, :] = jnp.where(special, ar + bi, br)
+            conv_s[at + 32 : at + 40, :] = jnp.where(special, ai + br, ai)
+            conv_s[at + 48 : at + 56, :] = jnp.where(special, br - ai, bi)
 
 
 def wide_slab(ref, index):
@@ -632,22 +620,20 @@
 def levels_kernel(
     own_ref, before_ref, behind_ref, *refs
 ):
+    zf_ref, yf_ref, mzf_ref, zi_ref, yi_ref, mzi_ref = refs[:6]
     near_ref, mid_ref, freq_s, conv_s, mid_freq_s, mid_conv_s = refs[9:15]
-    zf_ref, yf_ref, mzf_ref, wide_ref, near_taps, zi_ref, yi_ref, mid_taps, mzi_ref = refs[15:24]
-    copies = started(list(zip(refs[:9], refs[15:24])), refs[24])
+    wide_ref, near_taps, mid_taps = refs[15:18]
+    copies = started(list(zip(refs[6:9], refs[15:18])), refs[18])
     freq_s[4 * 64 : 36 * 64, :] = own_ref[...]
     edges = [
         jnp.concatenate([ref[:128, :], ref[128:256, :]], axis=1) for ref in (before_ref, behind_ref)
     ]
-    copies[0].wait()
-    copies[1].wait()
     slabs = forward_chunk(jnp.concatenate(edges, axis=0), zf_ref, yf_ref, 1)
     for j in range(8):
         at = j if j < 4 else 32 + j
         freq_s[at * 64 : (at + 1) * 64, :] = slabs[j]
     zero = jnp.zeros((YD, 128), F32)
-    copies[2].wait()
-    copies[3].wait()
+    copies[0].wait()
     for p in range(3):
         pairs = []
         for j in range(8):
@@ -671,20 +657,18 @@
         for j in range(8):
             at = p * 8 + j
             mid_freq_s[at * 64 : (at + 1) * 64, :] = slabs[j]
-    copies[4].wait()
-    convolve(1, 8, 4, near_taps, freq_s, conv_s)
-    copies[5].wait()
-    copies[6].wait()
+    for copy in copies[1:]:
+        copy.wait()
     for p in range(4):
+        convolve(1, p * 8, 8, near_taps, freq_s, conv_s)
         slabs = [conv_s[(p * 8 + j) * 64 : (p * 8 + j + 1) * 64, :] for j in range(8)]
         space = inverse_chunk(slabs, zi_ref, yi_ref)
         for j in range(8):
             x = p * 8 + j
             near_ref[x * CY : (x + 1) * CY, :] = space[j * YD : j * YD + CY]
-    copies[7].wait()
-    copies[8].wait()
-    convolve(2, 9, 1, mid_taps, mid_freq_s, mid_conv_s)
     mid_conv_s[9 * 64 :, :] = jnp.zeros((7 * 64, 128), F32)
+    for first, count in ((0, 5), (5, 4)):
+        convolve(2, first, count, mid_taps, mid_freq_s, mid_conv_s)
     for p in range(2):
         slabs = [mid_conv_s[(p * 8 + j) * 64 : (p * 8 + j + 1) * 64, :] for j in range(8)]
         space = inverse_chunk(slabs, mzi_ref, yi_ref)
@@ -754,14 +738,10 @@
 def finish_kernel(
     near_ref, mid_ref, top_ref, *refs
 ):
-    out_ref, grown_s = refs[4:6]
-    grow_top_ref, grow_y_ref, grow_z_ref, grow_fine_ref, sems = refs[6:]
-    copies = started(list(zip(refs[:4], refs[6:10])), sems)
+    grow_top_ref, grow_y_ref, grow_z_ref, grow_fine_ref, out_ref, grown_s = refs
     total = top_ref[:8, :]
     for s in range(1, SIZE_Y):
         total = total + top_ref[s * 8 : (s + 1) * 8, :]
-    for copy in copies:
-        copy.wait()
     lanes = []
     for ip in range(5):
         lanes.append(exact_right(total[:, ip * 128 : (ip + 1) * 128], grow_top_ref))
@@ -801,7 +781,9 @@
     count = lax.axis_size(axis)
     forward = [(i, (i + 1) % count) for i in range(count)]
     backward = [(target, source) for source, target in forward]
-    return lax.ppermute(to_high, axis, forward), lax.ppermute(to_low, axis, backward)
+    before = lax.ppermute(to_high, axis, forward)
+    behind = lax.ppermute(to_low, axis, backward)
+    return before, behind
 
 
 def on_device(
@@ -834,10 +816,10 @@
     before, behind = swap(low, high, "gy")
     tops = lax.all_to_all(
         top.reshape(SIZE_X, TOP_ROWS, 128), "gx", split_axis=0, concat_axis=0, tiled=True
-    ).reshape(SIZE_X * TOP_ROWS, 128)
+    )
+    tops = tops.reshape(SIZE_X * TOP_ROWS, 128)
     partial = call(
         top_kernel,
-        "top",
         array(64, 640),
         [VM, SM, SM, SM],
         [pltpu.VMEM((256, 128), F32), pltpu.VMEM((256, 128), F32)],
@@ -849,26 +831,24 @@
     before, behind = swap(low, high, "gx")
     own = call(
         own_kernel,
-        "own",
         array(CX * 64, 128),
-        [HB] * 4,
-        buffers(fine, halo, zf, yf) + [pltpu.SemaphoreType.DMA((4,))],
+        [HB, HB, VM, VM],
+        buffers(fine, halo) + [pltpu.SemaphoreType.DMA((16,))],
     )(fine, halo, zf, yf)
-    tables = (zf, yf, mzf, wide, near_taps, zi, yi, mid_taps, mzi)
+    tables = (wide, near_taps, mid_taps)
     near, mid_near = call(
         levels_kernel,
-        "levels",
         (array(CX * CY, NZ), array(9 * 16, 256)),
-        [VM] * 3 + [HB] * 9,
+        [VM] * 9 + [HB] * 3,
         [
             pltpu.VMEM((40 * 64, 128), F32),
             pltpu.VMEM((32 * 64, 128), F32),
             pltpu.VMEM((24 * 64, 128), F32),
             pltpu.VMEM((16 * 64, 128), F32),
             *buffers(*tables),
-            pltpu.SemaphoreType.DMA((9,)),
+            pltpu.SemaphoreType.DMA((3,)),
         ],
-    )(own, before, behind, *tables)
+    )(own, before, behind, zf, yf, mzf, zi, yi, mzi, *tables)
     grow_z = grow_matrix(2 * 64, 65)
     grow_z[:, 0] += grow_z[:, 64]
     grow_fine_z = grow_matrix(2 * 128, 129)
@@ -880,11 +860,7 @@
         plain(np.kron(np.eye(8), padded(grow_matrix(CY, 13), CY, 16))),
     )
     out = call(
-        finish_kernel,
-        "finish",
-        array(CX * CY, NZ),
-        [VM] * 3 + [HB] * 4,
-        [pltpu.VMEM((24 * CY, NZ), F32), *buffers(*tables), pltpu.SemaphoreType.DMA((4,))],
+        finish_kernel, array(CX * CY, NZ), [VM] * 7, [pltpu.VMEM((24 * CY, NZ), F32)]
     )(near, mid_near, partial, *tables)
     return out.reshape(CX, CY, NZ)
 

time: 97.8 us -> 97.8 us (level)
    unnamed x20 -> x34, local copies, waits for them, and re-layouts: 2.31 us -> 2.33 us
where the time goes in v4:
time: 97.8 us; the launch traced here: 97.3 us
  Pallas kernels  34.3 us (35%)
  waiting for transfers between devices  28.2 us (29%)
  starting transfers between devices  26.9 us (28%)
  local copies, waits for them, and re-layouts  5.71 us (6%)
  other arithmetic  1.19 us (1%)
  between operations  1.05 us (1%)
    pallas_call x9, Pallas kernels, run(): return kernel(*placed)  34.3 us
    all_to_all x1, waiting for transfers between devices, on_device(): lax.all_to_all(outgoing.reshape(DEVICES, 1, ROWS * 128), ('gx', 'gy'), sp...  22.8 us
    all_to_all x1, starting transfers between devices, on_device(): lax.all_to_all(outgoing.reshape(DEVICES, 1, ROWS * 128), ('gx', 'gy'), sp...  11.5 us
    all_to_all x1, starting transfers between devices, on_device(): lax.all_to_all(partial.reshape(SIZE_Y, 8, 640), 'gy', split_axis=0, conca...  5.31 us
    ppermute x2, starting transfers between devices, swap(): behind = lax.ppermute(to_low, axis, backward)  3.68 us
    all_to_all x1, starting transfers between devices, on_device(): lax.all_to_all(top.reshape(SIZE_X, TOP_ROWS, 128), 'gx', split_axis=0, co...  3.59 us
    ppermute x2, starting transfers between devices, swap(): before = lax.ppermute(to_high, axis, forward)  2.78 us
    ppermute x2, waiting for transfers between devices, swap(): before = lax.ppermute(to_high, axis, forward)  2.7 us
  transfers between devices with their start and end apart: 7, of which 3 were waited for; matrix products, arithmetic and copies ran while one was open for 5% of the time, Pallas kernels for 16%

profile of v4, /device:TPU:1, one launch (start us, length us, event | category | flops | bytes accessed | tf_op | source)
XLA Modules:
  0.0 97.3 jit_solution(2037851273521028386)
XLA Ops:
  1.5 10.4 %shard_map.199.after_ref = f32[4224,128]{1,0:T(8,128)} custom-call(s32[32,128]{1,0:T(8,128)S(1)} %bitcast.20, s32[4]{0:T(128)S(1)} %pad_add_fusion.info_ref, f32[4096,128]{1,0:T(8,128)} %data_ref.1), custom_call_target="tpu_custom_call" | custom-call | tf_op jit(solution)/shard_map/pallas_call | solution.py:53
  11.9 11.5 %all-to-all-start = ((f32[128,1,4224]{2,1,0:T(1,128)}), f32[128,1,4224]{2,1,0:T(1,128)S(1)}, u32[]{:S(2)}, u32[]{:S(2)}) async-start(f32[128,1,4224]{2,1,0:T(1,128)} %bitcast.21), calls=%async_computation | async-start | bytes 4325376 | tf_op jit(solution)/shard_map/all_to_all | solution.py:798
  24.2 0.8 slice.49
  24.9 0.8 slice.51
  25.7 1.2 %concatenate.25 = f32[9,32,256]{2,1,0:T(8,128)S(1)} concatenate(f32[9,32,5]{2,1,0:T(8,128)} %slice.51, f32[9,32,119]{2,1,0:T(8,128)S(1)} %broadcast_in_dim.7, f32[9,32,9]{2,1,0:T(8,128)S(1)} %get-tuple-element.27, f32[9,32,119]{2,1,0:T(8,128)S(1)} %broadcast_in_dim.7, f32[9,32,4]{2,1,0:T(8,128)S(1)} %bitcast.22), dimensions={2} | concatenate | bytes 589824 | tf_op jit(solution)/shard_map/concatenate | solution.py:550
  26.9 1.0 %pad_maximum_fusion = f32[9,32,256]{2,1,0:T(8,128)S(1)} fusion(f32[9,32,4]{2,1,0:T(8,128)S(1)} %bitcast.23, f32[9,32,5]{2,1,0:T(8,128)} %slice.49, f32[256]{0:T(256)S(1)} %pad.6.clone), kind=kLoop, calls=%fused_computation | loop fusion | flops 147456 | bytes 306304 | tf_op jit(solution)/shard_map/concatenate | solution.py:547
  28.0 0.9 shard_map.201.refs_5_.refs_8_
  28.9 0.8 copy-done.1
  29.7 0.9 shard_map.200.refs_4_.refs_7_
  30.6 0.8 copy-done.2
  31.4 22.8 %all-to-all-done = f32[128,1,4224]{2,1,0:T(1,128)S(1)} async-done(((f32[128,1,4224]{2,1,0:T(1,128)}), f32[128,1,4224]{2,1,0:T(1,128)S(1)}, u32[]{:S(2)}, u32[]{:S(2)}) %all-to-all-start) | async-done | bytes 2162720 | tf_op jit(solution)/shard_map/all_to_all | solution.py:798
  54.2 6.5 %shard_map.202 = (f32[1536,128]{1,0:T(8,128)}, f32[384,128]{1,0:T(8,128)}, f32[376,128]{1,0:T(8,128)}, f32[376,128]{1,0:T(8,128)}, f32[640,128]{1,0:T(8,128)}) custom-call(f32[4224,128]{1,0:T(8,128)S(1)} %bitcast.15, bf16[256,128]{1,0:T(8,128)(2,1)} %constant.62.clone.refs_0_, bf16[128,192]{1,0:T(8,128)(2,1)} %constant.63.clone.refs_1_, ...), custom_call_target="tpu_custom_call" | custom-call | tf_op jit(solution)/shard_map/pallas_call | solution.py:53
  60.7 3.6 %all-to-all-start.1 = ((f32[16,40,128]{2,1,0:T(8,128)}), f32[16,40,128]{2,1,0:T(8,128)S(1)}, u32[]{:S(2)}, u32[]{:S(2)}) async-start(f32[16,40,128]{2,1,0:T(8,128)} %bitcast.24), calls=%async_computation.1 | async-start | bytes 655360 | tf_op jit(solution)/shard_map/all_to_all | solution.py:817
  64.3 1.2 %collective-permute-start = (f32[376,128]{1,0:T(8,128)}, f32[376,128]{1,0:T(8,128)S(1)}, u32[]{:S(2)}, u32[]{:S(2)}) collective-permute-start(f32[376,128]{1,0:T(8,128)} %get-tuple-element.18), channel_id=1, source_target_pairs={{0,1},{1,2},{2,3},{3,4},{4,5},{5,6},{6,7},{7,0},{8,9},{9,10},{10,1... | collective-permute-start | bytes 577544 | tf_op jit(solution)/shard_map/ppermute | solution.py:784
  65.7 2.7 %collective-permute-done.before_ref = f32[376,128]{1,0:T(8,128)S(1)} collective-permute-done((f32[376,128]{1,0:T(8,128)}, f32[376,128]{1,0:T(8,128)S(1)}, u32[]{:S(2)}, u32[]{:S(2)}) %collective-permute-start) | collective-permute-done | bytes 192544 | tf_op jit(solution)/shard_map/ppermute | solution.py:784
  68.4 2.7 %collective-permute-done.1.behind_ref = f32[376,128]{1,0:T(8,128)S(1)} collective-permute-done((f32[376,128]{1,0:T(8,128)}, f32[376,128]{1,0:T(8,128)S(1)}, u32[]{:S(2)}, u32[]{:S(2)}) %collective-permute-start.1) | collective-permute-done | bytes 192544 | tf_op jit(solution)/shard_map/ppermute | solution.py:785
  71.1 2.2 %shard_map.203 = (f32[512,128]{1,0:T(8,128)}, f32[768,128]{1,0:T(8,128)}, f32[376,128]{1,0:T(8,128)}, f32[376,128]{1,0:T(8,128)}) custom-call(f32[1536,128]{1,0:T(8,128)} %get-tuple-element.16.fine_hbm, f32[384,128]{1,0:T(8,128)} %get-tuple-element.17.mid_hbm, f32[376,128]{1,0:T(8,128)S(1)} %collective-permute-done.before_ref, ...), custom_call_target="tpu_custom_call" | custom-call | tf_op jit(solution)/shard_map/pallas_call | solution.py:53
  73.3 1.6 %collective-permute-start.2 = (f32[376,128]{1,0:T(8,128)}, f32[376,128]{1,0:T(8,128)S(1)}, u32[]{:S(2)}, u32[]{:S(2)}) collective-permute-start(f32[376,128]{1,0:T(8,128)} %get-tuple-element.21), channel_id=1, source_target_pairs={{0,8},{8,16},{16,24},{24,32},{32,40},{40,48},{48,56},{56,64},{64,7... | collective-permute-start | bytes 577544 | tf_op jit(solution)/shard_map/ppermute | solution.py:784
  74.9 3.5 %collective-permute-start.3 = (f32[376,128]{1,0:T(8,128)}, f32[376,128]{1,0:T(8,128)S(1)}, u32[]{:S(2)}, u32[]{:S(2)}) collective-permute-start(f32[376,128]{1,0:T(8,128)} %get-tuple-element.22), channel_id=1, source_target_pairs={{8,0},{16,8},{24,16},{32,24},{40,32},{48,40},{56,48},{64,56},{72,6... | collective-permute-start | bytes 577544 | tf_op jit(solution)/shard_map/ppermute | solution.py:785
  78.4 2.0 %shard_map.206 = f32[64,640]{1,0:T(8,128)} custom-call(f32[640,128]{1,0:T(8,128)S(1)} %bitcast.18, f32[4]{0:T(128)S(1)} %copy-done.13, f32[4]{0:T(128)S(1)} %copy-done.14, s32[4]{0:T(128)S(1)} %pad_add_fusion.info_ref), custom_call_target="tpu_custom_call" | custom-call | tf_op jit(solution)/shard_map/pallas_call | solution.py:53
  80.4 5.3 %all-to-all-start.2 = ((f32[8,8,640]{2,1,0:T(8,128)}), f32[8,8,640]{2,1,0:T(8,128)S(1)}, u32[]{:S(2)}, u32[]{:S(2)}) async-start(f32[8,8,640]{2,1,0:T(8,128)} %bitcast.10), calls=%async_computation.2 | async-start | bytes 327680 | tf_op jit(solution)/shard_map/all_to_all | solution.py:827
  85.7 3.8 %shard_map.204.own_ref = f32[2048,128]{1,0:T(8,128)S(1)} custom-call(f32[1536,128]{1,0:T(8,128)} %get-tuple-element.16.fine_hbm, f32[512,128]{1,0:T(8,128)} %get-tuple-element.20.halo_hbm, bf16[512,256]{1,0:T(8,128)(2,1)S(1)} %copy-done.3, bf16[256,512]{1,0:T(8,128)(2,1)S(1)} %copy-done), custom_call_target="tpu_custom_call" | custom-call | tf_op jit(solution)/shard_map/pallas_call | solution.py:53
  89.7 5.8 %shard_map.205 = (f32[768,256]{1,0:T(8,128)S(1)}, f32[144,256]{1,0:T(8,128)S(1)}) custom-call(f32[2048,128]{1,0:T(8,128)S(1)} %shard_map.204.own_ref, f32[376,128]{1,0:T(8,128)S(1)} %collective-permute-done.2.before_ref, f32[376,128]{1,0:T(8,128)S(1)} %collective-permute-done.3.behind_ref, bf16[512,256]{1,0:T(8,128)(2,1)S(1)} %copy-done.3, ...), custom_call_target="tpu_custom_call" | custom-call | tf_op jit(solution)/shard_map/pallas_call | solution.py:53
  95.5 1.8 %shard_map.207 = f32[768,256]{1,0:T(8,128)} custom-call(f32[768,256]{1,0:T(8,128)S(1)} %get-tuple-element.24.near_ref, f32[144,256]{1,0:T(8,128)S(1)} %get-tuple-element.25.mid_ref, f32[64,640]{1,0:T(8,128)S(1)} %bitcast.19, bf16[128,256]{1,0:T(8,128)(2,1)S(1)} %copy-done.9, bf16[16,128]{1,0:T(8,128)(2,1)S(1)} %copy-done.12, bf16[128,256]{1,0:T(8,128)(2,1)S(1)} %copy-done.8, ...), custom_call_target="tpu_custom_call" | custom-call | tf_op jit(solution)/shard_map/pallas_call | solution.py:53
  (56 shorter events, 1.8 us)
Async XLA Ops:
  11.8 11.5 %copy-start.15 = (f32[9,9,9]{2,1,0:T(8,128)S(1)}, f32[9,9,9]{2,1,0:T(8,128)}, u32[]{:S(2)}) copy-start(f32[9,9,9]{2,1,0:T(8,128)} %param.24) | copy-start | bytes 8752
  11.9 11.6 %copy-start.16 = (f32[9,9,9]{2,1,0:T(8,128)S(1)}, f32[9,9,9]{2,1,0:T(8,128)}, u32[]{:S(2)}) copy-start(f32[9,9,9]{2,1,0:T(8,128)} %param.25) | copy-start | bytes 8752
  11.9 12.0 %slice-start = ((f32[9,9,9]{2,1,0:T(8,128)}), f32[9,5,9]{2,1,0:T(8,128)S(1)}, s32[]{:S(2)}) async-start(f32[9,9,9]{2,1,0:T(8,128)} %param.24), calls=%async_computation.3 | async-start | bytes 73728 | tf_op jit(solution)/shard_map/slice | solution.py:544
  11.9 12.1 %slice-start.1 = ((f32[9,9,9]{2,1,0:T(8,128)}), f32[9,5,9]{2,1,0:T(8,128)S(1)}, s32[]{:S(2)}) async-start(f32[9,9,9]{2,1,0:T(8,128)} %param.25), calls=%async_computation.4 | async-start | bytes 73728 | tf_op jit(solution)/shard_map/slice | solution.py:544
  11.9 42.3 %all-to-all-start = ((f32[128,1,4224]{2,1,0:T(1,128)}), f32[128,1,4224]{2,1,0:T(1,128)S(1)}, u32[]{:S(2)}, u32[]{:S(2)}) async-start(f32[128,1,4224]{2,1,0:T(1,128)} %bitcast.21), calls=%async_computation | async-start | bytes 4325376 | tf_op jit(solution)/shard_map/all_to_all | solution.py:798
  24.1 4.0 %copy-start = (bf16[256,512]{1,0:T(8,128)(2,1)S(1)}, bf16[256,512]{1,0:T(8,128)(2,1)}, u32[]{:S(2)}) copy-start(bf16[256,512]{1,0:T(8,128)(2,1)} %constant.60.clone.y_ref.refs_1_) | copy-start | bytes 786436
  24.1 4.0 %copy-start.4 = (bf16[512,256]{1,0:T(8,128)(2,1)S(1)}, bf16[512,256]{1,0:T(8,128)(2,1)}, u32[]{:S(2)}) copy-start(bf16[512,256]{1,0:T(8,128)(2,1)} %constant.61.clone.z_ref.refs_2_) | copy-start | bytes 786436
  28.0 1.7 %copy-start.3 = (bf16[512,256]{1,0:T(8,128)(2,1)S(1)}, bf16[512,256]{1,0:T(8,128)(2,1)}, u32[]{:S(2)}) copy-start(bf16[512,256]{1,0:T(8,128)(2,1)} %constant.59.clone.z_ref.refs_0_) | copy-start | bytes 786436
  30.6 0.8 copy-start.2
  54.2 24.2 %copy-start.13 = (f32[4]{0:T(128)S(1)}, f32[4]{0:T(128)}, u32[]{:S(2)}) copy-start(f32[4]{0:T(128)} %weights_ref.1) | copy-start | bytes 52
  54.2 24.2 %copy-start.14 = (f32[4]{0:T(128)S(1)}, f32[4]{0:T(128)}, u32[]{:S(2)}) copy-start(f32[4]{0:T(128)} %widths_ref.1) | copy-start | bytes 52
  60.7 17.6 %all-to-all-start.1 = ((f32[16,40,128]{2,1,0:T(8,128)}), f32[16,40,128]{2,1,0:T(8,128)S(1)}, u32[]{:S(2)}, u32[]{:S(2)}) async-start(f32[16,40,128]{2,1,0:T(8,128)} %bitcast.24), calls=%async_computation.1 | async-start | bytes 655360 | tf_op jit(solution)/shard_map/all_to_all | solution.py:817
  64.3 4.1 %collective-permute-start = (f32[376,128]{1,0:T(8,128)}, f32[376,128]{1,0:T(8,128)S(1)}, u32[]{:S(2)}, u32[]{:S(2)}) collective-permute-start(f32[376,128]{1,0:T(8,128)} %get-tuple-element.18), channel_id=1, source_target_pairs={{0,1},{1,2},{2,3},{3,4},{4,5},{5,6},{6,7},{7,0},{8,9},{9,10},{10,1... | collective-permute-start | bytes 577544 | tf_op jit(solution)/shard_map/ppermute | solution.py:784
  65.5 5.6 %collective-permute-start.1 = (f32[376,128]{1,0:T(8,128)}, f32[376,128]{1,0:T(8,128)S(1)}, u32[]{:S(2)}, u32[]{:S(2)}) collective-permute-start(f32[376,128]{1,0:T(8,128)} %get-tuple-element.19), channel_id=1, source_target_pairs={{1,0},{2,1},{3,2},{4,3},{5,4},{6,5},{7,6},{0,7},{9,8},{10,9},{11,1... | collective-permute-start | bytes 577544 | tf_op jit(solution)/shard_map/ppermute | solution.py:785
  71.1 18.6 %copy-start.5 = (bf16[512,256]{1,0:T(8,128)(2,1)S(1)}, bf16[512,256]{1,0:T(8,128)(2,1)}, u32[]{:S(2)}) copy-start(bf16[512,256]{1,0:T(8,128)(2,1)} %constant.68.clone.refs_5_) | copy-start | bytes 786436
  71.1 18.6 %copy-start.6 = (bf16[256,512]{1,0:T(8,128)(2,1)S(1)}, bf16[256,512]{1,0:T(8,128)(2,1)}, u32[]{:S(2)}) copy-start(bf16[256,512]{1,0:T(8,128)(2,1)} %constant.67.clone.refs_4_) | copy-start | bytes 786436
  71.1 18.6 %copy-start.7 = (bf16[512,256]{1,0:T(8,128)(2,1)S(1)}, bf16[512,256]{1,0:T(8,128)(2,1)}, u32[]{:S(2)}) copy-start(bf16[512,256]{1,0:T(8,128)(2,1)} %constant.66.clone.refs_3_) | copy-start | bytes 786436
  73.3 16.3 %collective-permute-start.2 = (f32[376,128]{1,0:T(8,128)}, f32[376,128]{1,0:T(8,128)S(1)}, u32[]{:S(2)}, u32[]{:S(2)}) collective-permute-start(f32[376,128]{1,0:T(8,128)} %get-tuple-element.21), channel_id=1, source_target_pairs={{0,8},{8,16},{16,24},{24,32},{32,40},{40,48},{48,56},{56,64},{64,7... | collective-permute-start | bytes 577544 | tf_op jit(solution)/shard_map/ppermute | solution.py:784
  74.9 14.8 %collective-permute-start.3 = (f32[376,128]{1,0:T(8,128)}, f32[376,128]{1,0:T(8,128)S(1)}, u32[]{:S(2)}, u32[]{:S(2)}) collective-permute-start(f32[376,128]{1,0:T(8,128)} %get-tuple-element.22), channel_id=1, source_target_pairs={{8,0},{16,8},{24,16},{32,24},{40,32},{48,40},{56,48},{64,56},{72,6... | collective-permute-start | bytes 577544 | tf_op jit(solution)/shard_map/ppermute | solution.py:785
  80.4 15.0 %all-to-all-start.2 = ((f32[8,8,640]{2,1,0:T(8,128)}), f32[8,8,640]{2,1,0:T(8,128)S(1)}, u32[]{:S(2)}, u32[]{:S(2)}) async-start(f32[8,8,640]{2,1,0:T(8,128)} %bitcast.10), calls=%async_computation.2 | async-start | bytes 327680 | tf_op jit(solution)/shard_map/all_to_all | solution.py:827
  89.6 5.9 %copy-start.8 = (bf16[128,256]{1,0:T(8,128)(2,1)S(1)}, bf16[128,256]{1,0:T(8,128)(2,1)}, u32[]{:S(2)}) copy-start(bf16[128,256]{1,0:T(8,128)(2,1)} %constant.71.clone.refs_2_) | copy-start | bytes 196612
  89.6 5.9 %copy-start.9 = (bf16[128,256]{1,0:T(8,128)(2,1)S(1)}, bf16[128,256]{1,0:T(8,128)(2,1)}, u32[]{:S(2)}) copy-start(bf16[128,256]{1,0:T(8,128)(2,1)} %constant.69.clone.refs_0_) | copy-start | bytes 196612
  89.6 5.9 %copy-start.10 = (bf16[192,128]{1,0:T(8,128)(2,1)S(1)}, bf16[192,128]{1,0:T(8,128)(2,1)}, u32[]{:S(2)}) copy-start(bf16[192,128]{1,0:T(8,128)(2,1)} %constant.72.clone.refs_3_) | copy-start | bytes 147460
  89.6 5.9 %copy-start.12 = (bf16[16,128]{1,0:T(8,128)(2,1)S(1)}, bf16[16,128]{1,0:T(8,128)(2,1)}, u32[]{:S(2)}) copy-start(bf16[16,128]{1,0:T(8,128)(2,1)} %constant.70.clone.refs_1_) | copy-start | bytes 12292
  (2 other events, 1.5 us)

commit v5 on v4

--- a/solution.py
+++ b/solution.py
@@ -28,7 +28,7 @@
 HB = pl.BlockSpec(memory_space=pltpu.HBM)
 
 
-def call(body, out, ins, scratch=(), limit=20, flops=0, moved=0, outs=VM):
+def call(body, out, ins, scratch=(), limit=10, flops=0, moved=0, outs=VM):
     many = isinstance(out, tuple)
     outs = outs if isinstance(outs, tuple) else (outs,) * (len(out) if many else 1)
     shapes = tuple(
@@ -88,7 +88,8 @@
 
 
 def send_kernel(
-    tile_ref, info_ref, data_ref, out_ref, data_s, out_s, pos_ref, pos_s, owner_s, code_s, acc_s, sems
+    tile_ref, info_ref, data_ref, out_ref,
+    data_s, out_s, hit_s, count_s, place_s, source_s, source_smem, sems,
 ):
     (data_copy,) = started([(data_ref, data_s)], sems)
     tile = tile_ref[...]
@@ -103,56 +104,57 @@
         jnp.int32, tile.shape, 1
     )
     code = jnp.where(slot < info_ref[0], cell, DEAD)
-    owner_s[...] = owner
-    code_s[...] = code
-    lane_offset = info_ref[1]
-    lane = lax.broadcasted_iota(jnp.int32, (8, 128), 1)
     rows = lax.broadcasted_iota(jnp.int32, (128, 128), 0)
     before = lax.broadcasted_iota(jnp.int32, (128, 256), 0)
     after = lax.broadcasted_iota(jnp.int32, (128, 256), 1)
     prefix = jnp.where((before < after) | (after >= 128), 1.0, 0.0).astype(BF16)
-    acc_s[...] = jnp.zeros_like(acc_s)
-
-    def chunk(c, base):
-        own = owner_s[pl.ds(c, 1), :]
-        ids = code_s[pl.ds(c, 1), :]
-        hit = rows == own
-        one_hot = jnp.where(hit, 1.0, 0.0).astype(BF16)
-        counted = mm(one_hot, prefix)
-        rank = jnp.sum(jnp.where(hit, counted[:, :128] + base, 0.0), axis=0, keepdims=True)
-        rank = rank.astype(jnp.int32)
-        pos_ref[pl.ds(c, 1), :] = own * ROWS + rank
-        place = rows[:CAP] == rank
-        coarse = jnp.where(place, (ids >> 4).astype(F32), 0.0)
-        fine = jnp.where(place, (ids & 15).astype(F32), 0.0)
-        both = jnp.concatenate([coarse, fine, jnp.zeros((64, 128), F32)], axis=0).astype(BF16)
-        acc_s[...] += lax.dot_general(
-            one_hot, both, (((1,), (1,)), ((), ())), preferred_element_type=F32
-        )
-        return base + counted[:, 128:]
-
-    lax.fori_loop(0, tile.shape[0], chunk, jnp.zeros((128, 128), F32), unroll=4)
-    (pos_copy,) = started([(pos_ref, pos_s)], sems, 1)
-    for b in range(DEVICES // 8):
-        both = acc_s[b * 8 : b * 8 + 8, :]
-        ids = both * 16.0 + pltpu.roll(both, 128 - CAP, 1)
-        ids = pltpu.roll(jnp.where(lane < CAP, ids, 0.0), lane_offset, 1)
-        for j in range(8):
-            at = (b * 8 + j) * ROWS + CAP
-            out_s[at : at + 1, :] = ids[j : j + 1]
-    pos_copy.wait()
+    for c in range(32):
+        hit = jnp.where(rows == owner[c : c + 1], 1.0, 0.0)
+        hit_s[:, c * 128 : (c + 1) * 128] = hit.astype(BF16)
+    for g in range(8):
+        chunks = [hit_s[:, c * 128 : (c + 1) * 128] for c in range(g * 4, g * 4 + 4)]
+        count_s[g * 512 : (g + 1) * 512, :] = mm(jnp.concatenate(chunks, axis=0), prefix)
+    base = jnp.zeros((128, 128), F32)
+    lane = lax.broadcasted_iota(jnp.int32, (1, 128), 1)
+    for c in range(32):
+        counted = count_s[c * 128 : (c + 1) * 128, :128] + base
+        base = base + count_s[c * 128 : (c + 1) * 128, 128:]
+        hit = rows == owner[c : c + 1]
+        rank = jnp.sum(jnp.where(hit, counted, 0.0), axis=0, keepdims=True)
+        place = rows[:CAP] == rank.astype(jnp.int32)
+        ids = code[c : c + 1]
+        values = (ids >> 4, ids & 15, c * 2 + (lane >> 6), lane & 63)
+        both = [jnp.where(place, value.astype(F32), 0.0) for value in values]
+        place_s[:, c * 128 : (c + 1) * 128] = jnp.concatenate(both, axis=0).astype(BF16)
+    found = lax.dot_general(
+        hit_s[...], place_s[...], (((1,), (1,)), ((), ())), preferred_element_type=F32
+    )
+    source = found * 64.0 + pltpu.roll(found, 128 - CAP, 1)
+    source_s[...] = pltpu.roll(source, 64, 1).astype(jnp.int32)
+    (source_copy,) = started([(source_s, source_smem)], sems, 1)
+    lane = lax.broadcasted_iota(jnp.int32, (128, 128), 1)
+    ids = jnp.where(lane < CAP, found * 16.0 + pltpu.roll(found, 128 - CAP, 1), 0.0)
+    ids = pltpu.roll(ids, info_ref[1], 1)
+    for d in range(DEVICES):
+        at = d * ROWS + CAP
+        out_s[at : at + 1, :] = ids[d : d + 1]
+    source_copy.wait()
     data_copy.wait()
-
-    def body(c, carry):
-        for g in range(16):
-            block = data_s[pl.ds(pl.multiple_of(c * 128 + g * 8, 8), 8), :]
-            for j in range(8):
-                out_s[pl.ds(pos_s[c, g * 8 + j], 1), :] = block[j : j + 1]
-        return carry
-
-    lax.fori_loop(0, 32, body, 0)
-    (out_copy,) = started([(out_s, out_ref)], sems, 2)
-    out_copy.wait()
+    copies = []
+    for part in range(4):
+
+        def body(n, carry):
+            for q in range(4):
+                d = part * 32 + n * 4 + q
+                for r in range(CAP):
+                    out_s[pl.ds(d * ROWS + r, 1), :] = data_s[pl.ds(source_smem[d, r], 1), :]
+            return carry
+
+        lax.fori_loop(0, 8, body, 0)
+        at = pl.ds(part * 32 * ROWS, 32 * ROWS)
+        copies += started([(out_s.at[at], out_ref.at[at])], sems, 2 + part)
+    for copy in copies:
+        copy.wait()
 
 
 def send(tile, info, data):
@@ -163,14 +165,15 @@
         [
             pltpu.VMEM((4096, 128), F32),
             pltpu.VMEM((DEVICES * ROWS, 128), F32),
-            pltpu.VMEM((32, 128), jnp.int32),
-            pltpu.SMEM((32, 128), jnp.int32),
-            pltpu.VMEM((32, 128), jnp.int32),
-            pltpu.VMEM((32, 128), jnp.int32),
-            pltpu.VMEM((128, 128), F32),
-            pltpu.SemaphoreType.DMA((3,)),
+            pltpu.VMEM((128, 4096), BF16),
+            pltpu.VMEM((4096, 256), F32),
+            pltpu.VMEM((128, 4096), BF16),
+            pltpu.VMEM((128, 128), jnp.int32),
+            pltpu.SMEM((128, 128), jnp.int32),
+            pltpu.SemaphoreType.DMA((6,)),
         ],
         outs=HB,
+        limit=20,
     )(tile, info, data)
 
 
@@ -229,14 +232,16 @@
     return matrix
 
 
-def exact_left(matrix_ref, value):
+def exact_left(matrix, value):
+    matrix = matrix[...]
     top, rest = halves(value)
-    return mm(matrix_ref[...], top) + mm(matrix_ref[...], rest)
-
-
-def exact_right(value, matrix_ref):
+    return mm(matrix, top) + mm(matrix, rest)
+
+
+def exact_right(value, matrix):
+    matrix = matrix[...]
     top, rest = halves(value)
-    return mm(top, matrix_ref[...]) + mm(rest, matrix_ref[...])
+    return mm(top, matrix) + mm(rest, matrix)
 
 
 def collect_kernel(in_ref, *refs):
@@ -342,6 +347,7 @@
             pltpu.SemaphoreType.DMA((9,)),
         ],
         outs=HB,
+        limit=20,
     )(arrived, *tables, *after)
 
 
@@ -555,17 +561,9 @@
 
 
 def own_kernel(fine_hbm, halo_hbm, z_ref, y_ref, out_ref, fine_s, halo_s, sems):
-    waits = []
+    for copy in started([(fine_hbm, fine_s), (halo_hbm, halo_s)], sems):
+        copy.wait()
     for p in range(CX // 8):
-        pairs = []
-        for h in range(2):
-            for source, target, rows in ((fine_hbm, fine_s, CY), (halo_hbm, halo_s, 8)):
-                at = pl.ds((h * CX + p * 8) * rows, 8 * rows)
-                pairs.append((source.at[at], target.at[at]))
-        waits.append(started(pairs, sems, p * 4))
-    for p in range(CX // 8):
-        for copy in waits[p]:
-            copy.wait()
         columns = []
         for h in range(2):
             rows = []
@@ -620,10 +618,10 @@
 def levels_kernel(
     own_ref, before_ref, behind_ref, *refs
 ):
-    zf_ref, yf_ref, mzf_ref, zi_ref, yi_ref, mzi_ref = refs[:6]
-    near_ref, mid_ref, freq_s, conv_s, mid_freq_s, mid_conv_s = refs[9:15]
-    wide_ref, near_taps, mid_taps = refs[15:18]
-    copies = started(list(zip(refs[6:9], refs[15:18])), refs[18])
+    zf_ref, yf_ref = refs[:2]
+    near_ref, mid_ref, grow_ref, freq_s, conv_s, mid_freq_s, mid_conv_s = refs[10:17]
+    wide_ref, mzf_ref, near_taps, mid_taps, zi_ref, yi_ref, mzi_ref, sems = refs[17:]
+    copies = started(list(zip(refs[2:10], (*refs[17:24], grow_ref))), sems)
     freq_s[4 * 64 : 36 * 64, :] = own_ref[...]
     edges = [
         jnp.concatenate([ref[:128, :], ref[128:256, :]], axis=1) for ref in (before_ref, behind_ref)
@@ -634,6 +632,7 @@
         freq_s[at * 64 : (at + 1) * 64, :] = slabs[j]
     zero = jnp.zeros((YD, 128), F32)
     copies[0].wait()
+    copies[1].wait()
     for p in range(3):
         pairs = []
         for j in range(8):
@@ -657,7 +656,7 @@
         for j in range(8):
             at = p * 8 + j
             mid_freq_s[at * 64 : (at + 1) * 64, :] = slabs[j]
-    for copy in copies[1:]:
+    for copy in copies[2:]:
         copy.wait()
     for p in range(4):
         convolve(1, p * 8, 8, near_taps, freq_s, conv_s)
@@ -683,17 +682,41 @@
     return jnp.exp(-(distance * distance) / (width * width))
 
 
-def top_kernel(in_ref, weights_ref, widths_ref, info_ref, out_ref, plane_s, depth_s):
+def gauss_kernel(weights_ref, widths_ref, info_ref, after_ref, x_ref, y_ref, z_ref):
     first_x = info_ref[2] * 8
     first_y = info_ref[3] * 6
     row = lax.broadcasted_iota(jnp.int32, (16, 256), 0)
     column = lax.broadcasted_iota(jnp.int32, (16, 256), 1)
     source = jnp.where(column < 128, column, (column - 128) * 8 + 8)
     offset = (first_x + row - source) & 127
-    parts = [
-        jnp.where(column < 144, gauss(offset, 128, widths_ref[k]), 0.0) for k in range(4)
-    ]
-    left = halves(jnp.concatenate(parts, axis=0))
+    for k in range(4):
+        value = jnp.where(column < 144, gauss(offset, 128, widths_ref[k]), 0.0)
+        for n, part in enumerate(halves(value)):
+            x_ref[n * 64 + k * 16 : n * 64 + (k + 1) * 16, :] = part
+    row = lax.broadcasted_iota(jnp.int32, (128, 128), 0)
+    column = lax.broadcasted_iota(jnp.int32, (128, 128), 1)
+    for k in range(4):
+        value = gauss((row - column) & 63, 64, widths_ref[k]) * weights_ref[k]
+        value = jnp.where((row >> 6) == (column >> 6), value, 0.0)
+        for n, part in enumerate(halves(value)):
+            z_ref[(n * 4 + k) * 128 : (n * 4 + k + 1) * 128, :] = part
+    row = lax.broadcasted_iota(jnp.int32, (64, 128), 0)
+    column = lax.broadcasted_iota(jnp.int32, (64, 128), 1)
+    target = (row >> 3) * 6 + (row & 7)
+    source = first_y + (column & 3) * 2 + ((column >> 4) & 1)
+    offset = target - source
+    offset = jnp.where(offset < 0, offset + 48, offset)
+    offset = jnp.where(offset >= 48, offset - 48, offset)
+    chosen = (column >> 2) & 3
+    value = jnp.zeros((64, 128), F32)
+    for k in range(4):
+        value = jnp.where(chosen == k, gauss(offset, 48, widths_ref[k]), value)
+    for n, part in enumerate(halves(jnp.where(column < 32, value, 0.0))):
+        y_ref[n * 64 : (n + 1) * 64, :] = part
+
+
+def top_kernel(in_ref, x_ref, y_ref, z_ref, out_ref, plane_s, depth_s):
+    left = (x_ref[:64, :], x_ref[64:, :])
     for jp in range(4):
         tiles = [in_ref[s * TOP_ROWS + jp * 8 : s * TOP_ROWS + jp * 8 + 8, :] for s in range(16)]
         tiles.append(in_ref[pl.ds(32 + jp, SIZE_X, stride=TOP_ROWS), :])
@@ -702,11 +725,8 @@
         plane = mm(left[0], right[0]) + mm(left[0], right[1]) + mm(left[1], right[0])
         for k in range(4):
             plane_s[(k * 4 + jp) * 16 : (k * 4 + jp + 1) * 16, :] = plane[k * 16 : (k + 1) * 16]
-    row = lax.broadcasted_iota(jnp.int32, (128, 128), 0)
-    column = lax.broadcasted_iota(jnp.int32, (128, 128), 1)
     for k in range(4):
-        weight = gauss((row - column) & 63, 64, widths_ref[k]) * weights_ref[k]
-        weight = halves(jnp.where((row >> 6) == (column >> 6), weight, 0.0))
+        weight = [z_ref[(n * 4 + k) * 128 : (n * 4 + k + 1) * 128, :] for n in range(2)]
         value = halves(plane_s[k * 64 : (k + 1) * 64, :])
         depth_s[k * 64 : (k + 1) * 64, :] = (
             mm(value[0], weight[0]) + mm(value[0], weight[1]) + mm(value[1], weight[0])
@@ -720,31 +740,22 @@
         odd = jnp.where(lane < 64, pltpu.roll(first, 64, 1), second)
         tiles.append(jnp.concatenate([even, odd, jnp.zeros((96, 128), F32)], axis=0))
     right = halves(jnp.concatenate(tiles, axis=1))
-    row = lax.broadcasted_iota(jnp.int32, (64, 128), 0)
-    column = lax.broadcasted_iota(jnp.int32, (64, 128), 1)
-    target = (row >> 3) * 6 + (row & 7)
-    source = first_y + (column & 3) * 2 + ((column >> 4) & 1)
-    offset = target - source
-    offset = jnp.where(offset < 0, offset + 48, offset)
-    offset = jnp.where(offset >= 48, offset - 48, offset)
-    chosen = (column >> 2) & 3
-    left = jnp.zeros((64, 128), F32)
-    for k in range(4):
-        left = jnp.where(chosen == k, gauss(offset, 48, widths_ref[k]), left)
-    left = halves(jnp.where(column < 32, left, 0.0))
+    left = (y_ref[:64, :], y_ref[64:, :])
     out_ref[...] = mm(left[0], right[0]) + mm(left[0], right[1]) + mm(left[1], right[0])
 
 
 def finish_kernel(
     near_ref, mid_ref, top_ref, *refs
 ):
-    grow_top_ref, grow_y_ref, grow_z_ref, grow_fine_ref, out_ref, grown_s = refs
+    grow_ref, out_ref, grown_s = refs
+    grow_top, grow_z = grow_ref[:128, :], grow_ref[128:256, :]
+    grow_fine, grow_y = grow_ref[256:, :128], grow_ref[256:272, 128:]
     total = top_ref[:8, :]
     for s in range(1, SIZE_Y):
         total = total + top_ref[s * 8 : (s + 1) * 8, :]
     lanes = []
     for ip in range(5):
-        lanes.append(exact_right(total[:, ip * 128 : (ip + 1) * 128], grow_top_ref))
+        lanes.append(exact_right(total[:, ip * 128 : (ip + 1) * 128], grow_top))
     deep = jnp.concatenate(lanes, axis=1)
     tiles = []
     for i in range(17):
@@ -754,7 +765,7 @@
         tiles.append(tile)
     flat = jnp.concatenate(tiles, axis=1)
     flat = jnp.concatenate([flat, jnp.zeros((120, 17 * 128), F32)], axis=0)
-    tall = exact_left(grow_y_ref, flat)
+    tall = exact_left(grow_y, flat)
     slabs = []
     for i in range(24):
         if i > 16:
@@ -766,8 +777,8 @@
             + mid_ref[(i - 9 * h) * 16 : (i - 9 * h + 1) * 16, h * 128 : (h + 1) * 128]
         )
     for g in range(3):
-        part = exact_right(jnp.concatenate(slabs[g * 8 : (g + 1) * 8], axis=0), grow_z_ref)
-        grown_s[g * 192 : (g + 1) * 192, :] = exact_left(grow_fine_ref, part)
+        part = exact_right(jnp.concatenate(slabs[g * 8 : (g + 1) * 8], axis=0), grow_z)
+        grown_s[g * 192 : (g + 1) * 192, :] = exact_left(grow_fine, part)
     for x in range(CX):
         at = slice(x * CY, (x + 1) * CY)
         i = x // 2
@@ -812,7 +823,13 @@
     near_taps = taps(near_kernel, 1, zf, yf, outgoing)
     mid_taps = taps(mid_kernel, 2, mzf, yf, outgoing)
 
-    fine, mid, low, high, top = collect(arrived, near_taps, mid_taps)
+    bells = call(
+        gauss_kernel,
+        tuple(jax.ShapeDtypeStruct(n, BF16) for n in ((128, 256), (128, 128), (1024, 128))),
+        [SM, SM, SM, HB],
+    )(top_weights, top_widths, info, outgoing)
+
+    fine, mid, low, high, top = collect(arrived, near_taps, mid_taps, bells[0])
     before, behind = swap(low, high, "gy")
     tops = lax.all_to_all(
         top.reshape(SIZE_X, TOP_ROWS, 128), "gx", split_axis=0, concat_axis=0, tiled=True
@@ -821,9 +838,9 @@
     partial = call(
         top_kernel,
         array(64, 640),
-        [VM, SM, SM, SM],
+        [VM] * 4,
         [pltpu.VMEM((256, 128), F32), pltpu.VMEM((256, 128), F32)],
-    )(tops, top_weights, top_widths, info)
+    )(tops, *bells)
     partial = lax.all_to_all(
         partial.reshape(SIZE_Y, 8, 640), "gy", split_axis=0, concat_axis=0, tiled=True
     ).reshape(64, 640)
@@ -833,35 +850,34 @@
         own_kernel,
         array(CX * 64, 128),
         [HB, HB, VM, VM],
-        buffers(fine, halo) + [pltpu.SemaphoreType.DMA((16,))],
+        buffers(fine, halo) + [pltpu.SemaphoreType.DMA((2,))],
     )(fine, halo, zf, yf)
-    tables = (wide, near_taps, mid_taps)
-    near, mid_near = call(
+    grow_z = grow_matrix(2 * 64, 65)
+    grow_z[:, 0] += grow_z[:, 64]
+    grow_fine_z = grow_matrix(2 * 128, 129)
+    grow_fine_z[:, 0] += grow_fine_z[:, 128]
+    grow_y = np.zeros((192, 256))
+    grow_y[:, :128] = np.kron(np.eye(8), padded(grow_matrix(CY, 13), CY, 16))
+    grow_y[:16, 128:135] = padded(grow_matrix(13, 7), 16, 7)
+    grow = plain(np.concatenate([twice(grow_z[:, :64].T), grow_fine_z[:, :128].T, grow_y]))
+    tables = (wide, mzf, near_taps, mid_taps, zi, yi, mzi)
+    near, mid_near, grow = call(
         levels_kernel,
-        (array(CX * CY, NZ), array(9 * 16, 256)),
-        [VM] * 9 + [HB] * 3,
+        (array(CX * CY, NZ), array(9 * 16, 256), jax.ShapeDtypeStruct(grow.shape, BF16)),
+        [VM] * 5 + [HB] * 8,
         [
             pltpu.VMEM((40 * 64, 128), F32),
             pltpu.VMEM((32 * 64, 128), F32),
             pltpu.VMEM((24 * 64, 128), F32),
             pltpu.VMEM((16 * 64, 128), F32),
             *buffers(*tables),
-            pltpu.SemaphoreType.DMA((3,)),
+            pltpu.SemaphoreType.DMA((8,)),
         ],
-    )(own, before, behind, zf, yf, mzf, zi, yi, mzi, *tables)
-    grow_z = grow_matrix(2 * 64, 65)
-    grow_z[:, 0] += grow_z[:, 64]
-    grow_fine_z = grow_matrix(2 * 128, 129)
-    grow_fine_z[:, 0] += grow_fine_z[:, 128]
-    tables = (
-        plain(twice(grow_z[:, :64].T)),
-        plain(padded(grow_matrix(13, 7), 16, 128)),
-        plain(grow_fine_z[:, :128].T),
-        plain(np.kron(np.eye(8), padded(grow_matrix(CY, 13), CY, 16))),
-    )
+        limit=14,
+    )(own, before, behind, zf, yf, *tables, grow)
     out = call(
-        finish_kernel, array(CX * CY, NZ), [VM] * 7, [pltpu.VMEM((24 * CY, NZ), F32)]
-    )(near, mid_near, partial, *tables)
+        finish_kernel, array(CX * CY, NZ), [VM] * 4, [pltpu.VMEM((24 * CY, NZ), F32)]
+    )(near, mid_near, partial, grow)
     return out.reshape(CX, CY, NZ)
 
 

time: 97.8 us -> 93.3 us (0.954)
  Pallas kernels: 34.3 us -> 30.6 us
  waiting for transfers between devices: 28.2 us -> 26.8 us
    pallas_call x9 -> x10, Pallas kernels: 34.3 us -> 30.6 us  [run(): return kernel(*placed)]
    all_to_all x1, waiting for transfers between devices: 22.8 us -> 21.4 us  [on_device(): lax.all_to_all(outgoing.reshape(DEVICES, 1, ROWS * 128), ('gx', 'gy'), sp...]
    unnamed x34 -> x24, local copies, waits for them, and re-layouts: 2.33 us -> 2.95 us
  transfers between devices with their start and end apart: 7 -> 7, of which waited for: 3 -> 3; matrix products, arithmetic and copies ran while one was open for 5% -> 5% of each run, Pallas kernels for 16% -> 15%
where the time goes in v5:
time: 93.3 us; the launch traced here: 92.7 us
  Pallas kernels  30.6 us (33%)
  starting transfers between devices  26.9 us (29%)
  waiting for transfers between devices  26.8 us (29%)
  local copies, waits for them, and re-layouts  6.32 us (7%)
  other arithmetic  1.19 us (1%)
  between operations  0.97 us (1%)
    pallas_call x10, Pallas kernels, run(): return kernel(*placed)  30.6 us
    all_to_all x1, waiting for transfers between devices, on_device(): lax.all_to_all(outgoing.reshape(DEVICES, 1, ROWS * 128), ('gx', 'gy'), sp...  21.4 us
    all_to_all x1, starting transfers between devices, on_device(): lax.all_to_all(outgoing.reshape(DEVICES, 1, ROWS * 128), ('gx', 'gy'), sp...  11.5 us
    all_to_all x1, starting transfers between devices, on_device(): lax.all_to_all(partial.reshape(SIZE_Y, 8, 640), 'gy', split_axis=0, conca...  5.31 us
    ppermute x2, starting transfers between devices, swap(): behind = lax.ppermute(to_low, axis, backward)  3.68 us
    all_to_all x1, starting transfers between devices, on_device(): lax.all_to_all(top.reshape(SIZE_X, TOP_ROWS, 128), 'gx', split_axis=0, co...  3.59 us
    unnamed x24, local copies, waits for them, and re-layouts  2.95 us
    ppermute x2, starting transfers between devices, swap(): before = lax.ppermute(to_high, axis, forward)  2.78 us
  transfers between devices with their start and end apart: 7, of which 3 were waited for; matrix products, arithmetic and copies ran while one was open for 5% of the time, Pallas kernels for 15%

profile of v5, /device:TPU:1, one launch (start us, length us, event | category | flops | bytes accessed | tf_op | source)
XLA Modules:
  0.0 92.7 jit_solution(4776266045944321985)
XLA Ops:
  1.5 8.1 %shard_map.172.after_ref = f32[4224,128]{1,0:T(8,128)} custom-call(s32[32,128]{1,0:T(8,128)S(1)} %bitcast.20, s32[4]{0:T(128)S(1)} %pad_add_fusion.info_ref, f32[4096,128]{1,0:T(8,128)} %data_ref.1), custom_call_target="tpu_custom_call" | custom-call | tf_op jit(solution)/shard_map/pallas_call | solution.py:53
  9.6 11.5 %all-to-all-start = ((f32[128,1,4224]{2,1,0:T(1,128)}), f32[128,1,4224]{2,1,0:T(1,128)S(1)}, u32[]{:S(2)}, u32[]{:S(2)}) async-start(f32[128,1,4224]{2,1,0:T(1,128)} %bitcast.21), calls=%async_computation | async-start | bytes 4325376 | tf_op jit(solution)/shard_map/all_to_all | solution.py:809
  21.9 0.8 slice.49
  22.6 0.8 slice.51
  23.4 1.2 %concatenate.25 = f32[9,32,256]{2,1,0:T(8,128)S(1)} concatenate(f32[9,32,5]{2,1,0:T(8,128)} %slice.51, f32[9,32,119]{2,1,0:T(8,128)S(1)} %broadcast_in_dim.7, f32[9,32,9]{2,1,0:T(8,128)S(1)} %get-tuple-element.35, f32[9,32,119]{2,1,0:T(8,128)S(1)} %broadcast_in_dim.7, f32[9,32,4]{2,1,0:T(8,128)S(1)} %bitcast.22), dimensions={2} | concatenate | bytes 589824 | tf_op jit(solution)/shard_map/concatenate | solution.py:556
  24.6 1.0 %pad_maximum_fusion = f32[9,32,256]{2,1,0:T(8,128)S(1)} fusion(f32[9,32,4]{2,1,0:T(8,128)S(1)} %bitcast.23, f32[9,32,5]{2,1,0:T(8,128)} %slice.49, f32[256]{0:T(256)S(1)} %pad.6.clone), kind=kLoop, calls=%fused_computation | loop fusion | flops 147456 | bytes 306304 | tf_op jit(solution)/shard_map/concatenate | solution.py:553
  25.7 0.9 shard_map.174.refs_5_
  26.6 0.8 copy-done.1
  27.4 0.9 shard_map.173.refs_4_
  28.3 0.8 copy-done.2
  30.5 21.4 %all-to-all-done = f32[128,1,4224]{2,1,0:T(1,128)S(1)} async-done(((f32[128,1,4224]{2,1,0:T(1,128)}), f32[128,1,4224]{2,1,0:T(1,128)S(1)}, u32[]{:S(2)}, u32[]{:S(2)}) %all-to-all-start) | async-done | bytes 2162720 | tf_op jit(solution)/shard_map/all_to_all | solution.py:809
  51.9 6.5 %shard_map.176 = (f32[1536,128]{1,0:T(8,128)}, f32[384,128]{1,0:T(8,128)}, f32[376,128]{1,0:T(8,128)}, f32[376,128]{1,0:T(8,128)}, f32[640,128]{1,0:T(8,128)}) custom-call(f32[4224,128]{1,0:T(8,128)S(1)} %bitcast.15, bf16[256,128]{1,0:T(8,128)(2,1)} %constant.56.clone.refs_0_, bf16[128,192]{1,0:T(8,128)(2,1)} %constant.57.clone.refs_1_, ...), custom_call_target="tpu_custom_call" | custom-call | tf_op jit(solution)/shard_map/pallas_call | solution.py:53
  58.4 3.6 %all-to-all-start.1 = ((f32[16,40,128]{2,1,0:T(8,128)}), f32[16,40,128]{2,1,0:T(8,128)S(1)}, u32[]{:S(2)}, u32[]{:S(2)}) async-start(f32[16,40,128]{2,1,0:T(8,128)} %bitcast.24), calls=%async_computation.1 | async-start | bytes 655360 | tf_op jit(solution)/shard_map/all_to_all | solution.py:834
  62.0 1.2 %collective-permute-start = (f32[376,128]{1,0:T(8,128)}, f32[376,128]{1,0:T(8,128)S(1)}, u32[]{:S(2)}, u32[]{:S(2)}) collective-permute-start(f32[376,128]{1,0:T(8,128)} %get-tuple-element.23), channel_id=1, source_target_pairs={{0,1},{1,2},{2,3},{3,4},{4,5},{5,6},{6,7},{7,0},{8,9},{9,10},{10,1... | collective-permute-start | bytes 577544 | tf_op jit(solution)/shard_map/ppermute | solution.py:795
  63.4 2.7 %collective-permute-done.before_ref = f32[376,128]{1,0:T(8,128)S(1)} collective-permute-done((f32[376,128]{1,0:T(8,128)}, f32[376,128]{1,0:T(8,128)S(1)}, u32[]{:S(2)}, u32[]{:S(2)}) %collective-permute-start) | collective-permute-done | bytes 192544 | tf_op jit(solution)/shard_map/ppermute | solution.py:795
  66.1 2.7 %collective-permute-done.1.behind_ref = f32[376,128]{1,0:T(8,128)S(1)} collective-permute-done((f32[376,128]{1,0:T(8,128)}, f32[376,128]{1,0:T(8,128)S(1)}, u32[]{:S(2)}, u32[]{:S(2)}) %collective-permute-start.1) | collective-permute-done | bytes 192544 | tf_op jit(solution)/shard_map/ppermute | solution.py:796
  68.8 2.1 %shard_map.177 = (f32[512,128]{1,0:T(8,128)}, f32[768,128]{1,0:T(8,128)}, f32[376,128]{1,0:T(8,128)}, f32[376,128]{1,0:T(8,128)}) custom-call(f32[1536,128]{1,0:T(8,128)} %get-tuple-element.21.fine_hbm, f32[384,128]{1,0:T(8,128)} %get-tuple-element.22.mid_hbm, f32[376,128]{1,0:T(8,128)S(1)} %collective-permute-done.before_ref, ...), custom_call_target="tpu_custom_call" | custom-call | tf_op jit(solution)/shard_map/pallas_call | solution.py:53
  70.9 1.6 %collective-permute-start.2 = (f32[376,128]{1,0:T(8,128)}, f32[376,128]{1,0:T(8,128)S(1)}, u32[]{:S(2)}, u32[]{:S(2)}) collective-permute-start(f32[376,128]{1,0:T(8,128)} %get-tuple-element.26), channel_id=1, source_target_pairs={{0,8},{8,16},{16,24},{24,32},{32,40},{40,48},{48,56},{56,64},{64,7... | collective-permute-start | bytes 577544 | tf_op jit(solution)/shard_map/ppermute | solution.py:795
  72.5 3.5 %collective-permute-start.3 = (f32[376,128]{1,0:T(8,128)}, f32[376,128]{1,0:T(8,128)S(1)}, u32[]{:S(2)}, u32[]{:S(2)}) collective-permute-start(f32[376,128]{1,0:T(8,128)} %get-tuple-element.27), channel_id=1, source_target_pairs={{8,0},{16,8},{24,16},{32,24},{40,32},{48,40},{56,48},{64,56},{72,6... | collective-permute-start | bytes 577544 | tf_op jit(solution)/shard_map/ppermute | solution.py:796
  76.0 1.5 %shard_map.180 = f32[64,640]{1,0:T(8,128)} custom-call(f32[640,128]{1,0:T(8,128)S(1)} %bitcast.18, bf16[128,256]{1,0:T(8,128)(2,1)S(1)} %copy-done.6, bf16[128,128]{1,0:T(8,128)(2,1)S(1)} %get-tuple-element.32.y_ref, bf16[1024,128]{1,0:T(8,128)(2,1)S(1)} %get-tuple-element.33.z_ref), custom_call_target="tpu_custom_call" | custom-call | tf_op jit(solution)/shard_map/pallas_call | solution.py:53
  77.4 5.3 %all-to-all-start.2 = ((f32[8,8,640]{2,1,0:T(8,128)}), f32[8,8,640]{2,1,0:T(8,128)S(1)}, u32[]{:S(2)}, u32[]{:S(2)}) async-start(f32[8,8,640]{2,1,0:T(8,128)} %bitcast.10), calls=%async_computation.2 | async-start | bytes 327680 | tf_op jit(solution)/shard_map/all_to_all | solution.py:844
  82.7 2.5 %shard_map.178.own_ref = f32[2048,128]{1,0:T(8,128)S(1)} custom-call(f32[1536,128]{1,0:T(8,128)} %get-tuple-element.21.fine_hbm, f32[512,128]{1,0:T(8,128)} %get-tuple-element.25.halo_hbm, bf16[512,256]{1,0:T(8,128)(2,1)S(1)} %copy-done.3, bf16[256,512]{1,0:T(8,128)(2,1)S(1)} %copy-done), custom_call_target="tpu_custom_call" | custom-call | tf_op jit(solution)/shard_map/pallas_call | solution.py:53
  85.3 5.7 %shard_map.179 = (f32[768,256]{1,0:T(8,128)S(1)}, f32[144,256]{1,0:T(8,128)S(1)}, bf16[448,256]{1,0:T(8,128)(2,1)S(1)}) custom-call(f32[2048,128]{1,0:T(8,128)S(1)} %shard_map.178.own_ref, f32[376,128]{1,0:T(8,128)S(1)} %collective-permute-done.2.before_ref, f32[376,128]{1,0:T(8,128)S(1)} %collective-permute-done.3.behind_ref, ...), custom_call_target="tpu_custom_call" | custom-call | tf_op jit(solution)/shard_map/pallas_call | solution.py:53
  91.0 1.8 %shard_map.181 = f32[768,256]{1,0:T(8,128)} custom-call(f32[768,256]{1,0:T(8,128)S(1)} %get-tuple-element.29.near_ref, f32[144,256]{1,0:T(8,128)S(1)} %get-tuple-element.30.mid_ref, f32[64,640]{1,0:T(8,128)S(1)} %bitcast.19, bf16[448,256]{1,0:T(8,128)(2,1)S(1)} %get-tuple-element.34.refs_0_), custom_call_target="tpu_custom_call" | custom-call | tf_op jit(solution)/shard_map/pallas_call | solution.py:53
  (47 shorter events, 3.2 us)
Async XLA Ops:
  0.7 0.7 copy-start.7
  9.6 11.5 %copy-start.10 = (f32[9,9,9]{2,1,0:T(8,128)S(1)}, f32[9,9,9]{2,1,0:T(8,128)}, u32[]{:S(2)}) copy-start(f32[9,9,9]{2,1,0:T(8,128)} %param.21) | copy-start | bytes 8752
  9.6 11.6 %copy-start.11 = (f32[9,9,9]{2,1,0:T(8,128)S(1)}, f32[9,9,9]{2,1,0:T(8,128)}, u32[]{:S(2)}) copy-start(f32[9,9,9]{2,1,0:T(8,128)} %param.22) | copy-start | bytes 8752
  9.6 12.0 %slice-start = ((f32[9,9,9]{2,1,0:T(8,128)}), f32[9,5,9]{2,1,0:T(8,128)S(1)}, s32[]{:S(2)}) async-start(f32[9,9,9]{2,1,0:T(8,128)} %param.21), calls=%async_computation.3 | async-start | bytes 73728 | tf_op jit(solution)/shard_map/slice | solution.py:550
  9.6 12.1 %slice-start.1 = ((f32[9,9,9]{2,1,0:T(8,128)}), f32[9,5,9]{2,1,0:T(8,128)S(1)}, s32[]{:S(2)}) async-start(f32[9,9,9]{2,1,0:T(8,128)} %param.22), calls=%async_computation.4 | async-start | bytes 73728 | tf_op jit(solution)/shard_map/slice | solution.py:550
  9.6 42.3 %all-to-all-start = ((f32[128,1,4224]{2,1,0:T(1,128)}), f32[128,1,4224]{2,1,0:T(1,128)S(1)}, u32[]{:S(2)}, u32[]{:S(2)}) async-start(f32[128,1,4224]{2,1,0:T(1,128)} %bitcast.21), calls=%async_computation | async-start | bytes 4325376 | tf_op jit(solution)/shard_map/all_to_all | solution.py:809
  21.8 4.0 %copy-start = (bf16[256,512]{1,0:T(8,128)(2,1)S(1)}, bf16[256,512]{1,0:T(8,128)(2,1)}, u32[]{:S(2)}) copy-start(bf16[256,512]{1,0:T(8,128)(2,1)} %constant.54.clone.y_ref.refs_1_) | copy-start | bytes 786436
  21.8 4.0 %copy-start.4 = (bf16[512,256]{1,0:T(8,128)(2,1)S(1)}, bf16[512,256]{1,0:T(8,128)(2,1)}, u32[]{:S(2)}) copy-start(bf16[512,256]{1,0:T(8,128)(2,1)} %constant.55.clone.z_ref.refs_3_) | copy-start | bytes 786436
  25.7 1.8 %copy-start.3 = (bf16[512,256]{1,0:T(8,128)(2,1)S(1)}, bf16[512,256]{1,0:T(8,128)(2,1)}, u32[]{:S(2)}) copy-start(bf16[512,256]{1,0:T(8,128)(2,1)} %constant.53.clone.z_ref.refs_0_) | copy-start | bytes 786436
  26.6 0.8 copy-start.1
  27.4 1.7 %copy-start.8 = (f32[4]{0:T(128)S(1)}, f32[4]{0:T(128)}, u32[]{:S(2)}) copy-start(f32[4]{0:T(128)} %weights_ref.1) | copy-start | bytes 52
  27.4 1.7 %copy-start.9 = (f32[4]{0:T(128)S(1)}, f32[4]{0:T(128)}, u32[]{:S(2)}) copy-start(f32[4]{0:T(128)} %widths_ref.1) | copy-start | bytes 52
  28.3 0.8 copy-start.2
  29.8 0.6 copy-start.5
  51.9 24.1 %copy-start.6 = (bf16[128,256]{1,0:T(8,128)(2,1)S(1)}, bf16[128,256]{1,0:T(8,128)(2,1)}, u32[]{:S(2)}) copy-start(bf16[128,256]{1,0:T(8,128)(2,1)} %copy-done.5) | copy-start | bytes 196612
  58.4 17.6 %all-to-all-start.1 = ((f32[16,40,128]{2,1,0:T(8,128)}), f32[16,40,128]{2,1,0:T(8,128)S(1)}, u32[]{:S(2)}, u32[]{:S(2)}) async-start(f32[16,40,128]{2,1,0:T(8,128)} %bitcast.24), calls=%async_computation.1 | async-start | bytes 655360 | tf_op jit(solution)/shard_map/all_to_all | solution.py:834
  62.0 4.1 %collective-permute-start = (f32[376,128]{1,0:T(8,128)}, f32[376,128]{1,0:T(8,128)S(1)}, u32[]{:S(2)}, u32[]{:S(2)}) collective-permute-start(f32[376,128]{1,0:T(8,128)} %get-tuple-element.23), channel_id=1, source_target_pairs={{0,1},{1,2},{2,3},{3,4},{4,5},{5,6},{6,7},{7,0},{8,9},{9,10},{10,1... | collective-permute-start | bytes 577544 | tf_op jit(solution)/shard_map/ppermute | solution.py:795
  63.2 5.6 %collective-permute-start.1 = (f32[376,128]{1,0:T(8,128)}, f32[376,128]{1,0:T(8,128)S(1)}, u32[]{:S(2)}, u32[]{:S(2)}) collective-permute-start(f32[376,128]{1,0:T(8,128)} %get-tuple-element.24), channel_id=1, source_target_pairs={{1,0},{2,1},{3,2},{4,3},{5,4},{6,5},{7,6},{0,7},{9,8},{10,9},{11,1... | collective-permute-start | bytes 577544 | tf_op jit(solution)/shard_map/ppermute | solution.py:796
  70.9 14.4 %collective-permute-start.2 = (f32[376,128]{1,0:T(8,128)}, f32[376,128]{1,0:T(8,128)S(1)}, u32[]{:S(2)}, u32[]{:S(2)}) collective-permute-start(f32[376,128]{1,0:T(8,128)} %get-tuple-element.26), channel_id=1, source_target_pairs={{0,8},{8,16},{16,24},{24,32},{32,40},{40,48},{48,56},{56,64},{64,7... | collective-permute-start | bytes 577544 | tf_op jit(solution)/shard_map/ppermute | solution.py:795
  72.5 12.8 %collective-permute-start.3 = (f32[376,128]{1,0:T(8,128)}, f32[376,128]{1,0:T(8,128)S(1)}, u32[]{:S(2)}, u32[]{:S(2)}) collective-permute-start(f32[376,128]{1,0:T(8,128)} %get-tuple-element.27), channel_id=1, source_target_pairs={{8,0},{16,8},{24,16},{32,24},{40,32},{48,40},{56,48},{64,56},{72,6... | collective-permute-start | bytes 577544 | tf_op jit(solution)/shard_map/ppermute | solution.py:796
  77.4 13.5 %all-to-all-start.2 = ((f32[8,8,640]{2,1,0:T(8,128)}), f32[8,8,640]{2,1,0:T(8,128)S(1)}, u32[]{:S(2)}, u32[]{:S(2)}) async-start(f32[8,8,640]{2,1,0:T(8,128)} %bitcast.10), calls=%async_computation.2 | async-start | bytes 327680 | tf_op jit(solution)/shard_map/all_to_all | solution.py:844

commit v6 on v5

--- a/solution.py
+++ b/solution.py
@@ -266,19 +266,24 @@
     one, zero = jnp.ones((256, 128), BF16), jnp.zeros((256, 128), BF16)
 
     def block(b, carry):
-        first = pl.multiple_of(b * 256, 256)
-        acc = jnp.zeros((256, 256), F32)
+        first = pl.multiple_of(b * 512, 512)
+        acc = [jnp.zeros((256, 256), F32)] * 2
         for k in range(16):
-            parts = []
-            for q in range(2):
-                ids = jnp.clip(ids_s[2 * k + q : 2 * k + q + 1, :] - first, -1, 256)
-                line = jnp.broadcast_to(ids.astype(F32), (16, 128)).astype(BF16)
-                parts.append(jnp.where(rows == jnp.concatenate([line] * 16, axis=0), one, zero))
-            acc = acc + mm(jnp.concatenate(parts, axis=1), data_s[k * 256 : (k + 1) * 256, :])
-        fine_ref[pl.ds(first, 256), :] = acc[:, :128] + acc[:, 128:]
+            for m in range(2):
+                parts = []
+                for q in range(2):
+                    ids = ids_s[2 * k + q : 2 * k + q + 1, :] - (first + m * 256)
+                    line = jnp.clip(ids, -1, 256).astype(F32)
+                    line = jnp.broadcast_to(line, (16, 128)).astype(BF16)
+                    parts.append(jnp.where(rows == jnp.concatenate([line] * 16, axis=0), one, zero))
+                hit = jnp.concatenate(parts, axis=1)
+                acc[m] = acc[m] + mm(hit, data_s[k * 256 : (k + 1) * 256, :])
+        for m in range(2):
+            value = acc[m][:, :128] + acc[m][:, 128:]
+            fine_ref[pl.ds(pl.multiple_of(first + m * 256, 256), 256), :] = value
         return carry
 
-    lax.fori_loop(0, 6, block, 0)
+    lax.fori_loop(0, 3, block, 0)
     out_copies = started([(fine_ref, outs[0])], sems, 4)
     for i in range(17):
         total = None
@@ -352,24 +357,16 @@
 
 
 def merge_kernel(
-    fine_hbm, mid_hbm, before_ref, behind_ref, halo_hbm, wide_hbm, low_hbm, high_hbm,
-    fine_s, mid_ref, halo_ref, wide_ref, low_ref, high_ref, sems,
+    fine_hbm, mid_hbm, before_ref, behind_ref, fine_s, halo_ref, wide_hbm, low_hbm, high_hbm,
+    mid_ref, wide_ref, low_ref, high_ref, sems,
 ):
-    pairs = [(mid_hbm, mid_ref)]
-    for h in range(2):
-        for first, at in ((0, 0), (CX - 4, 4)):
-            start = (h * CX + first) * CY
-            pairs.append(
-                (fine_hbm.at[pl.ds(start, 4 * CY)], fine_s.at[pl.ds((h * 8 + at) * CY, 4 * CY)])
-            )
-    mid_copy, *fine_copies = started(pairs, sems)
+    mid_copy, fine_copy = started([(mid_hbm, mid_ref), (fine_hbm, fine_s)], sems)
     for h in range(2):
         for c in range(4):
             at = slice((h * 4 + c) * CX, (h * 4 + c + 1) * CX)
             start = h * CX * 8 + c
             halo_ref[pl.ds(start, CX, stride=8), :] = behind_ref[at, :]
             halo_ref[pl.ds(start + 4, CX, stride=8), :] = before_ref[at, :]
-    out_copies = started([(halo_ref, halo_hbm)], sems, 5)
     mid_copy.wait()
     for i in range(24):
         wide_ref[i * YD : i * YD + 16, :] = mid_ref[i * 16 : (i + 1) * 16, :]
@@ -385,14 +382,13 @@
         if j == 4:
             before = before + wide_ref[pl.ds(0, 24, stride=YD), :]
         wide_ref[pl.ds(row, 24, stride=YD), :] = before
-    out_copies += started([(wide_ref, wide_hbm)], sems, 6)
-    for copy in fine_copies:
-        copy.wait()
-    for ref, first, at_fine, mid_first in ((low_ref, 0, 0, 0), (high_ref, CX - 4, 4, 12)):
+    out_copies = started([(wide_ref, wide_hbm)], sems, 2)
+    fine_copy.wait()
+    for ref, first, mid_first in ((low_ref, 0, 0), (high_ref, CX - 4, 12)):
         for h in range(2):
             for x in range(4):
                 at = h * 128 + x * YD
-                source = (h * 8 + at_fine + x) * CY
+                source = (h * CX + first + x) * CY
                 ref[at : at + CY, :] = fine_s[source : source + CY, :]
                 source = (h * CX + first + x) * 8
                 ref[at + CY : at + YD, :] = halo_ref[source : source + 8, :]
@@ -403,24 +399,29 @@
             ref[at + 16 : at + 24, :] = (
                 wide_ref[base + 16 : base + 24, :] + wide_ref[base + 24 : base + 32, :]
             )
-    out_copies += started([(low_ref, low_hbm), (high_ref, high_hbm)], sems, 7)
+    out_copies += started([(low_ref, low_hbm), (high_ref, high_hbm)], sems, 3)
     for copy in out_copies:
         copy.wait()
 
 
 def merge(fine, mid, before, behind):
-    out = (array(2 * CX * 8, 128), array(24 * YD, 128), array(SEND, 128), array(SEND, 128))
+    out = (
+        array(2 * CX * CY, 128),
+        array(2 * CX * 8, 128),
+        array(24 * YD, 128),
+        array(SEND, 128),
+        array(SEND, 128),
+    )
     return call(
         merge_kernel,
         out,
         [HB, HB, VM, VM],
         [
-            pltpu.VMEM((16 * CY, 128), F32),
             pltpu.VMEM((24 * 16, 128), F32),
-            *buffers(*out),
-            pltpu.SemaphoreType.DMA((9,)),
+            *buffers(*out[2:]),
+            pltpu.SemaphoreType.DMA((5,)),
         ],
-        outs=HB,
+        outs=(VM, VM, HB, HB, HB),
     )(fine, mid, before, behind)
 
 
@@ -529,8 +530,6 @@
 
 
 def taps_kernel(copies, in_ref, z_ref, y_ref, after_ref, out_ref):
-    lane_special, row = special_mask(copies, YD)
-    special = lane_special & ((row == 0) | (row == 16))
     for p in range(2):
         slabs = forward_chunk(in_ref[p * 256 : (p + 1) * 256, :], z_ref, y_ref, copies)
         for j in range(8):
@@ -538,7 +537,7 @@
             if dx > 8:
                 break
             real, imag = slabs[j][:YD], slabs[j][YD:]
-            values = (real, jnp.where(special, imag, real), jnp.where(special, 0.0, imag))
+            values = (real, imag, real + imag)
             for part in range(3):
                 at = (part * 9 + dx) * YD
                 out_ref[at : at + YD, :] = values[part]
@@ -560,9 +559,7 @@
     )(wide.reshape(16 * YD, 256), z_matrix, y_matrix, after)
 
 
-def own_kernel(fine_hbm, halo_hbm, z_ref, y_ref, out_ref, fine_s, halo_s, sems):
-    for copy in started([(fine_hbm, fine_s), (halo_hbm, halo_s)], sems):
-        copy.wait()
+def own_kernel(fine_s, halo_s, z_ref, y_ref, out_ref):
     for p in range(CX // 8):
         columns = []
         for h in range(2):
@@ -578,32 +575,40 @@
 
 def convolve(copies, first, count, taps_ref, freq_s, conv_s):
     lane_special, row = special_mask(copies, 8)
+    whole = lane_special & (row == 0)
     for v in range(2):
-        sums = [[None] * 4 for _ in range(count)]
+        sums = [[None] * 6 for _ in range(count)]
         for dx in range(9):
             coefs = []
             for half in range(2):
                 at = dx * YD + half * 16 + v * 8
                 coefs.append([taps_ref[at + part * 288 : at + part * 288 + 8, :] for part in range(3)])
             for j in range(count):
-                old = sums[j]
                 for half in range(2):
-                    at = (first + j + dx) * 64 + v * 8 + half * 16
-                    re = freq_s[at : at + 8, :]
-                    im = freq_s[at + 32 : at + 40, :]
-                    a, t, b = coefs[half]
-                    new_re = a * re - b * im
-                    new_im = b * re + t * im
-                    old[2 * half] = new_re if dx == 0 else old[2 * half] + new_re
-                    old[2 * half + 1] = new_im if dx == 0 else old[2 * half + 1] + new_im
-        special = lane_special & (row != 0) if v == 0 else lane_special
+                    at = (first + j + dx) * 96 + v * 8 + half * 16
+                    for part in range(3):
+                        term = coefs[half][part] * freq_s[at + part * 32 : at + part * 32 + 8, :]
+                        n = 3 * half + part
+                        sums[j][n] = term if dx == 0 else sums[j][n] + term
         for j in range(count):
-            ar, ai, br, bi = sums[j]
+            values = []
+            for half in range(2):
+                re, im, both = sums[j][3 * half : 3 * half + 3]
+                real, imag = re - im, both - re - im
+                if v == 0:
+                    real, imag = jnp.where(whole, re, real), jnp.where(whole, im, imag)
+                values += [real, imag]
+            ar, ai, br, bi = values
+            special = lane_special & (row != 0) if v == 0 else lane_special
             at = (first + j) * 64 + v * 8
             conv_s[at : at + 8, :] = jnp.where(special, ar - bi, ar)
             conv_s[at + 16 : at + 24, :] = jnp.where(special, ar + bi, br)
             conv_s[at + 32 : at + 40, :] = jnp.where(special, ai + br, ai)
             conv_s[at + 48 : at + 56, :] = jnp.where(special, br - ai, bi)
+
+
+def with_sum(slab):
+    return jnp.concatenate([slab, slab[:YD] + slab[YD:]], axis=0)
 
 
 def wide_slab(ref, index):
@@ -622,14 +627,15 @@
     near_ref, mid_ref, grow_ref, freq_s, conv_s, mid_freq_s, mid_conv_s = refs[10:17]
     wide_ref, mzf_ref, near_taps, mid_taps, zi_ref, yi_ref, mzi_ref, sems = refs[17:]
     copies = started(list(zip(refs[2:10], (*refs[17:24], grow_ref))), sems)
-    freq_s[4 * 64 : 36 * 64, :] = own_ref[...]
+    for x in range(CX):
+        freq_s[(x + 4) * 96 : (x + 5) * 96, :] = with_sum(own_ref[x * 64 : (x + 1) * 64, :])
     edges = [
         jnp.concatenate([ref[:128, :], ref[128:256, :]], axis=1) for ref in (before_ref, behind_ref)
     ]
     slabs = forward_chunk(jnp.concatenate(edges, axis=0), zf_ref, yf_ref, 1)
     for j in range(8):
         at = j if j < 4 else 32 + j
-        freq_s[at * 64 : (at + 1) * 64, :] = slabs[j]
+        freq_s[at * 96 : (at + 1) * 96, :] = with_sum(slabs[j])
     zero = jnp.zeros((YD, 128), F32)
     copies[0].wait()
     copies[1].wait()
@@ -655,7 +661,7 @@
         slabs = forward_chunk(jnp.concatenate(pairs, axis=0), mzf_ref, yf_ref, 2)
         for j in range(8):
             at = p * 8 + j
-            mid_freq_s[at * 64 : (at + 1) * 64, :] = slabs[j]
+            mid_freq_s[at * 96 : (at + 1) * 96, :] = with_sum(slabs[j])
     for copy in copies[2:]:
         copy.wait()
     for p in range(4):
@@ -844,14 +850,9 @@
     partial = lax.all_to_all(
         partial.reshape(SIZE_Y, 8, 640), "gy", split_axis=0, concat_axis=0, tiled=True
     ).reshape(64, 640)
-    halo, wide, low, high = merge(fine, mid, before, behind)
+    fine, halo, wide, low, high = merge(fine, mid, before, behind)
     before, behind = swap(low, high, "gx")
-    own = call(
-        own_kernel,
-        array(CX * 64, 128),
-        [HB, HB, VM, VM],
-        buffers(fine, halo) + [pltpu.SemaphoreType.DMA((2,))],
-    )(fine, halo, zf, yf)
+    own = call(own_kernel, array(CX * 64, 128), [VM] * 4)(fine, halo, zf, yf)
     grow_z = grow_matrix(2 * 64, 65)
     grow_z[:, 0] += grow_z[:, 64]
     grow_fine_z = grow_matrix(2 * 128, 129)
@@ -866,9 +867,9 @@
         (array(CX * CY, NZ), array(9 * 16, 256), jax.ShapeDtypeStruct(grow.shape, BF16)),
         [VM] * 5 + [HB] * 8,
         [
-            pltpu.VMEM((40 * 64, 128), F32),
+            pltpu.VMEM((40 * 96, 128), F32),
             pltpu.VMEM((32 * 64, 128), F32),
-            pltpu.VMEM((24 * 64, 128), F32),
+            pltpu.VMEM((24 * 96, 128), F32),
             pltpu.VMEM((16 * 64, 128), F32),
             *buffers(*tables),
             pltpu.SemaphoreType.DMA((8,)),

time: 93.3 us -> 91.1 us (0.976)
  Pallas kernels: 30.6 us -> 28.4 us
    pallas_call x10, Pallas kernels: 30.6 us -> 28.4 us  [run(): return kernel(*placed)]
  transfers between devices with their start and end apart: 7 -> 7, of which waited for: 3 -> 3; matrix products, arithmetic and copies ran while one was open for 5% -> 5% of each run, Pallas kernels for 15% -> 14%
where the time goes in v6:
time: 91.1 us; the launch traced here: 90.6 us
  Pallas kernels  28.4 us (31%)
  starting transfers between devices  26.8 us (29%)
  waiting for transfers between devices  26.8 us (29%)
  local copies, waits for them, and re-layouts  6.32 us (7%)
  other arithmetic  1.19 us (1%)
  between operations  0.97 us (1%)
    pallas_call x10, Pallas kernels, run(): return kernel(*placed)  28.4 us
    all_to_all x1, waiting for transfers between devices, on_device(): lax.all_to_all(outgoing.reshape(DEVICES, 1, ROWS * 128), ('gx', 'gy'), sp...  21.4 us
    all_to_all x1, starting transfers between devices, on_device(): lax.all_to_all(outgoing.reshape(DEVICES, 1, ROWS * 128), ('gx', 'gy'), sp...  11.5 us
    all_to_all x1, starting transfers between devices, on_device(): lax.all_to_all(partial.reshape(SIZE_Y, 8, 640), 'gy', split_axis=0, conca...  5.3 us
    ppermute x2, starting transfers between devices, swap(): behind = lax.ppermute(to_low, axis, backward)  3.68 us
    all_to_all x1, starting transfers between devices, on_device(): lax.all_to_all(top.reshape(SIZE_X, TOP_ROWS, 128), 'gx', split_axis=0, co...  3.59 us
    unnamed x24, local copies, waits for them, and re-layouts  2.95 us
    ppermute x2, starting transfers between devices, swap(): before = lax.ppermute(to_high, axis, forward)  2.78 us
  transfers between devices with their start and end apart: 7, of which 3 were waited for; matrix products, arithmetic and copies ran while one was open for 5% of the time, Pallas kernels for 14%

profile of v6, /device:TPU:1, one launch (start us, length us, event | category | flops | bytes accessed | tf_op | source)
XLA Modules:
  0.0 90.6 jit_solution(6251143127466289166)
XLA Ops:
  1.5 8.1 %shard_map.172.after_ref = f32[4224,128]{1,0:T(8,128)} custom-call(s32[32,128]{1,0:T(8,128)S(1)} %bitcast.20, s32[4]{0:T(128)S(1)} %pad_add_fusion.info_ref, f32[4096,128]{1,0:T(8,128)} %data_ref.1), custom_call_target="tpu_custom_call" | custom-call | tf_op jit(solution)/shard_map/pallas_call | solution.py:53
  9.6 11.5 %all-to-all-start = ((f32[128,1,4224]{2,1,0:T(1,128)}), f32[128,1,4224]{2,1,0:T(1,128)S(1)}, u32[]{:S(2)}, u32[]{:S(2)}) async-start(f32[128,1,4224]{2,1,0:T(1,128)} %bitcast.21), calls=%async_computation | async-start | bytes 4325376 | tf_op jit(solution)/shard_map/all_to_all | solution.py:815
  21.9 0.8 slice.49
  22.6 0.8 slice.51
  23.4 1.2 %concatenate.25 = f32[9,32,256]{2,1,0:T(8,128)S(1)} concatenate(f32[9,32,5]{2,1,0:T(8,128)} %slice.51, f32[9,32,119]{2,1,0:T(8,128)S(1)} %broadcast_in_dim.7, f32[9,32,9]{2,1,0:T(8,128)S(1)} %get-tuple-element.37, f32[9,32,119]{2,1,0:T(8,128)S(1)} %broadcast_in_dim.7, f32[9,32,4]{2,1,0:T(8,128)S(1)} %bitcast.22), dimensions={2} | concatenate | bytes 589824 | tf_op jit(solution)/shard_map/concatenate | solution.py:555
  24.6 1.0 %pad_maximum_fusion = f32[9,32,256]{2,1,0:T(8,128)S(1)} fusion(f32[9,32,4]{2,1,0:T(8,128)S(1)} %bitcast.23, f32[9,32,5]{2,1,0:T(8,128)} %slice.49, f32[256]{0:T(256)S(1)} %pad.6.clone), kind=kLoop, calls=%fused_computation | loop fusion | flops 147456 | bytes 306304 | tf_op jit(solution)/shard_map/concatenate | solution.py:552
  25.7 0.9 shard_map.174.refs_5_
  26.6 0.8 copy-done.1
  27.4 0.9 shard_map.173.refs_4_
  28.3 0.8 copy-done.2
  30.5 21.4 %all-to-all-done = f32[128,1,4224]{2,1,0:T(1,128)S(1)} async-done(((f32[128,1,4224]{2,1,0:T(1,128)}), f32[128,1,4224]{2,1,0:T(1,128)S(1)}, u32[]{:S(2)}, u32[]{:S(2)}) %all-to-all-start) | async-done | bytes 2162720 | tf_op jit(solution)/shard_map/all_to_all | solution.py:815
  51.9 6.0 %shard_map.176 = (f32[1536,128]{1,0:T(8,128)}, f32[384,128]{1,0:T(8,128)}, f32[376,128]{1,0:T(8,128)}, f32[376,128]{1,0:T(8,128)}, f32[640,128]{1,0:T(8,128)}) custom-call(f32[4224,128]{1,0:T(8,128)S(1)} %bitcast.15, bf16[256,128]{1,0:T(8,128)(2,1)} %constant.56.clone.refs_0_, bf16[128,192]{1,0:T(8,128)(2,1)} %constant.57.clone.refs_1_, ...), custom_call_target="tpu_custom_call" | custom-call | tf_op jit(solution)/shard_map/pallas_call | solution.py:53
  57.9 3.6 %all-to-all-start.1 = ((f32[16,40,128]{2,1,0:T(8,128)}), f32[16,40,128]{2,1,0:T(8,128)S(1)}, u32[]{:S(2)}, u32[]{:S(2)}) async-start(f32[16,40,128]{2,1,0:T(8,128)} %bitcast.24), calls=%async_computation.1 | async-start | bytes 655360 | tf_op jit(solution)/shard_map/all_to_all | solution.py:840
  61.5 1.2 %collective-permute-start = (f32[376,128]{1,0:T(8,128)}, f32[376,128]{1,0:T(8,128)S(1)}, u32[]{:S(2)}, u32[]{:S(2)}) collective-permute-start(f32[376,128]{1,0:T(8,128)} %get-tuple-element.24), channel_id=1, source_target_pairs={{0,1},{1,2},{2,3},{3,4},{4,5},{5,6},{6,7},{7,0},{8,9},{9,10},{10,1... | collective-permute-start | bytes 577544 | tf_op jit(solution)/shard_map/ppermute | solution.py:801
  62.9 2.7 %collective-permute-done.before_ref = f32[376,128]{1,0:T(8,128)S(1)} collective-permute-done((f32[376,128]{1,0:T(8,128)}, f32[376,128]{1,0:T(8,128)S(1)}, u32[]{:S(2)}, u32[]{:S(2)}) %collective-permute-start) | collective-permute-done | bytes 192544 | tf_op jit(solution)/shard_map/ppermute | solution.py:801
  65.6 2.7 %collective-permute-done.1.behind_ref = f32[376,128]{1,0:T(8,128)S(1)} collective-permute-done((f32[376,128]{1,0:T(8,128)}, f32[376,128]{1,0:T(8,128)S(1)}, u32[]{:S(2)}, u32[]{:S(2)}) %collective-permute-start.1) | collective-permute-done | bytes 192544 | tf_op jit(solution)/shard_map/ppermute | solution.py:802
  68.2 2.1 %shard_map.177 = (f32[1536,128]{1,0:T(8,128)S(1)}, f32[512,128]{1,0:T(8,128)S(1)}, f32[768,128]{1,0:T(8,128)}, f32[376,128]{1,0:T(8,128)}, f32[376,128]{1,0:T(8,128)}) custom-call(f32[1536,128]{1,0:T(8,128)} %get-tuple-element.22.fine_hbm, f32[384,128]{1,0:T(8,128)} %get-tuple-element.23.mid_hbm, f32[376,128]{1,0:T(8,128)S(1)} %collective-permute-done.before_ref, ...), custom_call_target="tpu_custom_call" | custom-call | tf_op jit(solution)/shard_map/pallas_call | solution.py:53
  70.3 1.6 %collective-permute-start.2 = (f32[376,128]{1,0:T(8,128)}, f32[376,128]{1,0:T(8,128)S(1)}, u32[]{:S(2)}, u32[]{:S(2)}) collective-permute-start(f32[376,128]{1,0:T(8,128)} %get-tuple-element.28), channel_id=1, source_target_pairs={{0,8},{8,16},{16,24},{24,32},{32,40},{40,48},{48,56},{56,64},{64,7... | collective-permute-start | bytes 577544 | tf_op jit(solution)/shard_map/ppermute | solution.py:801
  71.9 3.5 %collective-permute-start.3 = (f32[376,128]{1,0:T(8,128)}, f32[376,128]{1,0:T(8,128)S(1)}, u32[]{:S(2)}, u32[]{:S(2)}) collective-permute-start(f32[376,128]{1,0:T(8,128)} %get-tuple-element.29), channel_id=1, source_target_pairs={{8,0},{16,8},{24,16},{32,24},{40,32},{48,40},{56,48},{64,56},{72,6... | collective-permute-start | bytes 577544 | tf_op jit(solution)/shard_map/ppermute | solution.py:802
  75.4 1.5 %shard_map.180 = f32[64,640]{1,0:T(8,128)} custom-call(f32[640,128]{1,0:T(8,128)S(1)} %bitcast.18, bf16[128,256]{1,0:T(8,128)(2,1)S(1)} %copy-done.6, bf16[128,128]{1,0:T(8,128)(2,1)S(1)} %get-tuple-element.34.y_ref, bf16[1024,128]{1,0:T(8,128)(2,1)S(1)} %get-tuple-element.35.z_ref), custom_call_target="tpu_custom_call" | custom-call | tf_op jit(solution)/shard_map/pallas_call | solution.py:53
  76.9 5.3 %all-to-all-start.2 = ((f32[8,8,640]{2,1,0:T(8,128)}), f32[8,8,640]{2,1,0:T(8,128)S(1)}, u32[]{:S(2)}, u32[]{:S(2)}) async-start(f32[8,8,640]{2,1,0:T(8,128)} %bitcast.10), calls=%async_computation.2 | async-start | bytes 327680 | tf_op jit(solution)/shard_map/all_to_all | solution.py:850
  82.2 1.3 %shard_map.178.own_ref = f32[2048,128]{1,0:T(8,128)S(1)} custom-call(f32[1536,128]{1,0:T(8,128)S(1)} %get-tuple-element.26.fine_s, f32[512,128]{1,0:T(8,128)S(1)} %get-tuple-element.27.halo_s, bf16[512,256]{1,0:T(8,128)(2,1)S(1)} %copy-done.3, bf16[256,512]{1,0:T(8,128)(2,1)S(1)} %copy-done), custom_call_target="tpu_custom_call" | custom-call | tf_op jit(solution)/shard_map/pallas_call | solution.py:53
  83.5 5.2 %shard_map.179 = (f32[768,256]{1,0:T(8,128)S(1)}, f32[144,256]{1,0:T(8,128)S(1)}, bf16[448,256]{1,0:T(8,128)(2,1)S(1)}) custom-call(f32[2048,128]{1,0:T(8,128)S(1)} %shard_map.178.own_ref, f32[376,128]{1,0:T(8,128)S(1)} %collective-permute-done.2.before_ref, f32[376,128]{1,0:T(8,128)S(1)} %collective-permute-done.3.behind_ref, ...), custom_call_target="tpu_custom_call" | custom-call | tf_op jit(solution)/shard_map/pallas_call | solution.py:53
  88.8 1.8 %shard_map.181 = f32[768,256]{1,0:T(8,128)} custom-call(f32[768,256]{1,0:T(8,128)S(1)} %get-tuple-element.31.near_ref, f32[144,256]{1,0:T(8,128)S(1)} %get-tuple-element.32.mid_ref, f32[64,640]{1,0:T(8,128)S(1)} %bitcast.19, bf16[448,256]{1,0:T(8,128)(2,1)S(1)} %get-tuple-element.36.refs_0_), custom_call_target="tpu_custom_call" | custom-call | tf_op jit(solution)/shard_map/pallas_call | solution.py:53
  (47 shorter events, 3.2 us)
Async XLA Ops:
  0.7 0.7 copy-start.7
  9.6 11.5 %copy-start.10 = (f32[9,9,9]{2,1,0:T(8,128)S(1)}, f32[9,9,9]{2,1,0:T(8,128)}, u32[]{:S(2)}) copy-start(f32[9,9,9]{2,1,0:T(8,128)} %param.21) | copy-start | bytes 8752
  9.6 11.6 %copy-start.11 = (f32[9,9,9]{2,1,0:T(8,128)S(1)}, f32[9,9,9]{2,1,0:T(8,128)}, u32[]{:S(2)}) copy-start(f32[9,9,9]{2,1,0:T(8,128)} %param.22) | copy-start | bytes 8752
  9.6 12.0 %slice-start = ((f32[9,9,9]{2,1,0:T(8,128)}), f32[9,5,9]{2,1,0:T(8,128)S(1)}, s32[]{:S(2)}) async-start(f32[9,9,9]{2,1,0:T(8,128)} %param.21), calls=%async_computation.3 | async-start | bytes 73728 | tf_op jit(solution)/shard_map/slice | solution.py:549
  9.6 12.1 %slice-start.1 = ((f32[9,9,9]{2,1,0:T(8,128)}), f32[9,5,9]{2,1,0:T(8,128)S(1)}, s32[]{:S(2)}) async-start(f32[9,9,9]{2,1,0:T(8,128)} %param.22), calls=%async_computation.4 | async-start | bytes 73728 | tf_op jit(solution)/shard_map/slice | solution.py:549
  9.6 42.3 %all-to-all-start = ((f32[128,1,4224]{2,1,0:T(1,128)}), f32[128,1,4224]{2,1,0:T(1,128)S(1)}, u32[]{:S(2)}, u32[]{:S(2)}) async-start(f32[128,1,4224]{2,1,0:T(1,128)} %bitcast.21), calls=%async_computation | async-start | bytes 4325376 | tf_op jit(solution)/shard_map/all_to_all | solution.py:815
  21.8 4.0 %copy-start = (bf16[256,512]{1,0:T(8,128)(2,1)S(1)}, bf16[256,512]{1,0:T(8,128)(2,1)}, u32[]{:S(2)}) copy-start(bf16[256,512]{1,0:T(8,128)(2,1)} %constant.54.clone.y_ref.refs_1_) | copy-start | bytes 786436
  21.8 4.0 %copy-start.4 = (bf16[512,256]{1,0:T(8,128)(2,1)S(1)}, bf16[512,256]{1,0:T(8,128)(2,1)}, u32[]{:S(2)}) copy-start(bf16[512,256]{1,0:T(8,128)(2,1)} %constant.55.clone.z_ref.refs_3_) | copy-start | bytes 786436
  25.7 1.8 %copy-start.3 = (bf16[512,256]{1,0:T(8,128)(2,1)S(1)}, bf16[512,256]{1,0:T(8,128)(2,1)}, u32[]{:S(2)}) copy-start(bf16[512,256]{1,0:T(8,128)(2,1)} %constant.53.clone.z_ref.refs_0_) | copy-start | bytes 786436
  26.6 0.8 copy-start.1
  27.4 1.7 %copy-start.8 = (f32[4]{0:T(128)S(1)}, f32[4]{0:T(128)}, u32[]{:S(2)}) copy-start(f32[4]{0:T(128)} %weights_ref.1) | copy-start | bytes 52
  27.4 1.7 %copy-start.9 = (f32[4]{0:T(128)S(1)}, f32[4]{0:T(128)}, u32[]{:S(2)}) copy-start(f32[4]{0:T(128)} %widths_ref.1) | copy-start | bytes 52
  28.3 0.8 copy-start.2
  29.8 0.6 copy-start.5
  51.9 23.5 %copy-start.6 = (bf16[128,256]{1,0:T(8,128)(2,1)S(1)}, bf16[128,256]{1,0:T(8,128)(2,1)}, u32[]{:S(2)}) copy-start(bf16[128,256]{1,0:T(8,128)(2,1)} %copy-done.5) | copy-start | bytes 196612
  57.9 17.5 %all-to-all-start.1 = ((f32[16,40,128]{2,1,0:T(8,128)}), f32[16,40,128]{2,1,0:T(8,128)S(1)}, u32[]{:S(2)}, u32[]{:S(2)}) async-start(f32[16,40,128]{2,1,0:T(8,128)} %bitcast.24), calls=%async_computation.1 | async-start | bytes 655360 | tf_op jit(solution)/shard_map/all_to_all | solution.py:840
  61.5 4.1 %collective-permute-start = (f32[376,128]{1,0:T(8,128)}, f32[376,128]{1,0:T(8,128)S(1)}, u32[]{:S(2)}, u32[]{:S(2)}) collective-permute-start(f32[376,128]{1,0:T(8,128)} %get-tuple-element.24), channel_id=1, source_target_pairs={{0,1},{1,2},{2,3},{3,4},{4,5},{5,6},{6,7},{7,0},{8,9},{9,10},{10,1... | collective-permute-start | bytes 577544 | tf_op jit(solution)/shard_map/ppermute | solution.py:801
  62.7 5.6 %collective-permute-start.1 = (f32[376,128]{1,0:T(8,128)}, f32[376,128]{1,0:T(8,128)S(1)}, u32[]{:S(2)}, u32[]{:S(2)}) collective-permute-start(f32[376,128]{1,0:T(8,128)} %get-tuple-element.25), channel_id=1, source_target_pairs={{1,0},{2,1},{3,2},{4,3},{5,4},{6,5},{7,6},{0,7},{9,8},{10,9},{11,1... | collective-permute-start | bytes 577544 | tf_op jit(solution)/shard_map/ppermute | solution.py:802
  70.3 13.2 %collective-permute-start.2 = (f32[376,128]{1,0:T(8,128)}, f32[376,128]{1,0:T(8,128)S(1)}, u32[]{:S(2)}, u32[]{:S(2)}) collective-permute-start(f32[376,128]{1,0:T(8,128)} %get-tuple-element.28), channel_id=1, source_target_pairs={{0,8},{8,16},{16,24},{24,32},{32,40},{40,48},{48,56},{56,64},{64,7... | collective-permute-start | bytes 577544 | tf_op jit(solution)/shard_map/ppermute | solution.py:801
  71.9 11.6 %collective-permute-start.3 = (f32[376,128]{1,0:T(8,128)}, f32[376,128]{1,0:T(8,128)S(1)}, u32[]{:S(2)}, u32[]{:S(2)}) collective-permute-start(f32[376,128]{1,0:T(8,128)} %get-tuple-element.29), channel_id=1, source_target_pairs={{8,0},{16,8},{24,16},{32,24},{40,32},{48,40},{56,48},{64,56},{72,6... | collective-permute-start | bytes 577544 | tf_op jit(solution)/shard_map/ppermute | solution.py:802
  76.9 11.9 %all-to-all-start.2 = ((f32[8,8,640]{2,1,0:T(8,128)}), f32[8,8,640]{2,1,0:T(8,128)S(1)}, u32[]{:S(2)}, u32[]{:S(2)}) async-start(f32[8,8,640]{2,1,0:T(8,128)} %bitcast.10), calls=%async_computation.2 | async-start | bytes 327680 | tf_op jit(solution)/shard_map/all_to_all | solution.py:850

commit v7 on v6

--- a/solution.py
+++ b/solution.py
@@ -131,17 +131,18 @@
     )
     source = found * 64.0 + pltpu.roll(found, 128 - CAP, 1)
     source_s[...] = pltpu.roll(source, 64, 1).astype(jnp.int32)
-    (source_copy,) = started([(source_s, source_smem)], sems, 1)
+    quarters = [pl.ds(part * 32, 32) for part in range(4)]
+    source_copies = started([(source_s.at[at], source_smem.at[at]) for at in quarters], sems, 5)
     lane = lax.broadcasted_iota(jnp.int32, (128, 128), 1)
     ids = jnp.where(lane < CAP, found * 16.0 + pltpu.roll(found, 128 - CAP, 1), 0.0)
     ids = pltpu.roll(ids, info_ref[1], 1)
     for d in range(DEVICES):
         at = d * ROWS + CAP
         out_s[at : at + 1, :] = ids[d : d + 1]
-    source_copy.wait()
     data_copy.wait()
     copies = []
     for part in range(4):
+        source_copies[part].wait()
 
         def body(n, carry):
             for q in range(4):
@@ -152,7 +153,7 @@
 
         lax.fori_loop(0, 8, body, 0)
         at = pl.ds(part * 32 * ROWS, 32 * ROWS)
-        copies += started([(out_s.at[at], out_ref.at[at])], sems, 2 + part)
+        copies += started([(out_s.at[at], out_ref.at[at])], sems, 1 + part)
     for copy in copies:
         copy.wait()
 
@@ -170,7 +171,7 @@
             pltpu.VMEM((128, 4096), BF16),
             pltpu.VMEM((128, 128), jnp.int32),
             pltpu.SMEM((128, 128), jnp.int32),
-            pltpu.SemaphoreType.DMA((6,)),
+            pltpu.SemaphoreType.DMA((9,)),
         ],
         outs=HB,
         limit=20,
@@ -251,7 +252,8 @@
     thin_z_ref, thin_y_ref, top_rows_ref, top_z_ref = refs[-10:-6]
     fine_ref, mid_ref, low_ref, high_ref, top_ref, sems = refs[-6:]
     table_copies = started(list(zip(tables, refs[-10:-6])), sems)
-    for c in range(DEVICES // 4):
+
+    def unpack(c):
         total = None
         for j in range(4):
             base = (c * 4 + j) * ROWS
@@ -262,13 +264,17 @@
             line = in_ref[base + CAP : base + CAP + 1, :]
             total = line if total is None else total + line
         ids_s[c : c + 1, :] = total.astype(jnp.int32)
+
     rows = lax.broadcasted_iota(jnp.int32, (256, 128), 0).astype(F32).astype(BF16)
     one, zero = jnp.ones((256, 128), BF16), jnp.zeros((256, 128), BF16)
 
     def block(b, carry):
-        first = pl.multiple_of(b * 512, 512)
+        first = b * 512 if isinstance(b, int) else pl.multiple_of(b * 512, 512)
         acc = [jnp.zeros((256, 256), F32)] * 2
         for k in range(16):
+            if isinstance(b, int):
+                unpack(2 * k)
+                unpack(2 * k + 1)
             for m in range(2):
                 parts = []
                 for q in range(2):
@@ -280,10 +286,12 @@
                 acc[m] = acc[m] + mm(hit, data_s[k * 256 : (k + 1) * 256, :])
         for m in range(2):
             value = acc[m][:, :128] + acc[m][:, 128:]
-            fine_ref[pl.ds(pl.multiple_of(first + m * 256, 256), 256), :] = value
+            at = first + m * 256
+            fine_ref[pl.ds(at if isinstance(b, int) else pl.multiple_of(at, 256), 256), :] = value
         return carry
 
-    lax.fori_loop(0, 3, block, 0)
+    block(0, 0)
+    lax.fori_loop(1, 3, block, 0)
     out_copies = started([(fine_ref, outs[0])], sems, 4)
     for i in range(17):
         total = None
@@ -753,7 +761,7 @@
 def finish_kernel(
     near_ref, mid_ref, top_ref, *refs
 ):
-    grow_ref, out_ref, grown_s = refs
+    grow_ref, out_hbm, grown_s, out_ref, sems = refs
     grow_top, grow_z = grow_ref[:128, :], grow_ref[128:256, :]
     grow_fine, grow_y = grow_ref[256:, :128], grow_ref[256:272, 128:]
     total = top_ref[:8, :]
@@ -785,6 +793,7 @@
     for g in range(3):
         part = exact_right(jnp.concatenate(slabs[g * 8 : (g + 1) * 8], axis=0), grow_z)
         grown_s[g * 192 : (g + 1) * 192, :] = exact_left(grow_fine, part)
+    copies = []
     for x in range(CX):
         at = slice(x * CY, (x + 1) * CY)
         i = x // 2
@@ -792,6 +801,11 @@
         if x % 2:
             value = 0.5 * (value + grown_s[(i + 1) * CY : (i + 2) * CY, :])
         out_ref[at, :] = near_ref[at, :] + value
+        if x % 8 == 7:
+            at = pl.ds((x - 7) * CY, 8 * CY)
+            copies += started([(out_ref.at[at], out_hbm.at[at])], sems, x // 8)
+    for copy in copies:
+        copy.wait()
 
 
 def swap(to_low, to_high, axis):
@@ -877,7 +891,15 @@
         limit=14,
     )(own, before, behind, zf, yf, *tables, grow)
     out = call(
-        finish_kernel, array(CX * CY, NZ), [VM] * 4, [pltpu.VMEM((24 * CY, NZ), F32)]
+        finish_kernel,
+        array(CX * CY, NZ),
+        [VM] * 4,
+        [
+            pltpu.VMEM((24 * CY, NZ), F32),
+            pltpu.VMEM((CX * CY, NZ), F32),
+            pltpu.SemaphoreType.DMA((4,)),
+        ],
+        outs=HB,
     )(near, mid_near, partial, grow)
     return out.reshape(CX, CY, NZ)
 

time: 91.1 us -> 90.1 us (0.989)
  Pallas kernels: 28.4 us -> 27.3 us
    pallas_call x10, Pallas kernels: 28.4 us -> 27.3 us  [run(): return kernel(*placed)]
where the time goes in v7:
time: 90.1 us; the launch traced here: 89.6 us
  Pallas kernels  27.3 us (30%)
  starting transfers between devices  26.8 us (30%)
  waiting for transfers between devices  26.8 us (30%)
  local copies, waits for them, and re-layouts  6.32 us (7%)
  other arithmetic  1.19 us (1%)
  between operations  1.13 us (1%)
    pallas_call x10, Pallas kernels, run(): return kernel(*placed)  27.3 us
    all_to_all x1, waiting for transfers between devices, on_device(): lax.all_to_all(outgoing.reshape(DEVICES, 1, ROWS * 128), ('gx', 'gy'), sp...  21.4 us
    all_to_all x1, starting transfers between devices, on_device(): lax.all_to_all(outgoing.reshape(DEVICES, 1, ROWS * 128), ('gx', 'gy'), sp...  11.5 us
    all_to_all x1, starting transfers between devices, on_device(): lax.all_to_all(partial.reshape(SIZE_Y, 8, 640), 'gy', split_axis=0, conca...  5.3 us
    ppermute x2, starting transfers between devices, swap(): behind = lax.ppermute(to_low, axis, backward)  3.67 us
    all_to_all x1, starting transfers between devices, on_device(): lax.all_to_all(top.reshape(SIZE_X, TOP_ROWS, 128), 'gx', split_axis=0, co...  3.59 us
    unnamed x24, local copies, waits for them, and re-layouts  2.95 us
    ppermute x2, starting transfers between devices, swap(): before = lax.ppermute(to_high, axis, forward)  2.8 us
  transfers between devices with their start and end apart: 7, of which 3 were waited for; matrix products, arithmetic and copies ran while one was open for 5% of the time, Pallas kernels for 14%

profile of v7, /device:TPU:1, one launch (start us, length us, event | category | flops | bytes accessed | tf_op | source)
XLA Modules:
  0.0 89.6 jit_solution(10325262167673082939)
XLA Ops:
  1.5 7.3 %shard_map.172.after_ref = f32[4224,128]{1,0:T(8,128)} custom-call(s32[32,128]{1,0:T(8,128)S(1)} %bitcast.20, s32[4]{0:T(128)S(1)} %pad_add_fusion.info_ref, f32[4096,128]{1,0:T(8,128)} %data_ref.1), custom_call_target="tpu_custom_call" | custom-call | tf_op jit(solution)/shard_map/pallas_call | solution.py:53
  8.8 11.5 %all-to-all-start = ((f32[128,1,4224]{2,1,0:T(1,128)}), f32[128,1,4224]{2,1,0:T(1,128)S(1)}, u32[]{:S(2)}, u32[]{:S(2)}) async-start(f32[128,1,4224]{2,1,0:T(1,128)} %bitcast.21), calls=%async_computation | async-start | bytes 4325376 | tf_op jit(solution)/shard_map/all_to_all | solution.py:829
  21.1 0.8 slice.49
  21.9 0.8 slice.51
  22.7 1.2 %concatenate.25 = f32[9,32,256]{2,1,0:T(8,128)S(1)} concatenate(f32[9,32,5]{2,1,0:T(8,128)} %slice.51, f32[9,32,119]{2,1,0:T(8,128)S(1)} %broadcast_in_dim.7, f32[9,32,9]{2,1,0:T(8,128)S(1)} %get-tuple-element.37, f32[9,32,119]{2,1,0:T(8,128)S(1)} %broadcast_in_dim.7, f32[9,32,4]{2,1,0:T(8,128)S(1)} %bitcast.22), dimensions={2} | concatenate | bytes 589824 | tf_op jit(solution)/shard_map/concatenate | solution.py:563
  23.9 1.0 %pad_maximum_fusion = f32[9,32,256]{2,1,0:T(8,128)S(1)} fusion(f32[9,32,4]{2,1,0:T(8,128)S(1)} %bitcast.23, f32[9,32,5]{2,1,0:T(8,128)} %slice.49, f32[256]{0:T(256)S(1)} %pad.6.clone), kind=kLoop, calls=%fused_computation | loop fusion | flops 147456 | bytes 306304 | tf_op jit(solution)/shard_map/concatenate | solution.py:560
  25.0 0.9 shard_map.174.refs_5_
  25.9 0.8 copy-done.1
  26.7 0.9 shard_map.173.refs_4_
  27.6 0.8 copy-done.2
  29.7 21.4 %all-to-all-done = f32[128,1,4224]{2,1,0:T(1,128)S(1)} async-done(((f32[128,1,4224]{2,1,0:T(1,128)}), f32[128,1,4224]{2,1,0:T(1,128)S(1)}, u32[]{:S(2)}, u32[]{:S(2)}) %all-to-all-start) | async-done | bytes 2162720 | tf_op jit(solution)/shard_map/all_to_all | solution.py:829
  51.1 5.7 %shard_map.176 = (f32[1536,128]{1,0:T(8,128)}, f32[384,128]{1,0:T(8,128)}, f32[376,128]{1,0:T(8,128)}, f32[376,128]{1,0:T(8,128)}, f32[640,128]{1,0:T(8,128)}) custom-call(f32[4224,128]{1,0:T(8,128)S(1)} %bitcast.15, bf16[256,128]{1,0:T(8,128)(2,1)} %constant.56.clone.refs_0_, bf16[128,192]{1,0:T(8,128)(2,1)} %constant.57.clone.refs_1_, ...), custom_call_target="tpu_custom_call" | custom-call | tf_op jit(solution)/shard_map/pallas_call | solution.py:53
  56.8 3.6 %all-to-all-start.1 = ((f32[16,40,128]{2,1,0:T(8,128)}), f32[16,40,128]{2,1,0:T(8,128)S(1)}, u32[]{:S(2)}, u32[]{:S(2)}) async-start(f32[16,40,128]{2,1,0:T(8,128)} %bitcast.24), calls=%async_computation.1 | async-start | bytes 655360 | tf_op jit(solution)/shard_map/all_to_all | solution.py:854
  60.4 1.2 %collective-permute-start = (f32[376,128]{1,0:T(8,128)}, f32[376,128]{1,0:T(8,128)S(1)}, u32[]{:S(2)}, u32[]{:S(2)}) collective-permute-start(f32[376,128]{1,0:T(8,128)} %get-tuple-element.24), channel_id=1, source_target_pairs={{0,1},{1,2},{2,3},{3,4},{4,5},{5,6},{6,7},{7,0},{8,9},{9,10},{10,1... | collective-permute-start | bytes 577544 | tf_op jit(solution)/shard_map/ppermute | solution.py:815
  61.8 2.7 %collective-permute-done.before_ref = f32[376,128]{1,0:T(8,128)S(1)} collective-permute-done((f32[376,128]{1,0:T(8,128)}, f32[376,128]{1,0:T(8,128)S(1)}, u32[]{:S(2)}, u32[]{:S(2)}) %collective-permute-start) | collective-permute-done | bytes 192544 | tf_op jit(solution)/shard_map/ppermute | solution.py:815
  64.5 2.7 %collective-permute-done.1.behind_ref = f32[376,128]{1,0:T(8,128)S(1)} collective-permute-done((f32[376,128]{1,0:T(8,128)}, f32[376,128]{1,0:T(8,128)S(1)}, u32[]{:S(2)}, u32[]{:S(2)}) %collective-permute-start.1) | collective-permute-done | bytes 192544 | tf_op jit(solution)/shard_map/ppermute | solution.py:816
  67.2 2.1 %shard_map.177 = (f32[1536,128]{1,0:T(8,128)S(1)}, f32[512,128]{1,0:T(8,128)S(1)}, f32[768,128]{1,0:T(8,128)}, f32[376,128]{1,0:T(8,128)}, f32[376,128]{1,0:T(8,128)}) custom-call(f32[1536,128]{1,0:T(8,128)} %get-tuple-element.22.fine_hbm, f32[384,128]{1,0:T(8,128)} %get-tuple-element.23.mid_hbm, f32[376,128]{1,0:T(8,128)S(1)} %collective-permute-done.before_ref, ...), custom_call_target="tpu_custom_call" | custom-call | tf_op jit(solution)/shard_map/pallas_call | solution.py:53
  69.2 1.6 %collective-permute-start.2 = (f32[376,128]{1,0:T(8,128)}, f32[376,128]{1,0:T(8,128)S(1)}, u32[]{:S(2)}, u32[]{:S(2)}) collective-permute-start(f32[376,128]{1,0:T(8,128)} %get-tuple-element.28), channel_id=1, source_target_pairs={{0,8},{8,16},{16,24},{24,32},{32,40},{40,48},{48,56},{56,64},{64,7... | collective-permute-start | bytes 577544 | tf_op jit(solution)/shard_map/ppermute | solution.py:815
  70.8 3.5 %collective-permute-start.3 = (f32[376,128]{1,0:T(8,128)}, f32[376,128]{1,0:T(8,128)S(1)}, u32[]{:S(2)}, u32[]{:S(2)}) collective-permute-start(f32[376,128]{1,0:T(8,128)} %get-tuple-element.29), channel_id=1, source_target_pairs={{8,0},{16,8},{24,16},{32,24},{40,32},{48,40},{56,48},{64,56},{72,6... | collective-permute-start | bytes 577544 | tf_op jit(solution)/shard_map/ppermute | solution.py:816
  74.3 1.5 %shard_map.180 = f32[64,640]{1,0:T(8,128)} custom-call(f32[640,128]{1,0:T(8,128)S(1)} %bitcast.18, bf16[128,256]{1,0:T(8,128)(2,1)S(1)} %copy-done.6, bf16[128,128]{1,0:T(8,128)(2,1)S(1)} %get-tuple-element.34.y_ref, bf16[1024,128]{1,0:T(8,128)(2,1)S(1)} %get-tuple-element.35.z_ref), custom_call_target="tpu_custom_call" | custom-call | tf_op jit(solution)/shard_map/pallas_call | solution.py:53
  75.8 5.3 %all-to-all-start.2 = ((f32[8,8,640]{2,1,0:T(8,128)}), f32[8,8,640]{2,1,0:T(8,128)S(1)}, u32[]{:S(2)}, u32[]{:S(2)}) async-start(f32[8,8,640]{2,1,0:T(8,128)} %bitcast.10), calls=%async_computation.2 | async-start | bytes 327680 | tf_op jit(solution)/shard_map/all_to_all | solution.py:864
  81.1 1.3 %shard_map.178.own_ref = f32[2048,128]{1,0:T(8,128)S(1)} custom-call(f32[1536,128]{1,0:T(8,128)S(1)} %get-tuple-element.26.fine_s, f32[512,128]{1,0:T(8,128)S(1)} %get-tuple-element.27.halo_s, bf16[512,256]{1,0:T(8,128)(2,1)S(1)} %copy-done.3, bf16[256,512]{1,0:T(8,128)(2,1)S(1)} %copy-done), custom_call_target="tpu_custom_call" | custom-call | tf_op jit(solution)/shard_map/pallas_call | solution.py:53
  82.5 5.2 %shard_map.179 = (f32[768,256]{1,0:T(8,128)S(1)}, f32[144,256]{1,0:T(8,128)S(1)}, bf16[448,256]{1,0:T(8,128)(2,1)S(1)}) custom-call(f32[2048,128]{1,0:T(8,128)S(1)} %shard_map.178.own_ref, f32[376,128]{1,0:T(8,128)S(1)} %collective-permute-done.2.before_ref, f32[376,128]{1,0:T(8,128)S(1)} %collective-permute-done.3.behind_ref, ...), custom_call_target="tpu_custom_call" | custom-call | tf_op jit(solution)/shard_map/pallas_call | solution.py:53
  87.7 1.7 %shard_map.181 = f32[768,256]{1,0:T(8,128)} custom-call(f32[768,256]{1,0:T(8,128)S(1)} %get-tuple-element.31.near_ref, f32[144,256]{1,0:T(8,128)S(1)} %get-tuple-element.32.mid_ref, f32[64,640]{1,0:T(8,128)S(1)} %bitcast.19, bf16[448,256]{1,0:T(8,128)(2,1)S(1)} %get-tuple-element.36.refs_0_), custom_call_target="tpu_custom_call" | custom-call | tf_op jit(solution)/shard_map/pallas_call | solution.py:53
  (47 shorter events, 3.2 us)
Async XLA Ops:
  0.7 0.7 copy-start.7
  8.8 11.5 %copy-start.10 = (f32[9,9,9]{2,1,0:T(8,128)S(1)}, f32[9,9,9]{2,1,0:T(8,128)}, u32[]{:S(2)}) copy-start(f32[9,9,9]{2,1,0:T(8,128)} %param.21) | copy-start | bytes 8752
  8.8 11.6 %copy-start.11 = (f32[9,9,9]{2,1,0:T(8,128)S(1)}, f32[9,9,9]{2,1,0:T(8,128)}, u32[]{:S(2)}) copy-start(f32[9,9,9]{2,1,0:T(8,128)} %param.22) | copy-start | bytes 8752
  8.8 12.0 %slice-start = ((f32[9,9,9]{2,1,0:T(8,128)}), f32[9,5,9]{2,1,0:T(8,128)S(1)}, s32[]{:S(2)}) async-start(f32[9,9,9]{2,1,0:T(8,128)} %param.21), calls=%async_computation.3 | async-start | bytes 73728 | tf_op jit(solution)/shard_map/slice | solution.py:557
  8.8 12.1 %slice-start.1 = ((f32[9,9,9]{2,1,0:T(8,128)}), f32[9,5,9]{2,1,0:T(8,128)S(1)}, s32[]{:S(2)}) async-start(f32[9,9,9]{2,1,0:T(8,128)} %param.22), calls=%async_computation.4 | async-start | bytes 73728 | tf_op jit(solution)/shard_map/slice | solution.py:557
  8.8 42.3 %all-to-all-start = ((f32[128,1,4224]{2,1,0:T(1,128)}), f32[128,1,4224]{2,1,0:T(1,128)S(1)}, u32[]{:S(2)}, u32[]{:S(2)}) async-start(f32[128,1,4224]{2,1,0:T(1,128)} %bitcast.21), calls=%async_computation | async-start | bytes 4325376 | tf_op jit(solution)/shard_map/all_to_all | solution.py:829
  21.0 4.0 %copy-start = (bf16[256,512]{1,0:T(8,128)(2,1)S(1)}, bf16[256,512]{1,0:T(8,128)(2,1)}, u32[]{:S(2)}) copy-start(bf16[256,512]{1,0:T(8,128)(2,1)} %constant.54.clone.y_ref.refs_1_) | copy-start | bytes 786436
  21.0 4.0 %copy-start.4 = (bf16[512,256]{1,0:T(8,128)(2,1)S(1)}, bf16[512,256]{1,0:T(8,128)(2,1)}, u32[]{:S(2)}) copy-start(bf16[512,256]{1,0:T(8,128)(2,1)} %constant.55.clone.z_ref.refs_3_) | copy-start | bytes 786436
  24.9 1.8 %copy-start.3 = (bf16[512,256]{1,0:T(8,128)(2,1)S(1)}, bf16[512,256]{1,0:T(8,128)(2,1)}, u32[]{:S(2)}) copy-start(bf16[512,256]{1,0:T(8,128)(2,1)} %constant.53.clone.z_ref.refs_0_) | copy-start | bytes 786436
  25.9 0.8 copy-start.1
  26.6 1.7 %copy-start.8 = (f32[4]{0:T(128)S(1)}, f32[4]{0:T(128)}, u32[]{:S(2)}) copy-start(f32[4]{0:T(128)} %weights_ref.1) | copy-start | bytes 52
  26.6 1.7 %copy-start.9 = (f32[4]{0:T(128)S(1)}, f32[4]{0:T(128)}, u32[]{:S(2)}) copy-start(f32[4]{0:T(128)} %widths_ref.1) | copy-start | bytes 52
  27.5 0.8 copy-start.2
  29.1 0.6 copy-start.5
  51.1 23.2 %copy-start.6 = (bf16[128,256]{1,0:T(8,128)(2,1)S(1)}, bf16[128,256]{1,0:T(8,128)(2,1)}, u32[]{:S(2)}) copy-start(bf16[128,256]{1,0:T(8,128)(2,1)} %copy-done.5) | copy-start | bytes 196612
  56.8 17.5 %all-to-all-start.1 = ((f32[16,40,128]{2,1,0:T(8,128)}), f32[16,40,128]{2,1,0:T(8,128)S(1)}, u32[]{:S(2)}, u32[]{:S(2)}) async-start(f32[16,40,128]{2,1,0:T(8,128)} %bitcast.24), calls=%async_computation.1 | async-start | bytes 655360 | tf_op jit(solution)/shard_map/all_to_all | solution.py:854
  60.4 4.1 %collective-permute-start = (f32[376,128]{1,0:T(8,128)}, f32[376,128]{1,0:T(8,128)S(1)}, u32[]{:S(2)}, u32[]{:S(2)}) collective-permute-start(f32[376,128]{1,0:T(8,128)} %get-tuple-element.24), channel_id=1, source_target_pairs={{0,1},{1,2},{2,3},{3,4},{4,5},{5,6},{6,7},{7,0},{8,9},{9,10},{10,1... | collective-permute-start | bytes 577544 | tf_op jit(solution)/shard_map/ppermute | solution.py:815
  61.6 5.6 %collective-permute-start.1 = (f32[376,128]{1,0:T(8,128)}, f32[376,128]{1,0:T(8,128)S(1)}, u32[]{:S(2)}, u32[]{:S(2)}) collective-permute-start(f32[376,128]{1,0:T(8,128)} %get-tuple-element.25), channel_id=1, source_target_pairs={{1,0},{2,1},{3,2},{4,3},{5,4},{6,5},{7,6},{0,7},{9,8},{10,9},{11,1... | collective-permute-start | bytes 577544 | tf_op jit(solution)/shard_map/ppermute | solution.py:816
  69.2 13.2 %collective-permute-start.2 = (f32[376,128]{1,0:T(8,128)}, f32[376,128]{1,0:T(8,128)S(1)}, u32[]{:S(2)}, u32[]{:S(2)}) collective-permute-start(f32[376,128]{1,0:T(8,128)} %get-tuple-element.28), channel_id=1, source_target_pairs={{0,8},{8,16},{16,24},{24,32},{32,40},{40,48},{48,56},{56,64},{64,7... | collective-permute-start | bytes 577544 | tf_op jit(solution)/shard_map/ppermute | solution.py:815
  70.8 11.6 %collective-permute-start.3 = (f32[376,128]{1,0:T(8,128)}, f32[376,128]{1,0:T(8,128)S(1)}, u32[]{:S(2)}, u32[]{:S(2)}) collective-permute-start(f32[376,128]{1,0:T(8,128)} %get-tuple-element.29), channel_id=1, source_target_pairs={{8,0},{16,8},{24,16},{32,24},{40,32},{48,40},{56,48},{64,56},{72,6... | collective-permute-start | bytes 577544 | tf_op jit(solution)/shard_map/ppermute | solution.py:816
  75.8 11.9 %all-to-all-start.2 = ((f32[8,8,640]{2,1,0:T(8,128)}), f32[8,8,640]{2,1,0:T(8,128)S(1)}, u32[]{:S(2)}, u32[]{:S(2)}) async-start(f32[8,8,640]{2,1,0:T(8,128)} %bitcast.10), calls=%async_computation.2 | async-start | bytes 327680 | tf_op jit(solution)/shard_map/all_to_all | solution.py:864

commit v8 on v7

--- a/solution.py
+++ b/solution.py
@@ -247,11 +247,12 @@
 
 def collect_kernel(in_ref, *refs):
     tables = refs[:4]
-    outs = refs[-18:-13]
-    data_s, ids_s, slab_s = refs[-13:-10]
-    thin_z_ref, thin_y_ref, top_rows_ref, top_z_ref = refs[-10:-6]
-    fine_ref, mid_ref, low_ref, high_ref, top_ref, sems = refs[-6:]
-    table_copies = started(list(zip(tables, refs[-10:-6])), sems)
+    outs = refs[-15:-13]
+    low_ref, high_ref, top_ref = refs[-13:-10]
+    data_s, ids_s, slab_s = refs[-10:-7]
+    thin_z_ref, thin_y_ref, top_rows_ref, top_z_ref = refs[-7:-3]
+    fine_ref, mid_ref, sems = refs[-3:]
+    table_copies = started(list(zip(tables, refs[-7:-3])), sems)
 
     def unpack(c):
         total = None
@@ -313,6 +314,7 @@
     for g in range(3):
         part = exact_right(slab_s[g * 192 : (g + 1) * 192, :], thin_z_ref)
         mid_ref[g * 128 : (g + 1) * 128, :] = exact_left(thin_y_ref, part)
+    out_copies += started([(mid_ref, outs[1])], sems, 5)
     for h in range(2):
         for c in range(4):
             at = slice((h * 4 + c) * CX, (h * 4 + c + 1) * CX)
@@ -322,13 +324,11 @@
         at = slice(256 + j * 24, 256 + (j + 1) * 24)
         low_ref[at, :] = mid_ref[pl.ds(j, 24, stride=16), :]
         high_ref[at, :] = mid_ref[pl.ds(8 + j, 24, stride=16), :]
-    out_copies += started([(mid_ref, outs[1]), (low_ref, outs[2]), (high_ref, outs[3])], sems, 5)
     stacked = exact_left(top_rows_ref, mid_ref[: 17 * 16, :])
     pair = jnp.concatenate([stacked[:TOP_ROWS], stacked[TOP_ROWS:]], axis=1)
     top_charge = exact_right(pair, top_z_ref)
     for s in range(SIZE_X):
         top_ref[s * TOP_ROWS : (s + 1) * TOP_ROWS, :] = top_charge
-    out_copies += started([(top_ref, outs[4])], sems, 8)
     for copy in out_copies:
         copy.wait()
 
@@ -356,17 +356,17 @@
             pltpu.VMEM((DEVICES // 4, 128), jnp.int32),
             pltpu.VMEM((24 * CY, NZ), F32),
             *buffers(*tables),
-            *buffers(*out),
-            pltpu.SemaphoreType.DMA((9,)),
+            *buffers(*out[:2]),
+            pltpu.SemaphoreType.DMA((6,)),
         ],
-        outs=HB,
+        outs=(HB, HB, VM, VM, VM),
         limit=20,
     )(arrived, *tables, *after)
 
 
 def merge_kernel(
-    fine_hbm, mid_hbm, before_ref, behind_ref, fine_s, halo_ref, wide_hbm, low_hbm, high_hbm,
-    mid_ref, wide_ref, low_ref, high_ref, sems,
+    fine_hbm, mid_hbm, before_ref, behind_ref, fine_s, halo_ref, wide_hbm, low_ref, high_ref,
+    mid_ref, wide_ref, sems,
 ):
     mid_copy, fine_copy = started([(mid_hbm, mid_ref), (fine_hbm, fine_s)], sems)
     for h in range(2):
@@ -407,7 +407,6 @@
             ref[at + 16 : at + 24, :] = (
                 wide_ref[base + 16 : base + 24, :] + wide_ref[base + 24 : base + 32, :]
             )
-    out_copies += started([(low_ref, low_hbm), (high_ref, high_hbm)], sems, 3)
     for copy in out_copies:
         copy.wait()
 
@@ -426,10 +425,10 @@
         [HB, HB, VM, VM],
         [
             pltpu.VMEM((24 * 16, 128), F32),
-            *buffers(*out[2:]),
-            pltpu.SemaphoreType.DMA((5,)),
+            *buffers(out[2]),
+            pltpu.SemaphoreType.DMA((3,)),
         ],
-        outs=(VM, VM, HB, HB, HB),
+        outs=(VM, VM, HB, VM, VM),
     )(fine, mid, before, behind)
 
 
@@ -731,14 +730,18 @@
 
 def top_kernel(in_ref, x_ref, y_ref, z_ref, out_ref, plane_s, depth_s):
     left = (x_ref[:64, :], x_ref[64:, :])
+    columns = []
     for jp in range(4):
         tiles = [in_ref[s * TOP_ROWS + jp * 8 : s * TOP_ROWS + jp * 8 + 8, :] for s in range(16)]
         tiles.append(in_ref[pl.ds(32 + jp, SIZE_X, stride=TOP_ROWS), :])
         tiles.append(jnp.zeros((112, 128), F32))
-        right = halves(jnp.concatenate(tiles, axis=0))
-        plane = mm(left[0], right[0]) + mm(left[0], right[1]) + mm(left[1], right[0])
+        columns.append(jnp.concatenate(tiles, axis=0))
+    right = halves(jnp.concatenate(columns, axis=1))
+    plane = mm(left[0], right[0]) + mm(left[0], right[1]) + mm(left[1], right[0])
+    for jp in range(4):
         for k in range(4):
-            plane_s[(k * 4 + jp) * 16 : (k * 4 + jp + 1) * 16, :] = plane[k * 16 : (k + 1) * 16]
+            part = plane[k * 16 : (k + 1) * 16, jp * 128 : (jp + 1) * 128]
+            plane_s[(k * 4 + jp) * 16 : (k * 4 + jp + 1) * 16, :] = part
     for k in range(4):
         weight = [z_ref[(n * 4 + k) * 128 : (n * 4 + k + 1) * 128, :] for n in range(2)]
         value = halves(plane_s[k * 64 : (k + 1) * 64, :])

time: 90.1 us -> 90 us (level)
  no operation moved by 1% of the time
where the time goes in v8:
time: 90 us; the launch traced here: 89.5 us
  Pallas kernels  27.4 us (30%)
  starting transfers between devices  26.8 us (30%)
  waiting for transfers between devices  26.6 us (30%)
  local copies, waits for them, and re-layouts  6.32 us (7%)
  other arithmetic  1.19 us (1%)
  between operations  1.13 us (1%)
    pallas_call x10, Pallas kernels, run(): return kernel(*placed)  27.4 us
    all_to_all x1, waiting for transfers between devices, on_device(): lax.all_to_all(outgoing.reshape(DEVICES, 1, ROWS * 128), ('gx', 'gy'), sp...  21.4 us
    all_to_all x1, starting transfers between devices, on_device(): lax.all_to_all(outgoing.reshape(DEVICES, 1, ROWS * 128), ('gx', 'gy'), sp...  11.5 us
    all_to_all x1, starting transfers between devices, on_device(): lax.all_to_all(partial.reshape(SIZE_Y, 8, 640), 'gy', split_axis=0, conca...  5.3 us
    ppermute x2, starting transfers between devices, swap(): behind = lax.ppermute(to_low, axis, backward)  3.68 us
    all_to_all x1, starting transfers between devices, on_device(): lax.all_to_all(top.reshape(SIZE_X, TOP_ROWS, 128), 'gx', split_axis=0, co...  3.58 us
    unnamed x24, local copies, waits for them, and re-layouts  2.95 us
    ppermute x2, starting transfers between devices, swap(): before = lax.ppermute(to_high, axis, forward)  2.79 us
  transfers between devices with their start and end apart: 7, of which 3 were waited for; matrix products, arithmetic and copies ran while one was open for 5% of the time, Pallas kernels for 14%

profile of v8, /device:TPU:1, one launch (start us, length us, event | category | flops | bytes accessed | tf_op | source)
XLA Modules:
  0.0 89.5 jit_solution(12692038943663856268)
XLA Ops:
  1.5 7.3 %shard_map.172.after_ref = f32[4224,128]{1,0:T(8,128)} custom-call(s32[32,128]{1,0:T(8,128)S(1)} %bitcast.20, s32[4]{0:T(128)S(1)} %pad_add_fusion.info_ref, f32[4096,128]{1,0:T(8,128)} %data_ref.1), custom_call_target="tpu_custom_call" | custom-call | tf_op jit(solution)/shard_map/pallas_call | solution.py:53
  8.8 11.5 %all-to-all-start = ((f32[128,1,4224]{2,1,0:T(1,128)}), f32[128,1,4224]{2,1,0:T(1,128)S(1)}, u32[]{:S(2)}, u32[]{:S(2)}) async-start(f32[128,1,4224]{2,1,0:T(1,128)} %bitcast.21), calls=%async_computation | async-start | bytes 4325376 | tf_op jit(solution)/shard_map/all_to_all | solution.py:832
  21.1 0.8 slice.49
  21.9 0.8 slice.51
  22.7 1.2 %concatenate.25 = f32[9,32,256]{2,1,0:T(8,128)S(1)} concatenate(f32[9,32,5]{2,1,0:T(8,128)} %slice.51, f32[9,32,119]{2,1,0:T(8,128)S(1)} %broadcast_in_dim.7, f32[9,32,9]{2,1,0:T(8,128)S(1)} %get-tuple-element.37, f32[9,32,119]{2,1,0:T(8,128)S(1)} %broadcast_in_dim.7, f32[9,32,4]{2,1,0:T(8,128)S(1)} %bitcast.22), dimensions={2} | concatenate | bytes 589824 | tf_op jit(solution)/shard_map/concatenate | solution.py:562
  23.9 1.0 %pad_maximum_fusion = f32[9,32,256]{2,1,0:T(8,128)S(1)} fusion(f32[9,32,4]{2,1,0:T(8,128)S(1)} %bitcast.23, f32[9,32,5]{2,1,0:T(8,128)} %slice.49, f32[256]{0:T(256)S(1)} %pad.6.clone), kind=kLoop, calls=%fused_computation | loop fusion | flops 147456 | bytes 306304 | tf_op jit(solution)/shard_map/concatenate | solution.py:559
  25.0 0.9 shard_map.174.refs_5_
  25.9 0.8 copy-done.1
  26.7 0.9 shard_map.173.refs_4_
  27.6 0.8 copy-done.2
  29.7 21.4 %all-to-all-done = f32[128,1,4224]{2,1,0:T(1,128)S(1)} async-done(((f32[128,1,4224]{2,1,0:T(1,128)}), f32[128,1,4224]{2,1,0:T(1,128)S(1)}, u32[]{:S(2)}, u32[]{:S(2)}) %all-to-all-start) | async-done | bytes 2162720 | tf_op jit(solution)/shard_map/all_to_all | solution.py:832
  51.1 6.1 %shard_map.176 = (f32[1536,128]{1,0:T(8,128)}, f32[384,128]{1,0:T(8,128)}, f32[376,128]{1,0:T(8,128)S(1)}, f32[376,128]{1,0:T(8,128)S(1)}, f32[640,128]{1,0:T(8,128)}) custom-call(f32[4224,128]{1,0:T(8,128)S(1)} %bitcast.15, bf16[256,128]{1,0:T(8,128)(2,1)} %constant.56.clone.refs_0_, bf16[128,192]{1,0:T(8,128)(2,1)} %constant.57.clone.refs_1_, ...), custom_call_target="tpu_custom_call" | custom-call | tf_op jit(solution)/shard_map/pallas_call | solution.py:53
  57.2 3.6 %all-to-all-start.1 = ((f32[16,40,128]{2,1,0:T(8,128)}), f32[16,40,128]{2,1,0:T(8,128)S(1)}, u32[]{:S(2)}, u32[]{:S(2)}) async-start(f32[16,40,128]{2,1,0:T(8,128)} %bitcast.8), calls=%async_computation.1 | async-start | bytes 655360 | tf_op jit(solution)/shard_map/all_to_all | solution.py:857
  60.8 1.2 %collective-permute-start = (f32[376,128]{1,0:T(8,128)S(1)}, f32[376,128]{1,0:T(8,128)S(1)}, u32[]{:S(2)}, u32[]{:S(2)}) collective-permute-start(f32[376,128]{1,0:T(8,128)S(1)} %get-tuple-element.24), channel_id=1, source_target_pairs={{0,1},{1,2},{2,3},{3,4},{4,5},{5,6},{6,7},{7,0},{8,9},{9,10},{10,1... | collective-permute-start | bytes 577544 | tf_op jit(solution)/shard_map/ppermute | solution.py:818
  62.2 2.4 %collective-permute-done.before_ref = f32[376,128]{1,0:T(8,128)S(1)} collective-permute-done((f32[376,128]{1,0:T(8,128)S(1)}, f32[376,128]{1,0:T(8,128)S(1)}, u32[]{:S(2)}, u32[]{:S(2)}) %collective-permute-start) | collective-permute-done | bytes 192544 | tf_op jit(solution)/shard_map/ppermute | solution.py:818
  64.6 2.8 %collective-permute-done.1.behind_ref = f32[376,128]{1,0:T(8,128)S(1)} collective-permute-done((f32[376,128]{1,0:T(8,128)S(1)}, f32[376,128]{1,0:T(8,128)S(1)}, u32[]{:S(2)}, u32[]{:S(2)}) %collective-permute-start.1) | collective-permute-done | bytes 192544 | tf_op jit(solution)/shard_map/ppermute | solution.py:819
  67.4 1.9 %shard_map.177 = (f32[1536,128]{1,0:T(8,128)S(1)}, f32[512,128]{1,0:T(8,128)S(1)}, f32[768,128]{1,0:T(8,128)}, f32[376,128]{1,0:T(8,128)S(1)}, f32[376,128]{1,0:T(8,128)S(1)}) custom-call(f32[1536,128]{1,0:T(8,128)} %get-tuple-element.22.fine_hbm, f32[384,128]{1,0:T(8,128)} %get-tuple-element.23.mid_hbm, f32[376,128]{1,0:T(8,128)S(1)} %collective-permute-done.before_ref, ...), custom_call_target="tpu_custom_call" | custom-call | tf_op jit(solution)/shard_map/pallas_call | solution.py:53
  69.2 1.6 %collective-permute-start.2 = (f32[376,128]{1,0:T(8,128)S(1)}, f32[376,128]{1,0:T(8,128)S(1)}, u32[]{:S(2)}, u32[]{:S(2)}) collective-permute-start(f32[376,128]{1,0:T(8,128)S(1)} %get-tuple-element.28), channel_id=1, source_target_pairs={{0,8},{8,16},{16,24},{24,32},{32,40},{40,48},{48,56},{56,64},{64,7... | collective-permute-start | bytes 577544 | tf_op jit(solution)/shard_map/ppermute | solution.py:818
  70.8 3.5 %collective-permute-start.3 = (f32[376,128]{1,0:T(8,128)S(1)}, f32[376,128]{1,0:T(8,128)S(1)}, u32[]{:S(2)}, u32[]{:S(2)}) collective-permute-start(f32[376,128]{1,0:T(8,128)S(1)} %get-tuple-element.29), channel_id=1, source_target_pairs={{8,0},{16,8},{24,16},{32,24},{40,32},{48,40},{56,48},{64,56},{72,6... | collective-permute-start | bytes 577544 | tf_op jit(solution)/shard_map/ppermute | solution.py:819
  74.3 1.4 %shard_map.180 = f32[64,640]{1,0:T(8,128)} custom-call(f32[640,128]{1,0:T(8,128)S(1)} %bitcast.18, bf16[128,256]{1,0:T(8,128)(2,1)S(1)} %copy-done.6, bf16[128,128]{1,0:T(8,128)(2,1)S(1)} %get-tuple-element.34.y_ref, bf16[1024,128]{1,0:T(8,128)(2,1)S(1)} %get-tuple-element.35.z_ref), custom_call_target="tpu_custom_call" | custom-call | tf_op jit(solution)/shard_map/pallas_call | solution.py:53
  75.7 5.3 %all-to-all-start.2 = ((f32[8,8,640]{2,1,0:T(8,128)}), f32[8,8,640]{2,1,0:T(8,128)S(1)}, u32[]{:S(2)}, u32[]{:S(2)}) async-start(f32[8,8,640]{2,1,0:T(8,128)} %bitcast.10), calls=%async_computation.2 | async-start | bytes 327680 | tf_op jit(solution)/shard_map/all_to_all | solution.py:867
  81.0 1.3 %shard_map.178.own_ref = f32[2048,128]{1,0:T(8,128)S(1)} custom-call(f32[1536,128]{1,0:T(8,128)S(1)} %get-tuple-element.26.fine_s, f32[512,128]{1,0:T(8,128)S(1)} %get-tuple-element.27.halo_s, bf16[512,256]{1,0:T(8,128)(2,1)S(1)} %copy-done.3, bf16[256,512]{1,0:T(8,128)(2,1)S(1)} %copy-done), custom_call_target="tpu_custom_call" | custom-call | tf_op jit(solution)/shard_map/pallas_call | solution.py:53
  82.4 5.2 %shard_map.179 = (f32[768,256]{1,0:T(8,128)S(1)}, f32[144,256]{1,0:T(8,128)S(1)}, bf16[448,256]{1,0:T(8,128)(2,1)S(1)}) custom-call(f32[2048,128]{1,0:T(8,128)S(1)} %shard_map.178.own_ref, f32[376,128]{1,0:T(8,128)S(1)} %collective-permute-done.2.before_ref, f32[376,128]{1,0:T(8,128)S(1)} %collective-permute-done.3.behind_ref, ...), custom_call_target="tpu_custom_call" | custom-call | tf_op jit(solution)/shard_map/pallas_call | solution.py:53
  87.6 1.7 %shard_map.181 = f32[768,256]{1,0:T(8,128)} custom-call(f32[768,256]{1,0:T(8,128)S(1)} %get-tuple-element.31.near_ref, f32[144,256]{1,0:T(8,128)S(1)} %get-tuple-element.32.mid_ref, f32[64,640]{1,0:T(8,128)S(1)} %bitcast.19, bf16[448,256]{1,0:T(8,128)(2,1)S(1)} %get-tuple-element.36.refs_0_), custom_call_target="tpu_custom_call" | custom-call | tf_op jit(solution)/shard_map/pallas_call | solution.py:53
  (47 shorter events, 3.2 us)
Async XLA Ops:
  0.7 0.7 copy-start.7
  8.8 11.5 %copy-start.10 = (f32[9,9,9]{2,1,0:T(8,128)S(1)}, f32[9,9,9]{2,1,0:T(8,128)}, u32[]{:S(2)}) copy-start(f32[9,9,9]{2,1,0:T(8,128)} %param.21) | copy-start | bytes 8752
  8.8 11.6 %copy-start.11 = (f32[9,9,9]{2,1,0:T(8,128)S(1)}, f32[9,9,9]{2,1,0:T(8,128)}, u32[]{:S(2)}) copy-start(f32[9,9,9]{2,1,0:T(8,128)} %param.22) | copy-start | bytes 8752
  8.8 12.0 %slice-start = ((f32[9,9,9]{2,1,0:T(8,128)}), f32[9,5,9]{2,1,0:T(8,128)S(1)}, s32[]{:S(2)}) async-start(f32[9,9,9]{2,1,0:T(8,128)} %param.21), calls=%async_computation.3 | async-start | bytes 73728 | tf_op jit(solution)/shard_map/slice | solution.py:556
  8.8 12.1 %slice-start.1 = ((f32[9,9,9]{2,1,0:T(8,128)}), f32[9,5,9]{2,1,0:T(8,128)S(1)}, s32[]{:S(2)}) async-start(f32[9,9,9]{2,1,0:T(8,128)} %param.22), calls=%async_computation.4 | async-start | bytes 73728 | tf_op jit(solution)/shard_map/slice | solution.py:556
  8.8 42.3 %all-to-all-start = ((f32[128,1,4224]{2,1,0:T(1,128)}), f32[128,1,4224]{2,1,0:T(1,128)S(1)}, u32[]{:S(2)}, u32[]{:S(2)}) async-start(f32[128,1,4224]{2,1,0:T(1,128)} %bitcast.21), calls=%async_computation | async-start | bytes 4325376 | tf_op jit(solution)/shard_map/all_to_all | solution.py:832
  21.0 4.0 %copy-start = (bf16[256,512]{1,0:T(8,128)(2,1)S(1)}, bf16[256,512]{1,0:T(8,128)(2,1)}, u32[]{:S(2)}) copy-start(bf16[256,512]{1,0:T(8,128)(2,1)} %constant.54.clone.y_ref.refs_1_) | copy-start | bytes 786436
  21.0 4.0 %copy-start.4 = (bf16[512,256]{1,0:T(8,128)(2,1)S(1)}, bf16[512,256]{1,0:T(8,128)(2,1)}, u32[]{:S(2)}) copy-start(bf16[512,256]{1,0:T(8,128)(2,1)} %constant.55.clone.z_ref.refs_3_) | copy-start | bytes 786436
  24.9 1.8 %copy-start.3 = (bf16[512,256]{1,0:T(8,128)(2,1)S(1)}, bf16[512,256]{1,0:T(8,128)(2,1)}, u32[]{:S(2)}) copy-start(bf16[512,256]{1,0:T(8,128)(2,1)} %constant.53.clone.z_ref.refs_0_) | copy-start | bytes 786436
  25.9 0.8 copy-start.1
  26.6 1.7 %copy-start.8 = (f32[4]{0:T(128)S(1)}, f32[4]{0:T(128)}, u32[]{:S(2)}) copy-start(f32[4]{0:T(128)} %weights_ref.1) | copy-start | bytes 52
  26.6 1.7 %copy-start.9 = (f32[4]{0:T(128)S(1)}, f32[4]{0:T(128)}, u32[]{:S(2)}) copy-start(f32[4]{0:T(128)} %widths_ref.1) | copy-start | bytes 52
  27.5 0.8 copy-start.2
  29.1 0.6 copy-start.5
  51.1 23.2 %copy-start.6 = (bf16[128,256]{1,0:T(8,128)(2,1)S(1)}, bf16[128,256]{1,0:T(8,128)(2,1)}, u32[]{:S(2)}) copy-start(bf16[128,256]{1,0:T(8,128)(2,1)} %copy-done.5) | copy-start | bytes 196612
  57.2 17.1 %all-to-all-start.1 = ((f32[16,40,128]{2,1,0:T(8,128)}), f32[16,40,128]{2,1,0:T(8,128)S(1)}, u32[]{:S(2)}, u32[]{:S(2)}) async-start(f32[16,40,128]{2,1,0:T(8,128)} %bitcast.8), calls=%async_computation.1 | async-start | bytes 655360 | tf_op jit(solution)/shard_map/all_to_all | solution.py:857
  60.8 3.8 %collective-permute-start = (f32[376,128]{1,0:T(8,128)S(1)}, f32[376,128]{1,0:T(8,128)S(1)}, u32[]{:S(2)}, u32[]{:S(2)}) collective-permute-start(f32[376,128]{1,0:T(8,128)S(1)} %get-tuple-element.24), channel_id=1, source_target_pairs={{0,1},{1,2},{2,3},{3,4},{4,5},{5,6},{6,7},{7,0},{8,9},{9,10},{10,1... | collective-permute-start | bytes 577544 | tf_op jit(solution)/shard_map/ppermute | solution.py:818
  62.0 5.3 %collective-permute-start.1 = (f32[376,128]{1,0:T(8,128)S(1)}, f32[376,128]{1,0:T(8,128)S(1)}, u32[]{:S(2)}, u32[]{:S(2)}) collective-permute-start(f32[376,128]{1,0:T(8,128)S(1)} %get-tuple-element.25), channel_id=1, source_target_pairs={{1,0},{2,1},{3,2},{4,3},{5,4},{6,5},{7,6},{0,7},{9,8},{10,9},{11,1... | collective-permute-start | bytes 577544 | tf_op jit(solution)/shard_map/ppermute | solution.py:819
  69.2 13.1 %collective-permute-start.2 = (f32[376,128]{1,0:T(8,128)S(1)}, f32[376,128]{1,0:T(8,128)S(1)}, u32[]{:S(2)}, u32[]{:S(2)}) collective-permute-start(f32[376,128]{1,0:T(8,128)S(1)} %get-tuple-element.28), channel_id=1, source_target_pairs={{0,8},{8,16},{16,24},{24,32},{32,40},{40,48},{48,56},{56,64},{64,7... | collective-permute-start | bytes 577544 | tf_op jit(solution)/shard_map/ppermute | solution.py:818
  70.8 11.6 %collective-permute-start.3 = (f32[376,128]{1,0:T(8,128)S(1)}, f32[376,128]{1,0:T(8,128)S(1)}, u32[]{:S(2)}, u32[]{:S(2)}) collective-permute-start(f32[376,128]{1,0:T(8,128)S(1)} %get-tuple-element.29), channel_id=1, source_target_pairs={{8,0},{16,8},{24,16},{32,24},{40,32},{48,40},{56,48},{64,56},{72,6... | collective-permute-start | bytes 577544 | tf_op jit(solution)/shard_map/ppermute | solution.py:819
  75.7 11.9 %all-to-all-start.2 = ((f32[8,8,640]{2,1,0:T(8,128)}), f32[8,8,640]{2,1,0:T(8,128)S(1)}, u32[]{:S(2)}, u32[]{:S(2)}) async-start(f32[8,8,640]{2,1,0:T(8,128)} %bitcast.10), calls=%async_computation.2 | async-start | bytes 327680 | tf_op jit(solution)/shard_map/all_to_all | solution.py:867

commit v9 on v8

--- a/solution.py
+++ b/solution.py
@@ -247,12 +247,11 @@
 
 def collect_kernel(in_ref, *refs):
     tables = refs[:4]
-    outs = refs[-15:-13]
-    low_ref, high_ref, top_ref = refs[-13:-10]
-    data_s, ids_s, slab_s = refs[-10:-7]
-    thin_z_ref, thin_y_ref, top_rows_ref, top_z_ref = refs[-7:-3]
-    fine_ref, mid_ref, sems = refs[-3:]
-    table_copies = started(list(zip(tables, refs[-7:-3])), sems)
+    *outs, low_ref, high_ref, top_out = refs[-16:-11]
+    data_s, ids_s, slab_s = refs[-11:-8]
+    thin_z_ref, thin_y_ref, top_rows_ref, top_z_ref = refs[-8:-4]
+    fine_ref, mid_ref, top_ref, sems = refs[-4:]
+    table_copies = started(list(zip(tables, refs[-8:-4])), sems)
 
     def unpack(c):
         total = None
@@ -315,6 +314,12 @@
         part = exact_right(slab_s[g * 192 : (g + 1) * 192, :], thin_z_ref)
         mid_ref[g * 128 : (g + 1) * 128, :] = exact_left(thin_y_ref, part)
     out_copies += started([(mid_ref, outs[1])], sems, 5)
+    stacked = exact_left(top_rows_ref, mid_ref[: 17 * 16, :])
+    pair = jnp.concatenate([stacked[:TOP_ROWS], stacked[TOP_ROWS:]], axis=1)
+    top_charge = exact_right(pair, top_z_ref)
+    for s in range(SIZE_X):
+        top_ref[s * TOP_ROWS : (s + 1) * TOP_ROWS, :] = top_charge
+    out_copies += started([(top_ref, top_out)], sems, 6)
     for h in range(2):
         for c in range(4):
             at = slice((h * 4 + c) * CX, (h * 4 + c + 1) * CX)
@@ -324,11 +329,6 @@
         at = slice(256 + j * 24, 256 + (j + 1) * 24)
         low_ref[at, :] = mid_ref[pl.ds(j, 24, stride=16), :]
         high_ref[at, :] = mid_ref[pl.ds(8 + j, 24, stride=16), :]
-    stacked = exact_left(top_rows_ref, mid_ref[: 17 * 16, :])
-    pair = jnp.concatenate([stacked[:TOP_ROWS], stacked[TOP_ROWS:]], axis=1)
-    top_charge = exact_right(pair, top_z_ref)
-    for s in range(SIZE_X):
-        top_ref[s * TOP_ROWS : (s + 1) * TOP_ROWS, :] = top_charge
     for copy in out_copies:
         copy.wait()
 
@@ -356,17 +356,17 @@
             pltpu.VMEM((DEVICES // 4, 128), jnp.int32),
             pltpu.VMEM((24 * CY, NZ), F32),
             *buffers(*tables),
-            *buffers(*out[:2]),
-            pltpu.SemaphoreType.DMA((6,)),
+            *buffers(out[0], out[1], out[4]),
+            pltpu.SemaphoreType.DMA((7,)),
         ],
-        outs=(HB, HB, VM, VM, VM),
+        outs=(HB, HB, VM, VM, HB),
         limit=20,
     )(arrived, *tables, *after)
 
 
 def merge_kernel(
-    fine_hbm, mid_hbm, before_ref, behind_ref, fine_s, halo_ref, wide_hbm, low_ref, high_ref,
-    mid_ref, wide_ref, sems,
+    fine_hbm, mid_hbm, before_ref, behind_ref, fine_s, halo_ref, wide_hbm, low_hbm, high_hbm,
+    mid_ref, wide_ref, low_ref, high_ref, sems,
 ):
     mid_copy, fine_copy = started([(mid_hbm, mid_ref), (fine_hbm, fine_s)], sems)
     for h in range(2):
@@ -407,6 +407,7 @@
             ref[at + 16 : at + 24, :] = (
                 wide_ref[base + 16 : base + 24, :] + wide_ref[base + 24 : base + 32, :]
             )
+    out_copies += started([(low_ref, low_hbm), (high_ref, high_hbm)], sems, 3)
     for copy in out_copies:
         copy.wait()
 
@@ -425,10 +426,10 @@
         [HB, HB, VM, VM],
         [
             pltpu.VMEM((24 * 16, 128), F32),
-            *buffers(out[2]),
-            pltpu.SemaphoreType.DMA((3,)),
+            *buffers(*out[2:]),
+            pltpu.SemaphoreType.DMA((5,)),
         ],
-        outs=(VM, VM, HB, VM, VM),
+        outs=(VM, VM, HB, HB, HB),
     )(fine, mid, before, behind)
 
 

time: 90 us -> 89.8 us (level)
  no operation moved by 1% of the time
where the time goes in v9:
time: 89.8 us; the launch traced here: 89.3 us
  Pallas kernels  27.2 us (30%)
  starting transfers between devices  26.8 us (30%)
  waiting for transfers between devices  26.6 us (30%)
  local copies, waits for them, and re-layouts  6.32 us (7%)
  other arithmetic  1.19 us (1%)
  between operations  1.13 us (1%)
    pallas_call x10, Pallas kernels, run(): return kernel(*placed)  27.2 us
    all_to_all x1, waiting for transfers between devices, on_device(): lax.all_to_all(outgoing.reshape(DEVICES, 1, ROWS * 128), ('gx', 'gy'), sp...  21.4 us
    all_to_all x1, starting transfers between devices, on_device(): lax.all_to_all(outgoing.reshape(DEVICES, 1, ROWS * 128), ('gx', 'gy'), sp...  11.5 us
    all_to_all x1, starting transfers between devices, on_device(): lax.all_to_all(partial.reshape(SIZE_Y, 8, 640), 'gy', split_axis=0, conca...  5.3 us
    ppermute x2, starting transfers between devices, swap(): behind = lax.ppermute(to_low, axis, backward)  3.68 us
    all_to_all x1, starting transfers between devices, on_device(): lax.all_to_all(top.reshape(SIZE_X, TOP_ROWS, 128), 'gx', split_axis=0, co...  3.59 us
    unnamed x24, local copies, waits for them, and re-layouts  2.95 us
    ppermute x2, starting transfers between devices, swap(): before = lax.ppermute(to_high, axis, forward)  2.79 us
  transfers between devices with their start and end apart: 7, of which 3 were waited for; matrix products, arithmetic and copies ran while one was open for 5% of the time, Pallas kernels for 14%

profile of v9, /device:TPU:1, one launch (start us, length us, event | category | flops | bytes accessed | tf_op | source)
XLA Modules:
  0.0 89.3 jit_solution(6626613373738614139)
XLA Ops:
  1.5 7.3 %shard_map.172.after_ref = f32[4224,128]{1,0:T(8,128)} custom-call(s32[32,128]{1,0:T(8,128)S(1)} %bitcast.20, s32[4]{0:T(128)S(1)} %pad_add_fusion.info_ref, f32[4096,128]{1,0:T(8,128)} %data_ref.1), custom_call_target="tpu_custom_call" | custom-call | tf_op jit(solution)/shard_map/pallas_call | solution.py:53
  8.8 11.5 %all-to-all-start = ((f32[128,1,4224]{2,1,0:T(1,128)}), f32[128,1,4224]{2,1,0:T(1,128)S(1)}, u32[]{:S(2)}, u32[]{:S(2)}) async-start(f32[128,1,4224]{2,1,0:T(1,128)} %bitcast.21), calls=%async_computation | async-start | bytes 4325376 | tf_op jit(solution)/shard_map/all_to_all | solution.py:833
  21.1 0.8 slice.49
  21.9 0.8 slice.51
  22.7 1.2 %concatenate.25 = f32[9,32,256]{2,1,0:T(8,128)S(1)} concatenate(f32[9,32,5]{2,1,0:T(8,128)} %slice.51, f32[9,32,119]{2,1,0:T(8,128)S(1)} %broadcast_in_dim.7, f32[9,32,9]{2,1,0:T(8,128)S(1)} %get-tuple-element.37, f32[9,32,119]{2,1,0:T(8,128)S(1)} %broadcast_in_dim.7, f32[9,32,4]{2,1,0:T(8,128)S(1)} %bitcast.22), dimensions={2} | concatenate | bytes 589824 | tf_op jit(solution)/shard_map/concatenate | solution.py:563
  23.9 1.0 %pad_maximum_fusion = f32[9,32,256]{2,1,0:T(8,128)S(1)} fusion(f32[9,32,4]{2,1,0:T(8,128)S(1)} %bitcast.23, f32[9,32,5]{2,1,0:T(8,128)} %slice.49, f32[256]{0:T(256)S(1)} %pad.6.clone), kind=kLoop, calls=%fused_computation | loop fusion | flops 147456 | bytes 306304 | tf_op jit(solution)/shard_map/concatenate | solution.py:560
  25.0 0.9 shard_map.174.refs_5_
  25.9 0.8 copy-done.1
  26.7 0.9 shard_map.173.refs_4_
  27.6 0.8 copy-done.2
  29.7 21.4 %all-to-all-done = f32[128,1,4224]{2,1,0:T(1,128)S(1)} async-done(((f32[128,1,4224]{2,1,0:T(1,128)}), f32[128,1,4224]{2,1,0:T(1,128)S(1)}, u32[]{:S(2)}, u32[]{:S(2)}) %all-to-all-start) | async-done | bytes 2162720 | tf_op jit(solution)/shard_map/all_to_all | solution.py:833
  51.1 5.7 %shard_map.176 = (f32[1536,128]{1,0:T(8,128)}, f32[384,128]{1,0:T(8,128)}, f32[376,128]{1,0:T(8,128)S(1)}, f32[376,128]{1,0:T(8,128)S(1)}, f32[640,128]{1,0:T(8,128)}) custom-call(f32[4224,128]{1,0:T(8,128)S(1)} %bitcast.15, bf16[256,128]{1,0:T(8,128)(2,1)} %constant.56.clone.refs_0_, bf16[128,192]{1,0:T(8,128)(2,1)} %constant.57.clone.refs_1_, ...), custom_call_target="tpu_custom_call" | custom-call | tf_op jit(solution)/shard_map/pallas_call | solution.py:53
  56.8 3.6 %all-to-all-start.1 = ((f32[16,40,128]{2,1,0:T(8,128)}), f32[16,40,128]{2,1,0:T(8,128)S(1)}, u32[]{:S(2)}, u32[]{:S(2)}) async-start(f32[16,40,128]{2,1,0:T(8,128)} %bitcast.24), calls=%async_computation.1 | async-start | bytes 655360 | tf_op jit(solution)/shard_map/all_to_all | solution.py:858
  60.4 1.2 %collective-permute-start = (f32[376,128]{1,0:T(8,128)S(1)}, f32[376,128]{1,0:T(8,128)S(1)}, u32[]{:S(2)}, u32[]{:S(2)}) collective-permute-start(f32[376,128]{1,0:T(8,128)S(1)} %get-tuple-element.24), channel_id=1, source_target_pairs={{0,1},{1,2},{2,3},{3,4},{4,5},{5,6},{6,7},{7,0},{8,9},{9,10},{10,1... | collective-permute-start | bytes 577544 | tf_op jit(solution)/shard_map/ppermute | solution.py:819
  61.8 2.4 %collective-permute-done.before_ref = f32[376,128]{1,0:T(8,128)S(1)} collective-permute-done((f32[376,128]{1,0:T(8,128)S(1)}, f32[376,128]{1,0:T(8,128)S(1)}, u32[]{:S(2)}, u32[]{:S(2)}) %collective-permute-start) | collective-permute-done | bytes 192544 | tf_op jit(solution)/shard_map/ppermute | solution.py:819
  64.2 2.8 %collective-permute-done.1.behind_ref = f32[376,128]{1,0:T(8,128)S(1)} collective-permute-done((f32[376,128]{1,0:T(8,128)S(1)}, f32[376,128]{1,0:T(8,128)S(1)}, u32[]{:S(2)}, u32[]{:S(2)}) %collective-permute-start.1) | collective-permute-done | bytes 192544 | tf_op jit(solution)/shard_map/ppermute | solution.py:820
  67.0 2.1 %shard_map.177 = (f32[1536,128]{1,0:T(8,128)S(1)}, f32[512,128]{1,0:T(8,128)S(1)}, f32[768,128]{1,0:T(8,128)}, f32[376,128]{1,0:T(8,128)}, f32[376,128]{1,0:T(8,128)}) custom-call(f32[1536,128]{1,0:T(8,128)} %get-tuple-element.22.fine_hbm, f32[384,128]{1,0:T(8,128)} %get-tuple-element.23.mid_hbm, f32[376,128]{1,0:T(8,128)S(1)} %collective-permute-done.before_ref, ...), custom_call_target="tpu_custom_call" | custom-call | tf_op jit(solution)/shard_map/pallas_call | solution.py:53
  69.0 1.6 %collective-permute-start.2 = (f32[376,128]{1,0:T(8,128)}, f32[376,128]{1,0:T(8,128)S(1)}, u32[]{:S(2)}, u32[]{:S(2)}) collective-permute-start(f32[376,128]{1,0:T(8,128)} %get-tuple-element.28), channel_id=1, source_target_pairs={{0,8},{8,16},{16,24},{24,32},{32,40},{40,48},{48,56},{56,64},{64,7... | collective-permute-start | bytes 577544 | tf_op jit(solution)/shard_map/ppermute | solution.py:819
  70.6 3.5 %collective-permute-start.3 = (f32[376,128]{1,0:T(8,128)}, f32[376,128]{1,0:T(8,128)S(1)}, u32[]{:S(2)}, u32[]{:S(2)}) collective-permute-start(f32[376,128]{1,0:T(8,128)} %get-tuple-element.29), channel_id=1, source_target_pairs={{8,0},{16,8},{24,16},{32,24},{40,32},{48,40},{56,48},{64,56},{72,6... | collective-permute-start | bytes 577544 | tf_op jit(solution)/shard_map/ppermute | solution.py:820
  74.1 1.4 %shard_map.180 = f32[64,640]{1,0:T(8,128)} custom-call(f32[640,128]{1,0:T(8,128)S(1)} %bitcast.18, bf16[128,256]{1,0:T(8,128)(2,1)S(1)} %copy-done.6, bf16[128,128]{1,0:T(8,128)(2,1)S(1)} %get-tuple-element.34.y_ref, bf16[1024,128]{1,0:T(8,128)(2,1)S(1)} %get-tuple-element.35.z_ref), custom_call_target="tpu_custom_call" | custom-call | tf_op jit(solution)/shard_map/pallas_call | solution.py:53
  75.5 5.3 %all-to-all-start.2 = ((f32[8,8,640]{2,1,0:T(8,128)}), f32[8,8,640]{2,1,0:T(8,128)S(1)}, u32[]{:S(2)}, u32[]{:S(2)}) async-start(f32[8,8,640]{2,1,0:T(8,128)} %bitcast.10), calls=%async_computation.2 | async-start | bytes 327680 | tf_op jit(solution)/shard_map/all_to_all | solution.py:868
  80.8 1.3 %shard_map.178.own_ref = f32[2048,128]{1,0:T(8,128)S(1)} custom-call(f32[1536,128]{1,0:T(8,128)S(1)} %get-tuple-element.26.fine_s, f32[512,128]{1,0:T(8,128)S(1)} %get-tuple-element.27.halo_s, bf16[512,256]{1,0:T(8,128)(2,1)S(1)} %copy-done.3, bf16[256,512]{1,0:T(8,128)(2,1)S(1)} %copy-done), custom_call_target="tpu_custom_call" | custom-call | tf_op jit(solution)/shard_map/pallas_call | solution.py:53
  82.2 5.2 %shard_map.179 = (f32[768,256]{1,0:T(8,128)S(1)}, f32[144,256]{1,0:T(8,128)S(1)}, bf16[448,256]{1,0:T(8,128)(2,1)S(1)}) custom-call(f32[2048,128]{1,0:T(8,128)S(1)} %shard_map.178.own_ref, f32[376,128]{1,0:T(8,128)S(1)} %collective-permute-done.2.before_ref, f32[376,128]{1,0:T(8,128)S(1)} %collective-permute-done.3.behind_ref, ...), custom_call_target="tpu_custom_call" | custom-call | tf_op jit(solution)/shard_map/pallas_call | solution.py:53
  87.4 1.7 %shard_map.181 = f32[768,256]{1,0:T(8,128)} custom-call(f32[768,256]{1,0:T(8,128)S(1)} %get-tuple-element.31.near_ref, f32[144,256]{1,0:T(8,128)S(1)} %get-tuple-element.32.mid_ref, f32[64,640]{1,0:T(8,128)S(1)} %bitcast.19, bf16[448,256]{1,0:T(8,128)(2,1)S(1)} %get-tuple-element.36.refs_0_), custom_call_target="tpu_custom_call" | custom-call | tf_op jit(solution)/shard_map/pallas_call | solution.py:53
  (47 shorter events, 3.2 us)
Async XLA Ops:
  0.7 0.7 copy-start.7
  8.8 11.5 %copy-start.10 = (f32[9,9,9]{2,1,0:T(8,128)S(1)}, f32[9,9,9]{2,1,0:T(8,128)}, u32[]{:S(2)}) copy-start(f32[9,9,9]{2,1,0:T(8,128)} %param.21) | copy-start | bytes 8752
  8.8 11.6 %copy-start.11 = (f32[9,9,9]{2,1,0:T(8,128)S(1)}, f32[9,9,9]{2,1,0:T(8,128)}, u32[]{:S(2)}) copy-start(f32[9,9,9]{2,1,0:T(8,128)} %param.22) | copy-start | bytes 8752
  8.8 12.0 %slice-start = ((f32[9,9,9]{2,1,0:T(8,128)}), f32[9,5,9]{2,1,0:T(8,128)S(1)}, s32[]{:S(2)}) async-start(f32[9,9,9]{2,1,0:T(8,128)} %param.21), calls=%async_computation.3 | async-start | bytes 73728 | tf_op jit(solution)/shard_map/slice | solution.py:557
  8.8 12.1 %slice-start.1 = ((f32[9,9,9]{2,1,0:T(8,128)}), f32[9,5,9]{2,1,0:T(8,128)S(1)}, s32[]{:S(2)}) async-start(f32[9,9,9]{2,1,0:T(8,128)} %param.22), calls=%async_computation.4 | async-start | bytes 73728 | tf_op jit(solution)/shard_map/slice | solution.py:557
  8.8 42.3 %all-to-all-start = ((f32[128,1,4224]{2,1,0:T(1,128)}), f32[128,1,4224]{2,1,0:T(1,128)S(1)}, u32[]{:S(2)}, u32[]{:S(2)}) async-start(f32[128,1,4224]{2,1,0:T(1,128)} %bitcast.21), calls=%async_computation | async-start | bytes 4325376 | tf_op jit(solution)/shard_map/all_to_all | solution.py:833
  21.0 4.0 %copy-start = (bf16[256,512]{1,0:T(8,128)(2,1)S(1)}, bf16[256,512]{1,0:T(8,128)(2,1)}, u32[]{:S(2)}) copy-start(bf16[256,512]{1,0:T(8,128)(2,1)} %constant.54.clone.y_ref.refs_1_) | copy-start | bytes 786436
  21.0 4.0 %copy-start.4 = (bf16[512,256]{1,0:T(8,128)(2,1)S(1)}, bf16[512,256]{1,0:T(8,128)(2,1)}, u32[]{:S(2)}) copy-start(bf16[512,256]{1,0:T(8,128)(2,1)} %constant.55.clone.z_ref.refs_3_) | copy-start | bytes 786436
  24.9 1.8 %copy-start.3 = (bf16[512,256]{1,0:T(8,128)(2,1)S(1)}, bf16[512,256]{1,0:T(8,128)(2,1)}, u32[]{:S(2)}) copy-start(bf16[512,256]{1,0:T(8,128)(2,1)} %constant.53.clone.z_ref.refs_0_) | copy-start | bytes 786436
  25.9 0.8 copy-start.1
  26.6 1.7 %copy-start.8 = (f32[4]{0:T(128)S(1)}, f32[4]{0:T(128)}, u32[]{:S(2)}) copy-start(f32[4]{0:T(128)} %weights_ref.1) | copy-start | bytes 52
  26.6 1.7 %copy-start.9 = (f32[4]{0:T(128)S(1)}, f32[4]{0:T(128)}, u32[]{:S(2)}) copy-start(f32[4]{0:T(128)} %widths_ref.1) | copy-start | bytes 52
  27.5 0.8 copy-start.2
  29.1 0.6 copy-start.5
  51.1 23.0 %copy-start.6 = (bf16[128,256]{1,0:T(8,128)(2,1)S(1)}, bf16[128,256]{1,0:T(8,128)(2,1)}, u32[]{:S(2)}) copy-start(bf16[128,256]{1,0:T(8,128)(2,1)} %copy-done.5) | copy-start | bytes 196612
  56.8 17.3 %all-to-all-start.1 = ((f32[16,40,128]{2,1,0:T(8,128)}), f32[16,40,128]{2,1,0:T(8,128)S(1)}, u32[]{:S(2)}, u32[]{:S(2)}) async-start(f32[16,40,128]{2,1,0:T(8,128)} %bitcast.24), calls=%async_computation.1 | async-start | bytes 655360 | tf_op jit(solution)/shard_map/all_to_all | solution.py:858
  60.4 3.8 %collective-permute-start = (f32[376,128]{1,0:T(8,128)S(1)}, f32[376,128]{1,0:T(8,128)S(1)}, u32[]{:S(2)}, u32[]{:S(2)}) collective-permute-start(f32[376,128]{1,0:T(8,128)S(1)} %get-tuple-element.24), channel_id=1, source_target_pairs={{0,1},{1,2},{2,3},{3,4},{4,5},{5,6},{6,7},{7,0},{8,9},{9,10},{10,1... | collective-permute-start | bytes 577544 | tf_op jit(solution)/shard_map/ppermute | solution.py:819
  61.6 5.3 %collective-permute-start.1 = (f32[376,128]{1,0:T(8,128)S(1)}, f32[376,128]{1,0:T(8,128)S(1)}, u32[]{:S(2)}, u32[]{:S(2)}) collective-permute-start(f32[376,128]{1,0:T(8,128)S(1)} %get-tuple-element.25), channel_id=1, source_target_pairs={{1,0},{2,1},{3,2},{4,3},{5,4},{6,5},{7,6},{0,7},{9,8},{10,9},{11,1... | collective-permute-start | bytes 577544 | tf_op jit(solution)/shard_map/ppermute | solution.py:820
  69.0 13.1 %collective-permute-start.2 = (f32[376,128]{1,0:T(8,128)}, f32[376,128]{1,0:T(8,128)S(1)}, u32[]{:S(2)}, u32[]{:S(2)}) collective-permute-start(f32[376,128]{1,0:T(8,128)} %get-tuple-element.28), channel_id=1, source_target_pairs={{0,8},{8,16},{16,24},{24,32},{32,40},{40,48},{48,56},{56,64},{64,7... | collective-permute-start | bytes 577544 | tf_op jit(solution)/shard_map/ppermute | solution.py:819
  70.6 11.6 %collective-permute-start.3 = (f32[376,128]{1,0:T(8,128)}, f32[376,128]{1,0:T(8,128)S(1)}, u32[]{:S(2)}, u32[]{:S(2)}) collective-permute-start(f32[376,128]{1,0:T(8,128)} %get-tuple-element.29), channel_id=1, source_target_pairs={{8,0},{16,8},{24,16},{32,24},{40,32},{48,40},{56,48},{64,56},{72,6... | collective-permute-start | bytes 577544 | tf_op jit(solution)/shard_map/ppermute | solution.py:820
  75.5 11.9 %all-to-all-start.2 = ((f32[8,8,640]{2,1,0:T(8,128)}), f32[8,8,640]{2,1,0:T(8,128)S(1)}, u32[]{:S(2)}, u32[]{:S(2)}) async-start(f32[8,8,640]{2,1,0:T(8,128)} %bitcast.10), calls=%async_computation.2 | async-start | bytes 327680 | tf_op jit(solution)/shard_map/all_to_all | solution.py:868

commit v10 on v9

--- a/solution.py
+++ b/solution.py
@@ -20,6 +20,7 @@
 DEAD = 2047
 SEND = 376
 TOP_ROWS = 40
+TOP_SENT = 36
 YD = 32
 F32 = jnp.float32
 BF16 = jnp.bfloat16
@@ -318,7 +319,7 @@
     pair = jnp.concatenate([stacked[:TOP_ROWS], stacked[TOP_ROWS:]], axis=1)
     top_charge = exact_right(pair, top_z_ref)
     for s in range(SIZE_X):
-        top_ref[s * TOP_ROWS : (s + 1) * TOP_ROWS, :] = top_charge
+        top_ref[s * TOP_SENT : (s + 1) * TOP_SENT, :] = top_charge[:TOP_SENT]
     out_copies += started([(top_ref, top_out)], sems, 6)
     for h in range(2):
         for c in range(4):
@@ -345,7 +346,7 @@
         array(24 * 16, 128),
         array(SEND, 128),
         array(SEND, 128),
-        array(SIZE_X * TOP_ROWS, 128),
+        array(SIZE_X * TOP_SENT, 128),
     )
     return call(
         collect_kernel,
@@ -733,8 +734,8 @@
     left = (x_ref[:64, :], x_ref[64:, :])
     columns = []
     for jp in range(4):
-        tiles = [in_ref[s * TOP_ROWS + jp * 8 : s * TOP_ROWS + jp * 8 + 8, :] for s in range(16)]
-        tiles.append(in_ref[pl.ds(32 + jp, SIZE_X, stride=TOP_ROWS), :])
+        tiles = [in_ref[s * TOP_SENT + jp * 8 : s * TOP_SENT + jp * 8 + 8, :] for s in range(16)]
+        tiles.append(in_ref[pl.ds(32 + jp, SIZE_X, stride=TOP_SENT), :])
         tiles.append(jnp.zeros((112, 128), F32))
         columns.append(jnp.concatenate(tiles, axis=0))
     right = halves(jnp.concatenate(columns, axis=1))
@@ -856,9 +857,9 @@
     fine, mid, low, high, top = collect(arrived, near_taps, mid_taps, bells[0])
     before, behind = swap(low, high, "gy")
     tops = lax.all_to_all(
-        top.reshape(SIZE_X, TOP_ROWS, 128), "gx", split_axis=0, concat_axis=0, tiled=True
-    )
-    tops = tops.reshape(SIZE_X * TOP_ROWS, 128)
+        top.reshape(SIZE_X, 1, TOP_SENT * 128), "gx", split_axis=0, concat_axis=0, tiled=True
+    )
+    tops = tops.reshape(SIZE_X * TOP_SENT, 128)
     partial = call(
         top_kernel,
         array(64, 640),

time: 89.8 us -> 89.8 us (level)
  no operation moved by 1% of the time
where the time goes in v10:
time: 89.8 us; the launch traced here: 89.3 us
  Pallas kernels  27.2 us (30%)
  starting transfers between devices  26.8 us (30%)
  waiting for transfers between devices  26.6 us (30%)
  local copies, waits for them, and re-layouts  6.32 us (7%)
  other arithmetic  1.19 us (1%)
  between operations  1.13 us (1%)
    pallas_call x10, Pallas kernels, run(): return kernel(*placed)  27.2 us
    all_to_all x1, waiting for transfers between devices, on_device(): lax.all_to_all(outgoing.reshape(DEVICES, 1, ROWS * 128), ('gx', 'gy'), sp...  21.4 us
    all_to_all x1, starting transfers between devices, on_device(): lax.all_to_all(outgoing.reshape(DEVICES, 1, ROWS * 128), ('gx', 'gy'), sp...  11.5 us
    all_to_all x1, starting transfers between devices, on_device(): lax.all_to_all(partial.reshape(SIZE_Y, 8, 640), 'gy', split_axis=0, conca...  5.3 us
    ppermute x2, starting transfers between devices, swap(): behind = lax.ppermute(to_low, axis, backward)  3.68 us
    all_to_all x1, starting transfers between devices, on_device(): lax.all_to_all(top.reshape(SIZE_X, 1, TOP_SENT * 128), 'gx', split_axis=0...  3.59 us
    unnamed x24, local copies, waits for them, and re-layouts  2.95 us
    ppermute x2, starting transfers between devices, swap(): before = lax.ppermute(to_high, axis, forward)  2.79 us
  transfers between devices with their start and end apart: 7, of which 3 were waited for; matrix products, arithmetic and copies ran while one was open for 5% of the time, Pallas kernels for 14%

profile of v10, /device:TPU:1, one launch (start us, length us, event | category | flops | bytes accessed | tf_op | source)
XLA Modules:
  0.0 89.3 jit_solution(10385393400259399125)
XLA Ops:
  1.5 7.3 %shard_map.172.after_ref = f32[4224,128]{1,0:T(8,128)} custom-call(s32[32,128]{1,0:T(8,128)S(1)} %bitcast.20, s32[4]{0:T(128)S(1)} %pad_add_fusion.info_ref, f32[4096,128]{1,0:T(8,128)} %data_ref.1), custom_call_target="tpu_custom_call" | custom-call | tf_op jit(solution)/shard_map/pallas_call | solution.py:54
  8.8 11.5 %all-to-all-start = ((f32[128,1,4224]{2,1,0:T(1,128)}), f32[128,1,4224]{2,1,0:T(1,128)S(1)}, u32[]{:S(2)}, u32[]{:S(2)}) async-start(f32[128,1,4224]{2,1,0:T(1,128)} %bitcast.21), calls=%async_computation | async-start | bytes 4325376 | tf_op jit(solution)/shard_map/all_to_all | solution.py:834
  21.1 0.8 slice.49
  21.9 0.8 slice.51
  22.7 1.2 %concatenate.25 = f32[9,32,256]{2,1,0:T(8,128)S(1)} concatenate(f32[9,32,5]{2,1,0:T(8,128)} %slice.51, f32[9,32,119]{2,1,0:T(8,128)S(1)} %broadcast_in_dim.7, f32[9,32,9]{2,1,0:T(8,128)S(1)} %get-tuple-element.37, f32[9,32,119]{2,1,0:T(8,128)S(1)} %broadcast_in_dim.7, f32[9,32,4]{2,1,0:T(8,128)S(1)} %bitcast.22), dimensions={2} | concatenate | bytes 589824 | tf_op jit(solution)/shard_map/concatenate | solution.py:564
  23.9 1.0 %pad_maximum_fusion = f32[9,32,256]{2,1,0:T(8,128)S(1)} fusion(f32[9,32,4]{2,1,0:T(8,128)S(1)} %bitcast.23, f32[9,32,5]{2,1,0:T(8,128)} %slice.49, f32[256]{0:T(256)S(1)} %pad.6.clone), kind=kLoop, calls=%fused_computation | loop fusion | flops 147456 | bytes 306304 | tf_op jit(solution)/shard_map/concatenate | solution.py:561
  25.0 0.9 shard_map.174.refs_5_
  25.9 0.8 copy-done.1
  26.7 0.9 shard_map.173.refs_4_
  27.6 0.8 copy-done.2
  29.7 21.4 %all-to-all-done = f32[128,1,4224]{2,1,0:T(1,128)S(1)} async-done(((f32[128,1,4224]{2,1,0:T(1,128)}), f32[128,1,4224]{2,1,0:T(1,128)S(1)}, u32[]{:S(2)}, u32[]{:S(2)}) %all-to-all-start) | async-done | bytes 2162720 | tf_op jit(solution)/shard_map/all_to_all | solution.py:834
  51.1 5.7 %shard_map.176 = (f32[1536,128]{1,0:T(8,128)}, f32[384,128]{1,0:T(8,128)}, f32[376,128]{1,0:T(8,128)S(1)}, f32[376,128]{1,0:T(8,128)S(1)}, f32[576,128]{1,0:T(8,128)}) custom-call(f32[4224,128]{1,0:T(8,128)S(1)} %bitcast.15, bf16[256,128]{1,0:T(8,128)(2,1)} %constant.56.clone.refs_0_, bf16[128,192]{1,0:T(8,128)(2,1)} %constant.57.clone.refs_1_, ...), custom_call_target="tpu_custom_call" | custom-call | tf_op jit(solution)/shard_map/pallas_call | solution.py:54
  56.8 3.6 %all-to-all-start.1 = ((f32[16,1,4608]{2,1,0:T(1,128)}), f32[16,1,4608]{2,1,0:T(1,128)S(1)}, u32[]{:S(2)}, u32[]{:S(2)}) async-start(f32[16,1,4608]{2,1,0:T(1,128)} %bitcast.24), calls=%async_computation.1 | async-start | bytes 589824 | tf_op jit(solution)/shard_map/all_to_all | solution.py:859
  60.4 1.2 %collective-permute-start = (f32[376,128]{1,0:T(8,128)S(1)}, f32[376,128]{1,0:T(8,128)S(1)}, u32[]{:S(2)}, u32[]{:S(2)}) collective-permute-start(f32[376,128]{1,0:T(8,128)S(1)} %get-tuple-element.24), channel_id=1, source_target_pairs={{0,1},{1,2},{2,3},{3,4},{4,5},{5,6},{6,7},{7,0},{8,9},{9,10},{10,1... | collective-permute-start | bytes 577544 | tf_op jit(solution)/shard_map/ppermute | solution.py:820
  61.8 2.4 %collective-permute-done.before_ref = f32[376,128]{1,0:T(8,128)S(1)} collective-permute-done((f32[376,128]{1,0:T(8,128)S(1)}, f32[376,128]{1,0:T(8,128)S(1)}, u32[]{:S(2)}, u32[]{:S(2)}) %collective-permute-start) | collective-permute-done | bytes 192544 | tf_op jit(solution)/shard_map/ppermute | solution.py:820
  64.2 2.8 %collective-permute-done.1.behind_ref = f32[376,128]{1,0:T(8,128)S(1)} collective-permute-done((f32[376,128]{1,0:T(8,128)S(1)}, f32[376,128]{1,0:T(8,128)S(1)}, u32[]{:S(2)}, u32[]{:S(2)}) %collective-permute-start.1) | collective-permute-done | bytes 192544 | tf_op jit(solution)/shard_map/ppermute | solution.py:821
  67.0 2.1 %shard_map.177 = (f32[1536,128]{1,0:T(8,128)S(1)}, f32[512,128]{1,0:T(8,128)S(1)}, f32[768,128]{1,0:T(8,128)}, f32[376,128]{1,0:T(8,128)}, f32[376,128]{1,0:T(8,128)}) custom-call(f32[1536,128]{1,0:T(8,128)} %get-tuple-element.22.fine_hbm, f32[384,128]{1,0:T(8,128)} %get-tuple-element.23.mid_hbm, f32[376,128]{1,0:T(8,128)S(1)} %collective-permute-done.before_ref, ...), custom_call_target="tpu_custom_call" | custom-call | tf_op jit(solution)/shard_map/pallas_call | solution.py:54
  69.0 1.6 %collective-permute-start.2 = (f32[376,128]{1,0:T(8,128)}, f32[376,128]{1,0:T(8,128)S(1)}, u32[]{:S(2)}, u32[]{:S(2)}) collective-permute-start(f32[376,128]{1,0:T(8,128)} %get-tuple-element.28), channel_id=1, source_target_pairs={{0,8},{8,16},{16,24},{24,32},{32,40},{40,48},{48,56},{56,64},{64,7... | collective-permute-start | bytes 577544 | tf_op jit(solution)/shard_map/ppermute | solution.py:820
  70.6 3.5 %collective-permute-start.3 = (f32[376,128]{1,0:T(8,128)}, f32[376,128]{1,0:T(8,128)S(1)}, u32[]{:S(2)}, u32[]{:S(2)}) collective-permute-start(f32[376,128]{1,0:T(8,128)} %get-tuple-element.29), channel_id=1, source_target_pairs={{8,0},{16,8},{24,16},{32,24},{40,32},{48,40},{56,48},{64,56},{72,6... | collective-permute-start | bytes 577544 | tf_op jit(solution)/shard_map/ppermute | solution.py:821
  74.1 1.4 %shard_map.180 = f32[64,640]{1,0:T(8,128)} custom-call(f32[576,128]{1,0:T(8,128)S(1)} %bitcast.18, bf16[128,256]{1,0:T(8,128)(2,1)S(1)} %copy-done.6, bf16[128,128]{1,0:T(8,128)(2,1)S(1)} %get-tuple-element.34.y_ref, bf16[1024,128]{1,0:T(8,128)(2,1)S(1)} %get-tuple-element.35.z_ref), custom_call_target="tpu_custom_call" | custom-call | tf_op jit(solution)/shard_map/pallas_call | solution.py:54
  75.5 5.3 %all-to-all-start.2 = ((f32[8,8,640]{2,1,0:T(8,128)}), f32[8,8,640]{2,1,0:T(8,128)S(1)}, u32[]{:S(2)}, u32[]{:S(2)}) async-start(f32[8,8,640]{2,1,0:T(8,128)} %bitcast.10), calls=%async_computation.2 | async-start | bytes 327680 | tf_op jit(solution)/shard_map/all_to_all | solution.py:869
  80.8 1.3 %shard_map.178.own_ref = f32[2048,128]{1,0:T(8,128)S(1)} custom-call(f32[1536,128]{1,0:T(8,128)S(1)} %get-tuple-element.26.fine_s, f32[512,128]{1,0:T(8,128)S(1)} %get-tuple-element.27.halo_s, bf16[512,256]{1,0:T(8,128)(2,1)S(1)} %copy-done.3, bf16[256,512]{1,0:T(8,128)(2,1)S(1)} %copy-done), custom_call_target="tpu_custom_call" | custom-call | tf_op jit(solution)/shard_map/pallas_call | solution.py:54
  82.2 5.2 %shard_map.179 = (f32[768,256]{1,0:T(8,128)S(1)}, f32[144,256]{1,0:T(8,128)S(1)}, bf16[448,256]{1,0:T(8,128)(2,1)S(1)}) custom-call(f32[2048,128]{1,0:T(8,128)S(1)} %shard_map.178.own_ref, f32[376,128]{1,0:T(8,128)S(1)} %collective-permute-done.2.before_ref, f32[376,128]{1,0:T(8,128)S(1)} %collective-permute-done.3.behind_ref, ...), custom_call_target="tpu_custom_call" | custom-call | tf_op jit(solution)/shard_map/pallas_call | solution.py:54
  87.4 1.7 %shard_map.181 = f32[768,256]{1,0:T(8,128)} custom-call(f32[768,256]{1,0:T(8,128)S(1)} %get-tuple-element.31.near_ref, f32[144,256]{1,0:T(8,128)S(1)} %get-tuple-element.32.mid_ref, f32[64,640]{1,0:T(8,128)S(1)} %bitcast.19, bf16[448,256]{1,0:T(8,128)(2,1)S(1)} %get-tuple-element.36.refs_0_), custom_call_target="tpu_custom_call" | custom-call | tf_op jit(solution)/shard_map/pallas_call | solution.py:54
  (47 shorter events, 3.2 us)
Async XLA Ops:
  0.7 0.7 copy-start.7
  8.8 11.5 %copy-start.10 = (f32[9,9,9]{2,1,0:T(8,128)S(1)}, f32[9,9,9]{2,1,0:T(8,128)}, u32[]{:S(2)}) copy-start(f32[9,9,9]{2,1,0:T(8,128)} %param.21) | copy-start | bytes 8752
  8.8 11.6 %copy-start.11 = (f32[9,9,9]{2,1,0:T(8,128)S(1)}, f32[9,9,9]{2,1,0:T(8,128)}, u32[]{:S(2)}) copy-start(f32[9,9,9]{2,1,0:T(8,128)} %param.22) | copy-start | bytes 8752
  8.8 12.0 %slice-start = ((f32[9,9,9]{2,1,0:T(8,128)}), f32[9,5,9]{2,1,0:T(8,128)S(1)}, s32[]{:S(2)}) async-start(f32[9,9,9]{2,1,0:T(8,128)} %param.21), calls=%async_computation.3 | async-start | bytes 73728 | tf_op jit(solution)/shard_map/slice | solution.py:558
  8.8 12.1 %slice-start.1 = ((f32[9,9,9]{2,1,0:T(8,128)}), f32[9,5,9]{2,1,0:T(8,128)S(1)}, s32[]{:S(2)}) async-start(f32[9,9,9]{2,1,0:T(8,128)} %param.22), calls=%async_computation.4 | async-start | bytes 73728 | tf_op jit(solution)/shard_map/slice | solution.py:558
  8.8 42.3 %all-to-all-start = ((f32[128,1,4224]{2,1,0:T(1,128)}), f32[128,1,4224]{2,1,0:T(1,128)S(1)}, u32[]{:S(2)}, u32[]{:S(2)}) async-start(f32[128,1,4224]{2,1,0:T(1,128)} %bitcast.21), calls=%async_computation | async-start | bytes 4325376 | tf_op jit(solution)/shard_map/all_to_all | solution.py:834
  21.0 4.0 %copy-start = (bf16[256,512]{1,0:T(8,128)(2,1)S(1)}, bf16[256,512]{1,0:T(8,128)(2,1)}, u32[]{:S(2)}) copy-start(bf16[256,512]{1,0:T(8,128)(2,1)} %constant.54.clone.y_ref.refs_1_) | copy-start | bytes 786436
  21.0 4.0 %copy-start.4 = (bf16[512,256]{1,0:T(8,128)(2,1)S(1)}, bf16[512,256]{1,0:T(8,128)(2,1)}, u32[]{:S(2)}) copy-start(bf16[512,256]{1,0:T(8,128)(2,1)} %constant.55.clone.z_ref.refs_3_) | copy-start | bytes 786436
  24.9 1.8 %copy-start.3 = (bf16[512,256]{1,0:T(8,128)(2,1)S(1)}, bf16[512,256]{1,0:T(8,128)(2,1)}, u32[]{:S(2)}) copy-start(bf16[512,256]{1,0:T(8,128)(2,1)} %constant.53.clone.z_ref.refs_0_) | copy-start | bytes 786436
  25.9 0.8 copy-start.1
  26.6 1.7 %copy-start.8 = (f32[4]{0:T(128)S(1)}, f32[4]{0:T(128)}, u32[]{:S(2)}) copy-start(f32[4]{0:T(128)} %weights_ref.1) | copy-start | bytes 52
  26.6 1.7 %copy-start.9 = (f32[4]{0:T(128)S(1)}, f32[4]{0:T(128)}, u32[]{:S(2)}) copy-start(f32[4]{0:T(128)} %widths_ref.1) | copy-start | bytes 52
  27.5 0.8 copy-start.2
  29.1 0.6 copy-start.5
  51.1 23.0 %copy-start.6 = (bf16[128,256]{1,0:T(8,128)(2,1)S(1)}, bf16[128,256]{1,0:T(8,128)(2,1)}, u32[]{:S(2)}) copy-start(bf16[128,256]{1,0:T(8,128)(2,1)} %copy-done.5) | copy-start | bytes 196612
  56.8 17.3 %all-to-all-start.1 = ((f32[16,1,4608]{2,1,0:T(1,128)}), f32[16,1,4608]{2,1,0:T(1,128)S(1)}, u32[]{:S(2)}, u32[]{:S(2)}) async-start(f32[16,1,4608]{2,1,0:T(1,128)} %bitcast.24), calls=%async_computation.1 | async-start | bytes 589824 | tf_op jit(solution)/shard_map/all_to_all | solution.py:859
  60.4 3.8 %collective-permute-start = (f32[376,128]{1,0:T(8,128)S(1)}, f32[376,128]{1,0:T(8,128)S(1)}, u32[]{:S(2)}, u32[]{:S(2)}) collective-permute-start(f32[376,128]{1,0:T(8,128)S(1)} %get-tuple-element.24), channel_id=1, source_target_pairs={{0,1},{1,2},{2,3},{3,4},{4,5},{5,6},{6,7},{7,0},{8,9},{9,10},{10,1... | collective-permute-start | bytes 577544 | tf_op jit(solution)/shard_map/ppermute | solution.py:820
  61.6 5.3 %collective-permute-start.1 = (f32[376,128]{1,0:T(8,128)S(1)}, f32[376,128]{1,0:T(8,128)S(1)}, u32[]{:S(2)}, u32[]{:S(2)}) collective-permute-start(f32[376,128]{1,0:T(8,128)S(1)} %get-tuple-element.25), channel_id=1, source_target_pairs={{1,0},{2,1},{3,2},{4,3},{5,4},{6,5},{7,6},{0,7},{9,8},{10,9},{11,1... | collective-permute-start | bytes 577544 | tf_op jit(solution)/shard_map/ppermute | solution.py:821
  69.0 13.1 %collective-permute-start.2 = (f32[376,128]{1,0:T(8,128)}, f32[376,128]{1,0:T(8,128)S(1)}, u32[]{:S(2)}, u32[]{:S(2)}) collective-permute-start(f32[376,128]{1,0:T(8,128)} %get-tuple-element.28), channel_id=1, source_target_pairs={{0,8},{8,16},{16,24},{24,32},{32,40},{40,48},{48,56},{56,64},{64,7... | collective-permute-start | bytes 577544 | tf_op jit(solution)/shard_map/ppermute | solution.py:820
  70.6 11.6 %collective-permute-start.3 = (f32[376,128]{1,0:T(8,128)}, f32[376,128]{1,0:T(8,128)S(1)}, u32[]{:S(2)}, u32[]{:S(2)}) collective-permute-start(f32[376,128]{1,0:T(8,128)} %get-tuple-element.29), channel_id=1, source_target_pairs={{8,0},{16,8},{24,16},{32,24},{40,32},{48,40},{56,48},{64,56},{72,6... | collective-permute-start | bytes 577544 | tf_op jit(solution)/shard_map/ppermute | solution.py:821
  75.5 11.9 %all-to-all-start.2 = ((f32[8,8,640]{2,1,0:T(8,128)}), f32[8,8,640]{2,1,0:T(8,128)S(1)}, u32[]{:S(2)}, u32[]{:S(2)}) async-start(f32[8,8,640]{2,1,0:T(8,128)} %bitcast.10), calls=%async_computation.2 | async-start | bytes 327680 | tf_op jit(solution)/shard_map/all_to_all | solution.py:869
